TPU v7x, 512 devices: a whole 4x4x16 slice. The times are simulated.
512 devices in a mesh: dp: 32 (over z, core), mp: 16 (over x, y).
Axes of the slice: x: 4, y: 4, z: 16, core: 2. Of those that a mesh axis runs over, the one named last changes fastest.
Arguments:
- hidden_in: bfloat16 [64, 512, 8192], P('dp', None, 'mp'), may hold values from -6 to 6
- query_act: bfloat16 [64, 512, 8192], P('dp', None, 'mp'), may hold values from -6 to 6
- key_act: bfloat16 [64, 512, 1024], P('dp'), may hold values from -6 to 6
- value_act: bfloat16 [64, 512, 1024], P('dp'), may hold values from -6 to 6
- ctx_grad: bfloat16 [64, 512, 8192], P('dp', None, 'mp'), may hold values from -6 to 6
- segment_ids: int32 [64, 512], P('dp'), may hold values from 0 to 3, never falling along the last dimension, each value on 1 to 256 neighbouring positions
- down_query: bfloat16 [8192, 128], P('mp'), may hold values from -0.0625 to 0.0625
- up_query: bfloat16 [128, 8192], P(None, 'mp'), may hold values from -0.5 to 0.5
- down_value: bfloat16 [8192, 128], P('mp'), may hold values from -0.0625 to 0.0625
- up_value: bfloat16 [128, 1024], replicated, may hold values from -0.5 to 0.5
- block_rows: int32 [3, 8192], P(None, 'mp'), may hold values from 0 to 63
- tile_rows: int32 [3, 8192], P(None, 'mp'), may hold values from 0 to 7
- block_value: int32 [1024], replicated, may hold values from 0 to 63
- tile_value: int32 [1024], replicated, may hold values from 0 to 7
- tile_bank: bfloat16 [8, 128, 128], replicated, may hold values from -0.5 to 0.5
- seed_feats: bfloat16 [1024, 8192], P('dp', 'mp'), may hold values from -6 to 6
Outputs:
- scores: float32 [64, 1024], P('dp', 'mp')
All inputs are finite; a program needn't handle non-finite values.
Results may differ from a plain program's by a relative error of at most 0.022.
Values may be sent and summed in bfloat16 or wider, within the bound.
No kernel may reach another device: no remote copies, remote signals or barrier semaphores. Data moves between devices by JAX's collectives and lax.ppermute only.
A program may use at most 64 MiB of HBM per device.

v0:
```python
import math

import jax
import jax.numpy as jnp
from jax import lax
from jax.sharding import PartitionSpec as P

H = 64
KVH = 8
DH = 128
R = 128
K = 8192
PB = 128
NT = 8


EPS = 1e-06


def local(
    hidden_in,
    query_act,
    key_act,
    value_act,
    ctx_grad,
    segment_ids,
    down_query,
    up_query,
    down_value,
    up_value,
    block_rows,
    tile_rows,
    block_value,
    tile_value,
    tile_bank,
    seed_feats,
):
    model_index = lax.axis_index("mp")
    cand_count, seq_len, width_dev = query_act.shape
    heads_dev = width_dev // DH
    head_group = H // KVH
    kv_count = max(heads_dev // head_group, 1)
    repeats = heads_dev // kv_count
    kv_first = model_index * heads_dev // head_group
    kv_width = kv_count * DH
    key_local = lax.dynamic_slice_in_dim(key_act, kv_first * DH, kv_width, 2)
    value_local = lax.dynamic_slice_in_dim(value_act, kv_first * DH, kv_width, 2)
    up_local = lax.dynamic_slice_in_dim(up_value, kv_first * DH, kv_width, 1)
    block_local = lax.dynamic_slice_in_dim(block_value, kv_first * DH, kv_width, 0)
    tile_local = lax.dynamic_slice_in_dim(tile_value, kv_first * DH, kv_width, 0)

    def spread_heads(packed):
        five = packed.reshape(cand_count, seq_len, kv_count, 1, DH)
        return jnp.broadcast_to(five, (cand_count, seq_len, kv_count, repeats, DH)).reshape(
            cand_count, seq_len, heads_dev, DH
        )

    queries = query_act.reshape(cand_count, seq_len, heads_dev, DH)
    key_heads = spread_heads(key_local)
    value_heads = spread_heads(value_local)
    grad_heads = ctx_grad.reshape(cand_count, seq_len, heads_dev, DH)
    both_down = jnp.concatenate([down_query, down_value], axis=1)
    lowrank_part = jnp.einsum(
        "bsd,dr->bsr", hidden_in, both_down, preferred_element_type=jnp.float32
    )
    position = jnp.arange(seq_len, dtype=jnp.int32)
    allowed = (position[None, :] <= position[:, None])[None] & (
        segment_ids[:, :, None] == segment_ids[:, None, :]
    )
    score_scale = 1.0 / math.sqrt(DH)
    logits = (
        jnp.einsum("bqhd,bkhd->bhqk", queries, key_heads, preferred_element_type=jnp.float32)
        * score_scale
    )
    logits = jnp.where(allowed[:, None], logits, -1e30)
    row_top = jnp.max(logits, axis=-1, keepdims=True)
    exp_terms = jnp.exp(logits - row_top)
    attn_probs = exp_terms / jnp.sum(exp_terms, axis=-1, keepdims=True)
    value_grad = jnp.einsum(
        "bhqk,bqhd->bkhd",
        attn_probs.astype(jnp.bfloat16),
        grad_heads,
        preferred_element_type=jnp.float32,
    ).astype(jnp.bfloat16)
    prob_grad = jnp.einsum(
        "bqhd,bkhd->bhqk", grad_heads, value_heads, preferred_element_type=jnp.float32
    )
    row_delta = jnp.sum(attn_probs * prob_grad, axis=-1, keepdims=True)
    logit_grad = (attn_probs * (prob_grad - row_delta)).astype(jnp.bfloat16)
    query_grad = (
        jnp.einsum("bhqk,bkhd->bqhd", logit_grad, key_heads, preferred_element_type=jnp.float32)
        * score_scale
    )
    query_grad = query_grad.astype(jnp.bfloat16).reshape(cand_count, seq_len, width_dev)
    value_five = value_grad.reshape(cand_count, seq_len, kv_count, repeats, DH)
    up_three = up_local.reshape(R, kv_count, DH)
    back_query = jnp.einsum("bsc,rc->bsr", query_grad, up_query, preferred_element_type=jnp.float32)
    back_value = jnp.einsum(
        "bskgd,rkd->bsr", value_five, up_three, preferred_element_type=jnp.float32
    )
    back_part = jnp.concatenate([back_query, back_value], axis=2)
    lowrank_in, lowrank_back = lax.psum((lowrank_part, back_part), "mp")
    lowrank_in = lowrank_in.astype(jnp.bfloat16)
    lowrank_back = lowrank_back.astype(jnp.bfloat16)
    grad_down = jnp.einsum(
        "bsd,bsr->bdr", hidden_in, lowrank_back, preferred_element_type=jnp.float32
    )
    grad_upq = jnp.einsum(
        "bsr,bsc->bcr", lowrank_in[:, :, :R], query_grad, preferred_element_type=jnp.float32
    )
    grad_upv = jnp.einsum(
        "bsr,bskgd->bkdr", lowrank_in[:, :, R:], value_five, preferred_element_type=jnp.float32
    )
    grad_upv = grad_upv.reshape(cand_count, kv_width, R)
    grad_rows = jnp.concatenate(
        [grad_down[:, :, :R], grad_down[:, :, R:], grad_upq, grad_upv], axis=1
    )
    bucket_ids = jnp.concatenate(
        [(block_rows * NT + tile_rows).reshape(-1), block_local * NT + tile_local]
    )
    out_blocks = K // PB
    block_sums = jax.ops.segment_sum(
        jnp.moveaxis(grad_rows, 1, 0), bucket_ids, num_segments=out_blocks * NT
    )
    block_sums = (
        block_sums.reshape(out_blocks, NT, cand_count, R)
        .transpose(2, 0, 1, 3)
        .reshape(cand_count, out_blocks, NT * R)
    )
    tile_table = tile_bank.astype(jnp.float32).reshape(NT * R, PB)
    projected = jnp.einsum(
        "bkj,jp->bkp", block_sums, tile_table, precision=lax.Precision.HIGHEST
    ).reshape(cand_count, K)
    feat_slice = lax.psum_scatter(
        projected.astype(jnp.bfloat16), "mp", scatter_dimension=1, tiled=True
    ).astype(jnp.float32)
    feat_square = jnp.sum(feat_slice * feat_slice, axis=1)
    feat_half = feat_slice.astype(jnp.bfloat16)
    partial_value = jnp.einsum(
        "bk,sk->bs",
        feat_half,
        lax.all_gather(seed_feats, "dp", axis=0, tiled=True),
        preferred_element_type=jnp.float32,
    )
    total_square = lax.psum(feat_square, "mp")
    numerator = lax.psum_scatter(partial_value, "mp", scatter_dimension=1, tiled=True)
    return numerator * lax.rsqrt(total_square / K + EPS)[:, None] * K ** (-0.5)


def solution(mesh):
    return jax.shard_map(
        local,
        mesh=mesh,
        in_specs=(
            P("dp", None, "mp"),
            P("dp", None, "mp"),
            P("dp", None, None),
            P("dp", None, None),
            P("dp", None, "mp"),
            P("dp", None),
            P("mp", None),
            P(None, "mp"),
            P("mp", None),
            P(),
            P(None, "mp"),
            P(None, "mp"),
            P(),
            P(),
            P(),
            P("dp", "mp"),
        ),
        out_specs=P("dp", "mp"),
        check_vma=False,
    )
```

profile of v0, /device:TPU:6, one launch (start us, length us, event | category | flops | bytes accessed | tf_op | source)
XLA Modules:
  0.0 423.8 jit_solution(10338486193786208510)
XLA Ops:
  7.5 1.1 constant_dynamic-slice_fusion
  8.7 2.5 fusion.22
  11.2 0.4 compare_and_fusion
  11.7 6.1 %fusion.55 = (f32[2,4,512]{2,1,0:T(4,128)S(1)}, f32[2,4,512,512]{2,3,1,0:T(8,128)}) fusion(f32[2,4,512,512]{3,2,1,0:T(8,128)S(1)} %fusion.22, pred[2,512,512]{1,2,0:T(8,128)(4,1)S(1)} %compare_and_fusion), kind=kOutput, calls=%fused_computation.71 | output fusion | flops 12583423 | bytes 17317888 | tf_op jit(solution)/shard_map/sub | solution.py:77
  17.8 4.8 %convert_reduce_fusion = bf16[2,512,128]{2,1,0:T(8,128)(2,1)S(1)} fusion(f32[2,4,512,512]{2,3,1,0:T(8,128)} %get-tuple-element.10, f32[2,4,512]{2,1,0:T(4,128)S(1)} %get-tuple-element.9, bf16[2,512,512]{2,1,0:T(8,128)(2,1)S(1)} %copy-done), kind=kOutput, calls=%fused_computation.18 | convolution fusion | flops 542507008 | bytes 9715712 | tf_op jit(solution)/shard_map/bhqk,bqhd->bkhd/dot_general | solution.py:79
  22.6 0.9 copy-done.9
  23.5 1.5 fusion.1
  25.1 1.6 multiply_convert_fusion
  26.7 0.3 fusion.44
  27.0 1.0 fusion.46
  28.0 1.1 pad_maximum_fusion
  29.1 1.0 copy.37
  30.1 1.7 copy.38
  31.7 2.4 convolution_bitcast_fusion
  34.1 89.0 %all-reduce.2 = (bf16[2,512,256]{1,2,0:T(8,128)(2,1)}, bf16[2,512,256]{1,2,0:T(8,128)(2,1)}) all-reduce(f32[2,512,256]{1,2,0:T(8,128)} %convolution_bitcast_fusion, f32[2,512,256]{1,2,0:T(8,128)} %pad_maximum_fusion), channel_id=1, replica_groups=mesh['dp'=32,'mp'=16] {'mp'}, use_global_device_ids=true, to_apply=%region_5.6 | all-reduce | flops 524288 | bytes 3145728 | tf_op jit(solution)/shard_map/psum | solution.py:102
  123.2 1.4 fusion.39
  124.6 1.2 fusion.37
  125.8 1.5 convolution_bitcast_fusion.1
  127.4 1.3 maximum_bitcast_fusion
  128.7 3.2 copy.44
  132.0 0.8 dynamic-slice_add_fusion
  132.9 60.0 %scatter_fusion = f32[512,2,128]{2,1,0:T(2,128)S(1)} fusion(f32[512,2,128]{2,1,0:T(2,128)S(1)} %broadcast_in_dim.12, s32[1664]{0:T(1024)S(1)} %pad_add_fusion, f32[1664,2,128]{2,1,0:T(2,128)S(1)} %copy.44), kind=kCustom, calls=%fused_computation | custom fusion | flops 425984 | bytes 5118464 | tf_op jit(solution)/shard_map/scatter-add | solution.py:122
  192.9 0.5 fusion.18
  193.4 1.9 copy.58
  195.4 0.5 all-gather.2.cloned.1.call-update
  196.0 92.8 %reduce-scatter.7.cloned.1.call-done = bf16[512,2]{1,0:T(8,128)(2,1)} async-done(((bf16[8192,2]{1,0:T(8,128)(2,1)}), bf16[512,2]{1,0:T(8,128)(2,1)}) %reduce-scatter.7.cloned.1.call-update) | async-done | bytes 2064
  288.8 1.0 copy.55
  289.9 32.1 %psum.23 = f32[2]{0:T(128)S(1)} all-reduce(f32[2]{0:T(128)S(1)} %multiply_reduce_fusion), channel_id=1, replica_groups=mesh['dp'=32,'mp'=16] {'mp'}, use_global_device_ids=true, to_apply=%region_10.11 | all-reduce | flops 2 | bytes 16 | tf_op jit(solution)/shard_map/psum | solution.py:145
  322.1 2.5 convolution_bitcast_fusion.2
  324.6 90.3 %reduce-scatter.9.cloned.1.call-done = f32[64,2]{1,0:T(8,128)} async-done(((f32[1024,2]{1,0:T(8,128)}), f32[64,2]{1,0:T(8,128)}) %reduce-scatter.9.cloned.1.call-update) | async-done | bytes 528
  414.9 0.8 copy.57
  415.7 0.6 multiply_multiply_fusion
  (34 shorter events, 0.8 us)
Async XLA Ops:
  7.4 10.4 %copy-start = (bf16[2,512,512]{2,1,0:T(8,128)(2,1)S(1)}, bf16[2,512,512]{2,1,0:T(8,128)(2,1)}, u32[]{:S(2)}) copy-start(bf16[2,512,512]{2,1,0:T(8,128)(2,1)} %param.20) | copy-start | bytes 3145732
  7.4 3.9 copy-start.6
  7.4 281.4 %reduce-scatter.7.cloned.1.call-start = ((), (), s32[]{:S(2)}) async-start(), calls=%async_computation.3 | async-start | bytes 2228224
  17.8 5.8 %copy-start.9 = (f32[2,4,512,512]{2,3,1,0:T(8,128)S(1)}, f32[2,4,512,512]{2,3,1,0:T(8,128)}, u32[]{:S(2)}) copy-start(f32[2,4,512,512]{2,3,1,0:T(8,128)} %get-tuple-element.10) | copy-start | bytes 25165828
  22.6 4.4 %copy-start.2 = (bf16[2,512,128]{2,1,0:T(8,128)(2,1)}, bf16[2,512,128]{2,1,0:T(8,128)(2,1)S(1)}, u32[]{:S(2)}) copy-start(bf16[2,512,128]{2,1,0:T(8,128)(2,1)S(1)} %convert_reduce_fusion) | copy-start | bytes 786436
  25.0 1.6 copy-start.5
  25.1 6.7 %copy-start.1 = (bf16[2,512,512]{2,1,0:T(8,128)(2,1)S(1)}, bf16[2,512,512]{2,1,0:T(8,128)(2,1)}, u32[]{:S(2)}) copy-start(bf16[2,512,512]{2,1,0:T(8,128)(2,1)} %param.16) | copy-start | bytes 3145732
  28.0 96.6 %copy-start.3 = (bf16[2,512,128]{2,1,0:T(8,128)(2,1)S(1)}, bf16[2,512,128]{2,1,0:T(8,128)(2,1)}, u32[]{:S(2)}) copy-start(bf16[2,512,128]{2,1,0:T(8,128)(2,1)} %copy-done.2) | copy-start | bytes 786436
  34.1 97.8 %copy-start.7 = (s32[3,512]{1,0:T(4,128)S(1)}, s32[3,512]{1,0:T(4,128)}, u32[]{:S(2)}) copy-start(s32[3,512]{1,0:T(4,128)} %param.27) | copy-start | bytes 18436
  34.1 97.8 %copy-start.8 = (s32[3,512]{1,0:T(4,128)S(1)}, s32[3,512]{1,0:T(4,128)}, u32[]{:S(2)}) copy-start(s32[3,512]{1,0:T(4,128)} %param.26) | copy-start | bytes 18436
  125.8 67.1 %copy-start.4 = (bf16[8,128,128]{2,1,0:T(8,128)(2,1)S(1)}, bf16[8,128,128]{2,1,0:T(8,128)(2,1)}, u32[]{:S(2)}) copy-start(bf16[8,128,128]{2,1,0:T(8,128)(2,1)} %param.30) | copy-start | bytes 786436
  195.4 126.7 %all-gather.2.cloned.1.call-start = ((), (), s32[]{:S(2)}) async-start(), calls=%async_computation.2 | async-start | bytes 1081344 | tf_op jit(solution)/shard_map/all_gather | solution.py:142
  196.0 219.0 %reduce-scatter.9.cloned.1.call-start = ((), (), s32[]{:S(2)}) async-start(), calls=%async_computation.4 | async-start | bytes 557056
Sparse Core Ops, SparseCore 0:
  195.5 93.2 reduce-scatter.6
  324.7 90.1 reduce-scatter.8
Sparse Core Ops, SparseCore 1:
  198.2 75.0 all-gather.1
where the time goes:
time: 424 us
  waiting for transfers between devices  184 us (43%)
  blocking collectives  121 us (29%)
  other arithmetic  70.5 us (17%)
  matrix products  21.3 us (5%)
  between operations  15.1 us (4%)
  local copies, waits for them, and re-layouts  12.1 us (3%)
    unnamed x5, waiting for transfers between devices  184 us
    psum x1, blocking collectives, local(): lowrank_in, lowrank_back = lax.psum((lowrank_part, back_part), 'mp')  89 us
    scatter-add x1, other arithmetic, local(): jax.ops.segment_sum(jnp.moveaxis(grad_rows, 1, 0), bucket_ids, num_segmen...  60 us
    psum x1, blocking collectives, local(): total_square = lax.psum(feat_square, 'mp')  32.1 us
  transfers between devices with their start and end apart: 3, of which 2 were waited for; matrix products, arithmetic and copies ran while one was open for 0% of the time, Pallas kernels for 0%

commit v1 on v0

v1 whole, which is shorter than its diff:
```python
import math

import jax
import jax.numpy as jnp
from jax import lax
from jax.experimental import pallas as pl
from jax.experimental.pallas import tpu as pltpu
from jax.sharding import PartitionSpec as P

H = 64
KVH = 8
DH = 128
R = 128
K = 8192
PB = 128
NT = 8
S = 512
KB = 64
EPS = 1e-06
LONGEST = 256
ROWS = 128
F32 = jnp.float32
BF16 = jnp.bfloat16


def dot_nn(a, b):
    return lax.dot_general(a, b, (((1,), (0,)), ((), ())), preferred_element_type=F32)


def dot_nt(a, b):
    return lax.dot_general(a, b, (((1,), (1,)), ((), ())), preferred_element_type=F32)


def attention_kernel(
    kv_index,
    hidden_ref,
    query_ref,
    grad_ref,
    key_ref,
    value_ref,
    segment_ref,
    down_query_ref,
    down_value_ref,
    up_query_ref,
    up_value_ref,
    send_ref,
    query_grad_ref,
    value_grad_ref,
    value_sum,
):
    cand = pl.program_id(0)
    parts = send_ref.shape[0]
    chunk = send_ref.shape[2]
    quarter = R // chunk
    heads = query_ref.shape[2] // DH
    score_scale = 1.0 / math.sqrt(DH)
    exp_scale = score_scale * math.log2(math.e)

    down = jnp.concatenate([down_query_ref[...].T, down_value_ref[...].T], axis=0)
    lowrank_in = dot_nt(down, hidden_ref[0])
    send_ref[0 : 2 * quarter, 0] = lowrank_in.astype(BF16).reshape(2 * quarter, chunk, S)

    segment_row = segment_ref[pl.ds(cand, 1), :].astype(F32)
    segment_col = jnp.broadcast_to(segment_row, (8, S)).T[:, 0:1]
    key = key_ref[0]
    value = value_ref[0]
    key_t = key.T
    value_sum[...] = jnp.zeros_like(value_sum)

    for block in range(S // ROWS):
        first = block * ROWS
        low = max(0, (first - LONGEST + 1) // ROWS * ROWS)
        high = first + ROWS
        width = high - low
        key_pos = low + lax.broadcasted_iota(jnp.int32, (width, ROWS), 0)
        row_pos = first + lax.broadcasted_iota(jnp.int32, (width, ROWS), 1)
        allowed = (key_pos <= row_pos) & (
            segment_col[low:high] == segment_row[:, first:high]
        )
        bias = jnp.where(allowed, 0.0, -1e30)
        for head in range(heads):
            cols = slice(head * DH, (head + 1) * DH)
            grad = grad_ref[0, first:high, cols]
            logits = dot_nt(key[low:high], query_ref[0, first:high, cols]) + bias
            row_top = jnp.max(logits, axis=0, keepdims=True)
            exp_terms = jnp.exp2((logits - row_top) * exp_scale)
            probs = exp_terms * (1.0 / jnp.sum(exp_terms, axis=0, keepdims=True))
            prob_grad = dot_nt(value[low:high], grad)
            row_delta = jnp.sum(probs * prob_grad, axis=0, keepdims=True)
            logit_grad = (probs * (prob_grad - row_delta)).astype(BF16)
            value_sum[low:high] += dot_nn(probs.astype(BF16), grad)
            query_grad = dot_nn(key_t[:, low:high], logit_grad) * score_scale
            query_grad_ref[0, cols, first:high] = query_grad.astype(BF16)

    value_grad = value_sum[...].astype(BF16)
    value_grad_ref[0] = value_grad
    back_query = dot_nn(up_query_ref[...], query_grad_ref[0])
    back_value = dot_nt(up_value_ref[...], value_grad)
    send_ref[2 * quarter : 3 * quarter, 0] = back_query.astype(BF16).reshape(quarter, chunk, S)
    send_ref[3 * quarter : parts, 0] = back_value.astype(BF16).reshape(quarter, chunk, S)


def sum_kernel(parts_ref, out_ref):
    total = jnp.sum(parts_ref[...].astype(F32), axis=0)
    out_ref[...] = jnp.broadcast_to(total.astype(BF16)[None], out_ref.shape)


def feature_kernel(
    kv_index,
    lowrank_ref,
    hidden_ref,
    query_grad_ref,
    value_grad_ref,
    block_ref,
    tile_ref,
    block_value_ref,
    tile_value_ref,
    bank_ref,
    out_ref,
):
    cands = hidden_ref.shape[0]
    kv = kv_index[0]
    pieces = [[], [], [], []]
    for cand in range(cands):
        lowrank = lowrank_ref[:, cand].reshape(4 * R, S)
        down = dot_nn(lowrank[2 * R :], hidden_ref[cand])
        pieces[0].append(down[:R])
        pieces[1].append(down[R:])
        pieces[2].append(dot_nt(lowrank[:R], query_grad_ref[cand]))
        pieces[3].append(dot_nn(lowrank[R : 2 * R], value_grad_ref[cand]))
    buckets = KB * NT
    sums = jnp.zeros((buckets, cands * R), F32)
    for kind in range(4):
        if kind < 3:
            ids = tile_ref[kind : kind + 1, :] * KB + block_ref[kind : kind + 1, :]
        else:
            ids = tile_value_ref[pl.ds(kv, 1), :] * KB + block_value_ref[pl.ds(kv, 1), :]
        rows = jnp.concatenate(pieces[kind], axis=0).astype(BF16)
        where = lax.broadcasted_iota(jnp.int32, (buckets, rows.shape[1]), 0)
        chosen = jnp.where(where == ids, 1.0, 0.0).astype(BF16)
        sums = sums + dot_nt(chosen, rows)
    wide = jnp.concatenate(
        [
            jnp.concatenate(
                [sums[t * KB : (t + 1) * KB, c * R : (c + 1) * R] for t in range(NT)], axis=1
            )
            for c in range(cands)
        ],
        axis=0,
    )
    high = wide.astype(BF16)
    low = (wide - high.astype(F32)).astype(BF16)
    bank = bank_ref[...].reshape(NT * R, PB)
    feats = dot_nn(high, bank) + dot_nn(low, bank)
    out_ref[...] = jnp.broadcast_to(feats.astype(BF16)[None], out_ref.shape)


def score_kernel(parts_ref, seeds_ref, out_ref):
    cands = out_ref.shape[0]
    seeds = out_ref.shape[1]
    feats = jnp.sum(parts_ref[...].astype(F32), axis=0)
    per_part = seeds_ref.shape[2] // PB
    totals = [jnp.zeros((seeds, PB), F32) for _ in range(cands)]
    for block in range(KB):
        at = block % per_part * PB
        seed = seeds_ref[block // per_part, :, at : at + PB].astype(F32)
        for c in range(cands):
            row = c * KB + block
            totals[c] = totals[c] + feats[row : row + 1] * seed
    for c in range(cands):
        mine = feats[c * KB : (c + 1) * KB]
        square = jnp.sum(jnp.sum(mine * mine, axis=0, keepdims=True), axis=1, keepdims=True)
        numerator = jnp.sum(totals[c].T, axis=0, keepdims=True)
        out_ref[c : c + 1, :] = numerator * lax.rsqrt(square / K + EPS) * K ** (-0.5)


VMEM = pl.BlockSpec(memory_space=pltpu.VMEM)
SMEM = pl.BlockSpec(memory_space=pltpu.SMEM)
PARAMS = pltpu.CompilerParams(vmem_limit_bytes=40 << 20)


def local(
    hidden_in,
    query_act,
    key_act,
    value_act,
    ctx_grad,
    segment_ids,
    down_query,
    up_query,
    down_value,
    up_value,
    block_rows,
    tile_rows,
    block_value,
    tile_value,
    tile_bank,
    seed_feats,
):
    model_index = lax.axis_index("mp")
    data_size = lax.axis_size("dp")
    model_size = lax.axis_size("mp")
    cands, seq_len, width = query_act.shape
    heads = width // DH
    kv = (model_index * heads // (H // KVH)).astype(jnp.int32)
    kv_index = kv.reshape(1)
    seeds_dev = seed_feats.shape[0]
    out_seeds = data_size * seeds_dev // model_size

    seed_moved = lax.ppermute(
        seed_feats,
        ("dp", "mp"),
        [
            (d * model_size + m, (m * 2 + d % 2) * model_size + d // 2)
            for d in range(data_size)
            for m in range(model_size)
        ],
    )
    seed_pair = lax.all_gather(
        seed_moved,
        "dp",
        axis=0,
        tiled=True,
        axis_index_groups=[[2 * z, 2 * z + 1] for z in range(data_size // 2)],
    )
    seeds_all = lax.all_gather(
        seed_pair,
        "dp",
        axis=0,
        tiled=False,
        axis_index_groups=[[2 * z + core for z in range(data_size // 2)] for core in range(2)],
    )

    chunk = 4 * R // model_size

    def per_cand(*shape):
        return pl.BlockSpec((1, *shape), lambda c, kv_ref: (c, 0, 0))

    def whole(*shape):
        return pl.BlockSpec(shape, lambda c, kv_ref: (0,) * len(shape))

    send, query_grad, value_grad = pl.pallas_call(
        attention_kernel,
        name="attention_backward",
        out_shape=(
            jax.ShapeDtypeStruct((model_size, cands, chunk, seq_len), BF16),
            jax.ShapeDtypeStruct((cands, width, seq_len), BF16),
            jax.ShapeDtypeStruct((cands, seq_len, DH), BF16),
        ),
        grid_spec=pltpu.PrefetchScalarGridSpec(
            num_scalar_prefetch=1,
            grid=(cands,),
            in_specs=[
                per_cand(seq_len, hidden_in.shape[2]),
                per_cand(seq_len, width),
                per_cand(seq_len, width),
                pl.BlockSpec((1, seq_len, DH), lambda c, kv_ref: (c, 0, kv_ref[0])),
                pl.BlockSpec((1, seq_len, DH), lambda c, kv_ref: (c, 0, kv_ref[0])),
                whole(cands, seq_len),
                whole(*down_query.shape),
                whole(*down_value.shape),
                whole(*up_query.shape),
                pl.BlockSpec((R, DH), lambda c, kv_ref: (0, kv_ref[0])),
            ],
            out_specs=[
                pl.BlockSpec((model_size, 1, chunk, seq_len), lambda c, kv_ref: (0, c, 0, 0)),
                per_cand(width, seq_len),
                per_cand(seq_len, DH),
            ],
            scratch_shapes=[pltpu.VMEM((seq_len, DH), F32)],
        ),
        compiler_params=PARAMS,
        cost_estimate=pl.CostEstimate(
            flops=5_000_000_000, bytes_accessed=8_000_000, transcendentals=2_000_000
        ),
    )(
        kv_index,
        hidden_in,
        query_act,
        ctx_grad,
        key_act,
        value_act,
        segment_ids,
        down_query,
        down_value,
        up_query,
        up_value,
    )

    received = lax.all_to_all(send, "mp", 0, 0, tiled=True)
    summed = pl.pallas_call(
        sum_kernel,
        name="lowrank_sum",
        out_shape=jax.ShapeDtypeStruct(received.shape, BF16),
        in_specs=[VMEM],
        out_specs=VMEM,
        compiler_params=PARAMS,
    )(received)
    lowrank = lax.all_to_all(summed, "mp", 0, 0, tiled=True)

    feat_parts = pl.pallas_call(
        feature_kernel,
        name="partial_features",
        out_shape=jax.ShapeDtypeStruct((model_size, cands * KB, PB), BF16),
        in_specs=[SMEM] + [VMEM] * 9,
        out_specs=VMEM,
        compiler_params=PARAMS,
    )(
        kv_index,
        lowrank,
        hidden_in,
        query_grad,
        value_grad,
        block_rows,
        tile_rows,
        block_value.reshape(KVH, DH),
        tile_value.reshape(KVH, DH),
        tile_bank,
    )
    feat_all = lax.all_to_all(feat_parts, "mp", 0, 0, tiled=True)

    return pl.pallas_call(
        score_kernel,
        name="scores",
        out_shape=jax.ShapeDtypeStruct((cands, out_seeds), F32),
        in_specs=[VMEM, VMEM],
        out_specs=VMEM,
        compiler_params=PARAMS,
    )(feat_all, seeds_all)


def solution(mesh):
    return jax.shard_map(
        local,
        mesh=mesh,
        in_specs=(
            P("dp", None, "mp"),
            P("dp", None, "mp"),
            P("dp", None, None),
            P("dp", None, None),
            P("dp", None, "mp"),
            P("dp", None),
            P("mp", None),
            P(None, "mp"),
            P("mp", None),
            P(),
            P(None, "mp"),
            P(None, "mp"),
            P(),
            P(),
            P(),
            P("dp", "mp"),
        ),
        out_specs=P("dp", "mp"),
        check_vma=False,
    )
```

time: 424 us -> 142 us (0.33)
  the two profiles are of different devices: /device:TPU:6 before, /device:TPU:2 now
where the time goes in v1:
time: 142 us; the launch traced here: 141 us
  waiting for transfers between devices  46 us (32%)
  blocking collectives  30.7 us (22%)
  starting transfers between devices  22.1 us (16%)
  Pallas kernels  16 us (11%)
  between operations  13.5 us (10%)
  local copies, waits for them, and re-layouts  13.2 us (9%)
    all_gather x1, waiting for transfers between devices, local(): lax.all_gather(seed_pair, 'dp', axis=0, tiled=False, axis_index_groups=[[...  41.5 us
    all_to_all x1, blocking collectives, local(): lowrank = lax.all_to_all(summed, 'mp', 0, 0, tiled=True)  28.8 us
    unnamed x40, local copies, waits for them, and re-layouts  13.2 us
    pallas_call x1, Pallas kernels, local(): pl.pallas_call(attention_kernel, name='attention_backward', out_shape=(ja...  12.1 us
    all_to_all x1, starting transfers between devices, local(): received = lax.all_to_all(send, 'mp', 0, 0, tiled=True)  9.5 us
    ppermute x1, starting transfers between devices, local(): lax.ppermute(seed_feats, ('dp', 'mp'), [(d * model_size + m, (m * 2 + d %...  6.75 us
    all_to_all x1, starting transfers between devices, local(): feat_all = lax.all_to_all(feat_parts, 'mp', 0, 0, tiled=True)  5.77 us
    ppermute x1, waiting for transfers between devices, local(): lax.ppermute(seed_feats, ('dp', 'mp'), [(d * model_size + m, (m * 2 + d %...  3.96 us
  transfers between devices with their start and end apart: 4, of which 3 were waited for; matrix products, arithmetic and copies ran while one was open for 0% of the time, Pallas kernels for 2%

profile of v1, /device:TPU:2, one launch (start us, length us, event | category | flops | bytes accessed | tf_op | source)
XLA Modules:
  0.0 141.4 jit_solution(15981897234133899816)
XLA Ops:
  6.5 1.2 copy-done
  7.8 1.6 %copy-done.10 = bf16[2,512,1024]{2,1,0:T(8,128)(2,1)S(1)} copy-done((bf16[2,512,1024]{2,1,0:T(8,128)(2,1)S(1)}, bf16[2,512,1024]{2,1,0:T(8,128)(2,1)}, u32[]{:S(2)}) %copy-start.10) | copy-done | bytes 2097176
  9.4 1.6 %copy-done.11 = bf16[2,512,1024]{2,1,0:T(8,128)(2,1)S(1)} copy-done((bf16[2,512,1024]{2,1,0:T(8,128)(2,1)S(1)}, bf16[2,512,1024]{2,1,0:T(8,128)(2,1)}, u32[]{:S(2)}) %copy-start.11) | copy-done | bytes 2097176
  10.9 1.2 copy-done.12
  12.2 1.2 copy-done.13
  13.4 0.9 copy-done.14
  14.3 0.9 copy-done.15
  15.3 0.9 copy-done.16
  16.2 0.9 copy-done.17
  17.1 0.7 copy-done.18
  17.7 12.1 %attention_backward.1 = (bf16[16,2,32,512]{3,2,1,0:T(8,128)(2,1)}, bf16[2,512,512]{2,1,0:T(8,128)(2,1)S(1)}, bf16[2,512,128]{2,1,0:T(8,128)(2,1)S(1)}) custom-call(s32[1]{0:T(128)} %bitcast.kv_index, bf16[2,512,512]{2,1,0:T(8,128)(2,1)S(1)} %copy-done, bf16[2,512,512]{2,1,0:T(8,128)(2,1)S(1)} %copy-done.12, bf16[2,512,512]{2,1,0:T(8,128)(2,1)S(1)} %copy-done.13, ...), custom_call_target="tpu_custom_call" | custom-call | flops 5000000000 | bytes 8000000 | tf_op jit(solution)/shard_map/attention_backward/pallas_call | solution.py:242
  29.9 0.7 copy-done.4
  30.6 9.5 %all-to-all-start = ((bf16[16,2,32,512]{3,2,1,0:T(8,128)(2,1)}), bf16[16,2,32,512]{3,2,1,0:T(8,128)(2,1)S(1)}, u32[]{:S(2)}, u32[]{:S(2)}) async-start(bf16[16,2,32,512]{3,2,1,0:T(8,128)(2,1)} %get-tuple-element.8), calls=%async_computation | async-start | bytes 2097152 | tf_op jit(solution)/shard_map/all_to_all | solution.py:290
  40.1 0.0 all-gather.3.cloned.1.call-start
  40.1 6.8 %collective-permute-start = (bf16[32,512]{1,0:T(8,128)(2,1)S(1)}, bf16[32,512]{1,0:T(8,128)(2,1)S(1)}, u32[]{:S(2)}, u32[]{:S(2)}) collective-permute-start(bf16[32,512]{1,0:T(8,128)(2,1)S(1)} %copy-done.19), channel_id=1, source_target_pairs={{0,0},{1,32},{2,64},{3,96},{4,128},{5,160},{6,192},{7,224},{8,256}... | collective-permute-start | bytes 98312 | tf_op jit(solution)/shard_map/ppermute | solution.py:210
  46.9 4.0 %collective-permute-done = bf16[32,512]{1,0:T(8,128)(2,1)S(1)} collective-permute-done((bf16[32,512]{1,0:T(8,128)(2,1)S(1)}, bf16[32,512]{1,0:T(8,128)(2,1)S(1)}, u32[]{:S(2)}, u32[]{:S(2)}) %collective-permute-start) | collective-permute-done | bytes 32800 | tf_op jit(solution)/shard_map/ppermute | solution.py:210
  50.9 2.0 %all_gather.9 = bf16[64,512]{1,0:T(8,128)(2,1)} all-gather(bf16[32,512]{1,0:T(8,128)(2,1)S(1)} %collective-permute-done), channel_id=1, replica_groups={{0,16},{32,48},{64,80},{96,112},{128,144},{160,176},{192,208},{224,240}..., dimensions={0}, use_global_device_ids=true | all-gather | bytes 98304 | tf_op jit(solution)/shard_map/all_gather | solution.py:219
  52.8 0.0 all-gather.3.cloned.1.call-update
  52.9 0.0 copy-start.1
  52.9 0.0 copy-start.3
  52.9 0.0 copy-start.6
  52.9 0.0 copy-start.7
  52.9 0.0 copy-start.8
  52.9 0.0 copy-start.9
  52.9 0.5 all-to-all-done.parts_ref
  53.4 0.2 lowrank_sum.1
  53.6 28.8 %all_to_all.15.lowrank_ref = bf16[16,2,32,512]{3,2,1,0:T(8,128)(2,1)S(1)} all-to-all(bf16[16,2,32,512]{3,2,1,0:T(8,128)(2,1)S(1)} %lowrank_sum.1), channel_id=1, replica_groups=mesh['dp'=32,'mp'=16] {'mp'}, dimensions={0} | all-to-all | bytes 2097152 | tf_op jit(solution)/shard_map/all_to_all | solution.py:299
  82.4 2.5 %partial_features.1 = bf16[16,128,128]{2,1,0:T(8,128)(2,1)} custom-call(s32[1]{0:T(128)} %bitcast.kv_index, bf16[16,2,32,512]{3,2,1,0:T(8,128)(2,1)S(1)} %all_to_all.15.lowrank_ref, bf16[2,512,512]{2,1,0:T(8,128)(2,1)S(1)} %copy-done.1, bf16[2,512,512]{2,1,0:T(8,128)(2,1)S(1)} %get-tuple-element.9.query_grad_ref, bf16[2,512,128]{2,1,0:T(8,128)(2,1)S(1)} %copy-done.5, ...), custom_call_target="tpu_custom_call" | custom-call | tf_op jit(solution)/shard_map/partial_features/pallas_call | solution.py:301
  84.9 5.8 %all-to-all-start.2 = ((bf16[16,128,128]{2,1,0:T(8,128)(2,1)}), bf16[16,128,128]{2,1,0:T(8,128)(2,1)S(1)}, u32[]{:S(2)}, u32[]{:S(2)}) async-start(bf16[16,128,128]{2,1,0:T(8,128)(2,1)} %partial_features.1), calls=%async_computation.2 | async-start | bytes 1048576 | tf_op jit(solution)/shard_map/all_to_all | solution.py:320
  90.7 41.5 %all-gather.3.cloned.1.call-done = bf16[1024,512]{1,0:T(8,128)(2,1)} async-done(((bf16[64,512]{1,0:T(8,128)(2,1)}), bf16[1024,512]{1,0:T(8,128)(2,1)}) %all-gather.3.cloned.1.call-update) | async-done | bytes 1048592 | tf_op jit(solution)/shard_map/all_gather | solution.py:226
  132.2 1.2 copy-done.2
  133.4 1.2 scores.1
  (23 shorter events, 0.0 us)
Async XLA Ops:
  6.5 1.2 copy-start
  7.8 1.6 %copy-start.10 = (bf16[2,512,1024]{2,1,0:T(8,128)(2,1)S(1)}, bf16[2,512,1024]{2,1,0:T(8,128)(2,1)}, u32[]{:S(2)}) copy-start(bf16[2,512,1024]{2,1,0:T(8,128)(2,1)} %key_ref.1) | copy-start | bytes 6291460
  9.4 1.6 %copy-start.11 = (bf16[2,512,1024]{2,1,0:T(8,128)(2,1)S(1)}, bf16[2,512,1024]{2,1,0:T(8,128)(2,1)}, u32[]{:S(2)}) copy-start(bf16[2,512,1024]{2,1,0:T(8,128)(2,1)} %value_ref.1) | copy-start | bytes 6291460
  10.9 1.2 copy-start.12
  12.2 1.2 copy-start.13
  13.4 0.9 copy-start.14
  14.3 0.9 copy-start.15
  15.2 0.9 copy-start.16
  16.2 0.9 copy-start.17
  17.1 0.7 copy-start.18
  29.9 0.7 copy-start.4
  30.6 9.6 %copy-start.19 = (bf16[32,512]{1,0:T(8,128)(2,1)S(1)}, bf16[32,512]{1,0:T(8,128)(2,1)}, u32[]{:S(2)}) copy-start(bf16[32,512]{1,0:T(8,128)(2,1)} %param.31) | copy-start | bytes 98308
  30.6 22.8 %all-to-all-start = ((bf16[16,2,32,512]{3,2,1,0:T(8,128)(2,1)}), bf16[16,2,32,512]{3,2,1,0:T(8,128)(2,1)S(1)}, u32[]{:S(2)}, u32[]{:S(2)}) async-start(bf16[16,2,32,512]{3,2,1,0:T(8,128)(2,1)} %get-tuple-element.8), calls=%async_computation | async-start | bytes 2097152 | tf_op jit(solution)/shard_map/all_to_all | solution.py:290
  40.1 92.1 %all-gather.3.cloned.1.call-start = ((), (), s32[]{:S(2)}) async-start(), calls=%async_computation.3 | async-start | bytes 1114112 | tf_op jit(solution)/shard_map/all_gather | solution.py:226
  40.1 10.7 %collective-permute-start = (bf16[32,512]{1,0:T(8,128)(2,1)S(1)}, bf16[32,512]{1,0:T(8,128)(2,1)S(1)}, u32[]{:S(2)}, u32[]{:S(2)}) collective-permute-start(bf16[32,512]{1,0:T(8,128)(2,1)S(1)} %copy-done.19), channel_id=1, source_target_pairs={{0,0},{1,32},{2,64},{3,96},{4,128},{5,160},{6,192},{7,224},{8,256}... | collective-permute-start | bytes 98312 | tf_op jit(solution)/shard_map/ppermute | solution.py:210
  52.9 29.5 %copy-start.1 = (bf16[2,512,512]{2,1,0:T(8,128)(2,1)S(1)}, bf16[2,512,512]{2,1,0:T(8,128)(2,1)}, u32[]{:S(2)}) copy-start(bf16[2,512,512]{2,1,0:T(8,128)(2,1)} %hidden_ref.3) | copy-start | bytes 3145732
  52.9 29.5 %copy-start.3 = (bf16[8,128,128]{2,1,0:T(8,128)(2,1)S(1)}, bf16[8,128,128]{2,1,0:T(8,128)(2,1)}, u32[]{:S(2)}) copy-start(bf16[8,128,128]{2,1,0:T(8,128)(2,1)} %bank_ref.1) | copy-start | bytes 786436
  52.9 29.5 %copy-start.6 = (s32[3,512]{1,0:T(4,128)S(1)}, s32[3,512]{1,0:T(4,128)}, u32[]{:S(2)}) copy-start(s32[3,512]{1,0:T(4,128)} %block_ref.1) | copy-start | bytes 18436
  52.9 29.5 %copy-start.7 = (s32[3,512]{1,0:T(4,128)S(1)}, s32[3,512]{1,0:T(4,128)}, u32[]{:S(2)}) copy-start(s32[3,512]{1,0:T(4,128)} %tile_ref.1) | copy-start | bytes 18436
  52.9 29.5 %copy-start.8 = (s32[1024]{0:T(1024)S(1)}, s32[1024]{0:T(1024)}, u32[]{:S(2)}) copy-start(s32[1024]{0:T(1024)} %param.28) | copy-start | bytes 12292
  52.9 29.5 %copy-start.9 = (s32[1024]{0:T(1024)S(1)}, s32[1024]{0:T(1024)}, u32[]{:S(2)}) copy-start(s32[1024]{0:T(1024)} %param.29) | copy-start | bytes 12292
  53.4 29.0 %copy-start.5 = (bf16[2,512,128]{2,1,0:T(8,128)(2,1)S(1)}, bf16[2,512,128]{2,1,0:T(8,128)(2,1)}, u32[]{:S(2)}) copy-start(bf16[2,512,128]{2,1,0:T(8,128)(2,1)} %copy-done.4) | copy-start | bytes 786436
  84.9 47.3 %all-to-all-start.2 = ((bf16[16,128,128]{2,1,0:T(8,128)(2,1)}), bf16[16,128,128]{2,1,0:T(8,128)(2,1)S(1)}, u32[]{:S(2)}, u32[]{:S(2)}) async-start(bf16[16,128,128]{2,1,0:T(8,128)(2,1)} %partial_features.1), calls=%async_computation.2 | async-start | bytes 1048576 | tf_op jit(solution)/shard_map/all_to_all | solution.py:320
  132.2 1.2 copy-start.2
Sparse Core Ops, SparseCore 0:
  53.0 79.1 all-gather.2

commit v2 on v1

--- a/solution.py
+++ b/solution.py
@@ -155,22 +155,28 @@
     out_ref[...] = jnp.broadcast_to(feats.astype(BF16)[None], out_ref.shape)
 
 
-def score_kernel(parts_ref, seeds_ref, out_ref):
+def score_kernel(core_index, parts_ref, mine_ref, other_ref, out_ref):
     cands = out_ref.shape[0]
-    seeds = out_ref.shape[1]
+    seeds = mine_ref.shape[1]
     feats = jnp.sum(parts_ref[...].astype(F32), axis=0)
-    per_part = seeds_ref.shape[2] // PB
-    totals = [jnp.zeros((seeds, PB), F32) for _ in range(cands)]
+    per_part = mine_ref.shape[2] // PB
+    totals = [[jnp.zeros((seeds, PB), F32) for _ in range(2)] for _ in range(cands)]
     for block in range(KB):
         at = block % per_part * PB
-        seed = seeds_ref[block // per_part, :, at : at + PB].astype(F32)
-        for c in range(cands):
-            row = c * KB + block
-            totals[c] = totals[c] + feats[row : row + 1] * seed
+        for half, seeds_ref in enumerate((mine_ref, other_ref)):
+            seed = seeds_ref[block // per_part, :, at : at + PB].astype(F32)
+            for c in range(cands):
+                row = c * KB + block
+                totals[c][half] = totals[c][half] + feats[row : row + 1] * seed
+    first_core = core_index[0] == 0
     for c in range(cands):
         mine = feats[c * KB : (c + 1) * KB]
         square = jnp.sum(jnp.sum(mine * mine, axis=0, keepdims=True), axis=1, keepdims=True)
-        numerator = jnp.sum(totals[c].T, axis=0, keepdims=True)
+        here, there = totals[c]
+        ordered = jnp.concatenate(
+            [jnp.where(first_core, here, there), jnp.where(first_core, there, here)], axis=0
+        )
+        numerator = jnp.sum(ordered.T, axis=0, keepdims=True)
         out_ref[c : c + 1, :] = numerator * lax.rsqrt(square / K + EPS) * K ** (-0.5)
 
 
@@ -216,21 +222,6 @@
             for m in range(model_size)
         ],
     )
-    seed_pair = lax.all_gather(
-        seed_moved,
-        "dp",
-        axis=0,
-        tiled=True,
-        axis_index_groups=[[2 * z, 2 * z + 1] for z in range(data_size // 2)],
-    )
-    seeds_all = lax.all_gather(
-        seed_pair,
-        "dp",
-        axis=0,
-        tiled=False,
-        axis_index_groups=[[2 * z + core for z in range(data_size // 2)] for core in range(2)],
-    )
-
     chunk = 4 * R // model_size
 
     def per_cand(*shape):
@@ -269,7 +260,7 @@
             ],
             scratch_shapes=[pltpu.VMEM((seq_len, DH), F32)],
         ),
-        compiler_params=PARAMS,
+        compiler_params=pltpu.CompilerParams(vmem_limit_bytes=60 << 20),
         cost_estimate=pl.CostEstimate(
             flops=5_000_000_000, bytes_accessed=8_000_000, transcendentals=2_000_000
         ),
@@ -287,7 +278,19 @@
         up_value,
     )
 
+    send, seed_moved = lax.optimization_barrier((send, seed_moved))
     received = lax.all_to_all(send, "mp", 0, 0, tiled=True)
+    levels = data_size // 2
+    seeds_core = lax.all_to_all(
+        jnp.broadcast_to(seed_moved[None], (levels, *seed_moved.shape)),
+        "dp",
+        0,
+        0,
+        tiled=True,
+        axis_index_groups=[[2 * z + core for z in range(levels)] for core in range(2)],
+    )
+    seeds_other = lax.ppermute(seeds_core, "dp", [(d, d ^ 1) for d in range(data_size)])
+    core_index = (lax.axis_index("dp") % 2).astype(jnp.int32).reshape(1)
     summed = pl.pallas_call(
         sum_kernel,
         name="lowrank_sum",
@@ -323,10 +326,10 @@
         score_kernel,
         name="scores",
         out_shape=jax.ShapeDtypeStruct((cands, out_seeds), F32),
-        in_specs=[VMEM, VMEM],
+        in_specs=[SMEM, VMEM, VMEM, VMEM],
         out_specs=VMEM,
         compiler_params=PARAMS,
-    )(feat_all, seeds_all)
+    )(core_index, feat_all, seeds_core, seeds_other)
 
 
 def solution(mesh):

time: 142 us -> 124 us (0.87)
  the two profiles are of different devices: /device:TPU:2 before, /device:TPU:32 now
where the time goes in v2:
time: 124 us; the launch traced here: 123 us
  waiting for transfers between devices  46.5 us (38%)
  blocking collectives  35.2 us (28%)
  starting transfers between devices  19.8 us (16%)
  Pallas kernels  18.7 us (15%)
  local copies, waits for them, and re-layouts  3.07 us (2%)
    all_to_all x1, blocking collectives, local(): received = lax.all_to_all(send, 'mp', 0, 0, tiled=True)  35.2 us
    all_to_all x1, waiting for transfers between devices, local(): lax.all_to_all(jnp.broadcast_to(seed_moved[None], (levels, *seed_moved.sh...  25.5 us
    pallas_call x1, Pallas kernels, local(): pl.pallas_call(attention_kernel, name='attention_backward', out_shape=(ja...  13.8 us
    all_to_all x1, waiting for transfers between devices, local(): lowrank = lax.all_to_all(summed, 'mp', 0, 0, tiled=True)  11 us
    all_to_all x1, waiting for transfers between devices, local(): feat_all = lax.all_to_all(feat_parts, 'mp', 0, 0, tiled=True)  10.1 us
    all_to_all x1, starting transfers between devices, local(): lax.all_to_all(jnp.broadcast_to(seed_moved[None], (levels, *seed_moved.sh...  7.34 us
    all_to_all x1, starting transfers between devices, local(): lowrank = lax.all_to_all(summed, 'mp', 0, 0, tiled=True)  3.95 us
    all_to_all x1, starting transfers between devices, local(): feat_all = lax.all_to_all(feat_parts, 'mp', 0, 0, tiled=True)  3.57 us
  transfers between devices with their start and end apart: 5, of which 3 were waited for; matrix products, arithmetic and copies ran while one was open for 0% of the time, Pallas kernels for 14%

profile of v2, /device:TPU:32, one launch (start us, length us, event | category | flops | bytes accessed | tf_op | source)
XLA Modules:
  0.0 123.5 jit_solution(17639661195102066199)
XLA Ops:
  0.0 3.0 %collective-permute-start = (bf16[32,512]{1,0:T(8,128)(2,1)}, bf16[32,512]{1,0:T(8,128)(2,1)S(1)}, u32[]{:S(2)}, u32[]{:S(2)}) collective-permute-start(bf16[32,512]{1,0:T(8,128)(2,1)} %param.31), channel_id=1, source_target_pairs={{0,0},{1,32},{2,64},{3,96},{4,128},{5,160},{6,192},{7,224},{8,256}... | collective-permute-start | bytes 98312 | tf_op jit(solution)/shard_map/ppermute | solution.py:216
  3.0 13.8 %attention_backward.1 = (bf16[16,2,32,512]{3,2,1,0:T(8,128)(2,1)}, bf16[2,512,512]{2,1,0:T(8,128)(2,1)}, bf16[2,512,128]{2,1,0:T(8,128)(2,1)}) custom-call(s32[1]{0:T(128)} %bitcast.1.kv_index, bf16[2,512,512]{2,1,0:T(8,128)(2,1)} %hidden_ref.3, bf16[2,512,512]{2,1,0:T(8,128)(2,1)} %query_ref.1, bf16[2,512,512]{2,1,0:T(8,128)(2,1)} %grad_ref.1, ...), custom_call_target="tpu_custom_call" | custom-call | flops 5000000000 | bytes 8000000 | tf_op jit(solution)/shard_map/attention_backward/pallas_call | solution.py:233
  16.9 0.0 collective-permute-done
  16.9 35.2 %all_to_all.20.parts_ref = bf16[16,2,32,512]{3,2,1,0:T(8,128)(2,1)S(1)} all-to-all(bf16[16,2,32,512]{3,2,1,0:T(8,128)(2,1)} %get-tuple-element.11), channel_id=1, replica_groups=mesh['dp'=32,'mp'=16] {'mp'}, dimensions={0} | all-to-all | bytes 2097152 | tf_op jit(solution)/shard_map/all_to_all | solution.py:282
  52.1 0.9 broadcast_in_dim.2
  53.0 7.3 %all-to-all-start.3 = ((bf16[16,32,512]{2,1,0:T(8,128)(2,1)}), bf16[16,32,512]{2,1,0:T(8,128)(2,1)S(1)}, u32[]{:S(2)}, u32[]{:S(2)}) async-start(bf16[16,32,512]{2,1,0:T(8,128)(2,1)} %broadcast_in_dim.2), calls=%async_computation.3 | async-start | bytes 1048576 | tf_op jit(solution)/shard_map/all_to_all | solution.py:284
  60.3 0.0 copy-start
  60.3 0.0 copy-start.2
  60.3 0.0 copy-start.4
  60.3 0.0 copy-start.5
  60.3 0.0 copy-start.6
  60.3 0.0 copy-start.7
  60.4 1.2 lowrank_sum.1
  61.5 25.5 %all-to-all-done.3.mine_ref = bf16[16,32,512]{2,1,0:T(8,128)(2,1)S(1)} async-done(((bf16[16,32,512]{2,1,0:T(8,128)(2,1)}), bf16[16,32,512]{2,1,0:T(8,128)(2,1)S(1)}, u32[]{:S(2)}, u32[]{:S(2)}) %all-to-all-start.3) | async-done | bytes 524320 | tf_op jit(solution)/shard_map/all_to_all | solution.py:284
  87.0 3.9 %all-to-all-start.1 = ((bf16[16,2,32,512]{3,2,1,0:T(8,128)(2,1)}), bf16[16,2,32,512]{3,2,1,0:T(8,128)(2,1)S(1)}, u32[]{:S(2)}, u32[]{:S(2)}) async-start(bf16[16,2,32,512]{3,2,1,0:T(8,128)(2,1)} %lowrank_sum.1), calls=%async_computation.1 | async-start | bytes 2097152 | tf_op jit(solution)/shard_map/all_to_all | solution.py:302
  91.0 1.9 %collective-permute-start.1 = (bf16[16,32,512]{2,1,0:T(8,128)(2,1)S(1)}, bf16[16,32,512]{2,1,0:T(8,128)(2,1)S(1)}, u32[]{:S(2)}, u32[]{:S(2)}) collective-permute-start(bf16[16,32,512]{2,1,0:T(8,128)(2,1)S(1)} %all-to-all-done.3.mine_ref), channel_id=1, source_target_pairs={{0,16},{16,0},{32,48},{48,32},{64,80},{80,64},{96,112},{112,96},{1... | collective-permute-start | bytes 1572872 | tf_op jit(solution)/shard_map/ppermute | solution.py:292
  92.9 11.0 %all-to-all-done.1.lowrank_ref = bf16[16,2,32,512]{3,2,1,0:T(8,128)(2,1)S(1)} async-done(((bf16[16,2,32,512]{3,2,1,0:T(8,128)(2,1)}), bf16[16,2,32,512]{3,2,1,0:T(8,128)(2,1)S(1)}, u32[]{:S(2)}, u32[]{:S(2)}) %all-to-all-start.1) | async-done | bytes 1048608 | tf_op jit(solution)/shard_map/all_to_all | solution.py:302
  103.9 0.0 copy-done
  103.9 0.0 copy-done.2
  103.9 0.0 copy-done.4
  103.9 0.0 copy-done.5
  103.9 0.0 copy-done.6
  103.9 0.0 copy-done.7
  103.9 0.0 copy-start.1
  103.9 1.2 copy-done.1
  105.2 0.0 copy-start.3
  105.2 0.9 copy-done.3
  106.1 2.5 %partial_features.1 = bf16[16,128,128]{2,1,0:T(8,128)(2,1)} custom-call(s32[1]{0:T(128)} %bitcast.1.kv_index, bf16[16,2,32,512]{3,2,1,0:T(8,128)(2,1)S(1)} %all-to-all-done.1.lowrank_ref, bf16[2,512,512]{2,1,0:T(8,128)(2,1)S(1)} %copy-done, bf16[2,512,512]{2,1,0:T(8,128)(2,1)S(1)} %copy-done.1, bf16[2,512,128]{2,1,0:T(8,128)(2,1)S(1)} %copy-done.3, ...), custom_call_target="tpu_custom_call" | custom-call | tf_op jit(solution)/shard_map/partial_features/pallas_call | solution.py:304
  108.6 3.6 %all-to-all-start.2 = ((bf16[16,128,128]{2,1,0:T(8,128)(2,1)}), bf16[16,128,128]{2,1,0:T(8,128)(2,1)S(1)}, u32[]{:S(2)}, u32[]{:S(2)}) async-start(bf16[16,128,128]{2,1,0:T(8,128)(2,1)} %partial_features.1), calls=%async_computation.2 | async-start | bytes 1048576 | tf_op jit(solution)/shard_map/all_to_all | solution.py:323
  112.2 10.1 %all-to-all-done.2.parts_ref = bf16[16,128,128]{2,1,0:T(8,128)(2,1)S(1)} async-done(((bf16[16,128,128]{2,1,0:T(8,128)(2,1)}), bf16[16,128,128]{2,1,0:T(8,128)(2,1)S(1)}, u32[]{:S(2)}, u32[]{:S(2)}) %all-to-all-start.2) | async-done | bytes 524320 | tf_op jit(solution)/shard_map/all_to_all | solution.py:323
  122.2 0.0 collective-permute-done.1.other_ref
  122.2 1.2 scores.1
Async XLA Ops:
  0.0 16.9 %collective-permute-start = (bf16[32,512]{1,0:T(8,128)(2,1)}, bf16[32,512]{1,0:T(8,128)(2,1)S(1)}, u32[]{:S(2)}, u32[]{:S(2)}) collective-permute-start(bf16[32,512]{1,0:T(8,128)(2,1)} %param.31), channel_id=1, source_target_pairs={{0,0},{1,32},{2,64},{3,96},{4,128},{5,160},{6,192},{7,224},{8,256}... | collective-permute-start | bytes 98312 | tf_op jit(solution)/shard_map/ppermute | solution.py:216
  53.0 34.1 %all-to-all-start.3 = ((bf16[16,32,512]{2,1,0:T(8,128)(2,1)}), bf16[16,32,512]{2,1,0:T(8,128)(2,1)S(1)}, u32[]{:S(2)}, u32[]{:S(2)}) async-start(bf16[16,32,512]{2,1,0:T(8,128)(2,1)} %broadcast_in_dim.2), calls=%async_computation.3 | async-start | bytes 1048576 | tf_op jit(solution)/shard_map/all_to_all | solution.py:284
  60.3 43.6 %copy-start = (bf16[2,512,512]{2,1,0:T(8,128)(2,1)S(1)}, bf16[2,512,512]{2,1,0:T(8,128)(2,1)}, u32[]{:S(2)}) copy-start(bf16[2,512,512]{2,1,0:T(8,128)(2,1)} %hidden_ref.3) | copy-start | bytes 3145732
  60.3 43.6 %copy-start.2 = (bf16[8,128,128]{2,1,0:T(8,128)(2,1)S(1)}, bf16[8,128,128]{2,1,0:T(8,128)(2,1)}, u32[]{:S(2)}) copy-start(bf16[8,128,128]{2,1,0:T(8,128)(2,1)} %bank_ref.1) | copy-start | bytes 786436
  60.3 43.6 %copy-start.4 = (s32[3,512]{1,0:T(4,128)S(1)}, s32[3,512]{1,0:T(4,128)}, u32[]{:S(2)}) copy-start(s32[3,512]{1,0:T(4,128)} %block_ref.1) | copy-start | bytes 18436
  60.3 43.6 %copy-start.5 = (s32[3,512]{1,0:T(4,128)S(1)}, s32[3,512]{1,0:T(4,128)}, u32[]{:S(2)}) copy-start(s32[3,512]{1,0:T(4,128)} %tile_ref.1) | copy-start | bytes 18436
  60.3 43.6 %copy-start.6 = (s32[1024]{0:T(1024)S(1)}, s32[1024]{0:T(1024)}, u32[]{:S(2)}) copy-start(s32[1024]{0:T(1024)} %param.28) | copy-start | bytes 12292
  60.3 43.6 %copy-start.7 = (s32[1024]{0:T(1024)S(1)}, s32[1024]{0:T(1024)}, u32[]{:S(2)}) copy-start(s32[1024]{0:T(1024)} %param.29) | copy-start | bytes 12292
  87.0 16.9 %all-to-all-start.1 = ((bf16[16,2,32,512]{3,2,1,0:T(8,128)(2,1)}), bf16[16,2,32,512]{3,2,1,0:T(8,128)(2,1)S(1)}, u32[]{:S(2)}, u32[]{:S(2)}) async-start(bf16[16,2,32,512]{3,2,1,0:T(8,128)(2,1)} %lowrank_sum.1), calls=%async_computation.1 | async-start | bytes 2097152 | tf_op jit(solution)/shard_map/all_to_all | solution.py:302
  91.0 31.3 %collective-permute-start.1 = (bf16[16,32,512]{2,1,0:T(8,128)(2,1)S(1)}, bf16[16,32,512]{2,1,0:T(8,128)(2,1)S(1)}, u32[]{:S(2)}, u32[]{:S(2)}) collective-permute-start(bf16[16,32,512]{2,1,0:T(8,128)(2,1)S(1)} %all-to-all-done.3.mine_ref), channel_id=1, source_target_pairs={{0,16},{16,0},{32,48},{48,32},{64,80},{80,64},{96,112},{112,96},{1... | collective-permute-start | bytes 1572872 | tf_op jit(solution)/shard_map/ppermute | solution.py:292
  103.9 1.2 copy-start.1
  105.2 0.9 copy-start.3
  108.6 13.6 %all-to-all-start.2 = ((bf16[16,128,128]{2,1,0:T(8,128)(2,1)}), bf16[16,128,128]{2,1,0:T(8,128)(2,1)S(1)}, u32[]{:S(2)}, u32[]{:S(2)}) async-start(bf16[16,128,128]{2,1,0:T(8,128)(2,1)} %partial_features.1), calls=%async_computation.2 | async-start | bytes 1048576 | tf_op jit(solution)/shard_map/all_to_all | solution.py:323

commit v3 on v2

--- a/solution.py
+++ b/solution.py
@@ -155,22 +155,27 @@
     out_ref[...] = jnp.broadcast_to(feats.astype(BF16)[None], out_ref.shape)
 
 
-def score_kernel(core_index, parts_ref, mine_ref, other_ref, out_ref):
+def score_kernel(place, parts_ref, *refs):
+    mine_refs, other_refs, (out_ref, feats_ref) = refs[:4], refs[4:8], refs[8:]
     cands = out_ref.shape[0]
-    seeds = mine_ref.shape[1]
-    feats = jnp.sum(parts_ref[...].astype(F32), axis=0)
-    per_part = mine_ref.shape[2] // PB
+    fours, seeds, depth = mine_refs[0].shape
+    levels = 4 * fours
+    per_part = depth // PB
+    feats_ref[...] = jnp.sum(parts_ref[...].astype(F32), axis=0)
     totals = [[jnp.zeros((seeds, PB), F32) for _ in range(2)] for _ in range(cands)]
-    for block in range(KB):
-        at = block % per_part * PB
-        for half, seeds_ref in enumerate((mine_ref, other_ref)):
-            seed = seeds_ref[block // per_part, :, at : at + PB].astype(F32)
-            for c in range(cands):
-                row = c * KB + block
-                totals[c][half] = totals[c][half] + feats[row : row + 1] * seed
-    first_core = core_index[0] == 0
+    for at in range(levels):
+        source = (place[1] + (2 * levels - NEAR[at // 4] - 4 * (at % 4))) % levels
+        for part in range(per_part):
+            feat = [
+                feats_ref[pl.ds(c * KB + source * per_part + part, 1), :] for c in range(cands)
+            ]
+            for half, seeds_ref in enumerate((mine_refs[at // 4], other_refs[at // 4])):
+                seed = seeds_ref[at % 4, :, part * PB : (part + 1) * PB].astype(F32)
+                for c in range(cands):
+                    totals[c][half] = totals[c][half] + feat[c] * seed
+    first_core = place[0] == 0
     for c in range(cands):
-        mine = feats[c * KB : (c + 1) * KB]
+        mine = feats_ref[c * KB : (c + 1) * KB]
         square = jnp.sum(jnp.sum(mine * mine, axis=0, keepdims=True), axis=1, keepdims=True)
         here, there = totals[c]
         ordered = jnp.concatenate(
@@ -280,17 +285,8 @@
 
     send, seed_moved = lax.optimization_barrier((send, seed_moved))
     received = lax.all_to_all(send, "mp", 0, 0, tiled=True)
-    levels = data_size // 2
-    seeds_core = lax.all_to_all(
-        jnp.broadcast_to(seed_moved[None], (levels, *seed_moved.shape)),
-        "dp",
-        0,
-        0,
-        tiled=True,
-        axis_index_groups=[[2 * z + core for z in range(levels)] for core in range(2)],
-    )
-    seeds_other = lax.ppermute(seeds_core, "dp", [(d, d ^ 1) for d in range(data_size)])
-    core_index = (lax.axis_index("dp") % 2).astype(jnp.int32).reshape(1)
+    far = [seed_moved] + [move_z(seed_moved, 4 * j, data_size) for j in range(1, 4)]
+    received, *far = lax.optimization_barrier((received, *far))
     summed = pl.pallas_call(
         sum_kernel,
         name="lowrank_sum",
@@ -300,6 +296,9 @@
         compiler_params=PARAMS,
     )(received)
     lowrank = lax.all_to_all(summed, "mp", 0, 0, tiled=True)
+    four = jnp.stack(far)
+    near = [four] + [move_z(four, e, data_size) for e in NEAR[1:]]
+    lowrank, *near = lax.optimization_barrier((lowrank, *near))
 
     feat_parts = pl.pallas_call(
         feature_kernel,
@@ -320,16 +319,30 @@
         tile_value.reshape(KVH, DH),
         tile_bank,
     )
+    feat_parts, *near = lax.optimization_barrier((feat_parts, *near))
     feat_all = lax.all_to_all(feat_parts, "mp", 0, 0, tiled=True)
+    swap = [(d, d ^ 1) for d in range(data_size)]
+    other = [lax.ppermute(four, "dp", swap) for four in near]
+    place = jnp.stack([lax.axis_index("dp") % 2, lax.axis_index("dp") // 2]).astype(jnp.int32)
 
     return pl.pallas_call(
         score_kernel,
         name="scores",
         out_shape=jax.ShapeDtypeStruct((cands, out_seeds), F32),
-        in_specs=[SMEM, VMEM, VMEM, VMEM],
+        in_specs=[SMEM] + [VMEM] * 9,
         out_specs=VMEM,
+        scratch_shapes=[pltpu.VMEM((cands * KB, PB), F32)],
         compiler_params=PARAMS,
-    )(core_index, feat_all, seeds_core, seeds_other)
+    )(place, feat_all, *near, *other)
+
+
+NEAR = (0, 1, 2, -1)
+
+
+def move_z(block, steps, data_size):
+    return lax.ppermute(
+        block, "dp", [(d, (d + 2 * steps) % data_size) for d in range(data_size)]
+    )
 
 
 def solution(mesh):

time: 124 us -> 112 us (0.903)
  the two profiles are of different devices: /device:TPU:32 before, /device:TPU:1 now
where the time goes in v3:
time: 112 us; the launch traced here: 111 us
  starting transfers between devices  71 us (63%)
  Pallas kernels  19.5 us (17%)
  waiting for transfers between devices  14.6 us (13%)
  local copies, waits for them, and re-layouts  4.82 us (4%)
    ppermute x6, starting transfers between devices, move_z(): lax.ppermute(block, 'dp', [(d, (d + 2 * steps) % data_size) for d in rang...  25 us
    all_to_all x1, starting transfers between devices, local(): received = lax.all_to_all(send, 'mp', 0, 0, tiled=True)  20.5 us
    pallas_call x1, Pallas kernels, local(): pl.pallas_call(attention_kernel, name='attention_backward', out_shape=(ja...  13.8 us
    ppermute x6, waiting for transfers between devices, move_z(): lax.ppermute(block, 'dp', [(d, (d + 2 * steps) % data_size) for d in rang...  13.1 us
    ppermute x4, starting transfers between devices, local(): other = [lax.ppermute(four, 'dp', swap) for four in near]  11 us
    all_to_all x1, starting transfers between devices, local(): lowrank = lax.all_to_all(summed, 'mp', 0, 0, tiled=True)  6.67 us
    all_to_all x1, starting transfers between devices, local(): feat_all = lax.all_to_all(feat_parts, 'mp', 0, 0, tiled=True)  6.49 us
    unnamed x32, local copies, waits for them, and re-layouts  4.82 us
  transfers between devices with their start and end apart: 14, of which 5 were waited for; matrix products, arithmetic and copies ran while one was open for 1% of the time, Pallas kernels for 12%

profile of v3, /device:TPU:1, one launch (start us, length us, event | category | flops | bytes accessed | tf_op | source)
XLA Modules:
  0.0 111.1 jit_solution(5284139153714235282)
XLA Ops:
  0.0 1.4 %collective-permute-start = (bf16[32,512]{1,0:T(8,128)(2,1)}, bf16[32,512]{1,0:T(8,128)(2,1)S(1)}, u32[]{:S(2)}, u32[]{:S(2)}) collective-permute-start(bf16[32,512]{1,0:T(8,128)(2,1)} %param.31), channel_id=1, source_target_pairs={{0,0},{1,32},{2,64},{3,96},{4,128},{5,160},{6,192},{7,224},{8,256}... | collective-permute-start | bytes 98312 | tf_op jit(solution)/shard_map/ppermute | solution.py:221
  1.4 13.8 %attention_backward.1 = (bf16[16,2,32,512]{3,2,1,0:T(8,128)(2,1)}, bf16[2,512,512]{2,1,0:T(8,128)(2,1)}, bf16[2,512,128]{2,1,0:T(8,128)(2,1)}) custom-call(s32[1]{0:T(128)} %bitcast.2.kv_index, bf16[2,512,512]{2,1,0:T(8,128)(2,1)} %hidden_ref.3, bf16[2,512,512]{2,1,0:T(8,128)(2,1)} %query_ref.1, bf16[2,512,512]{2,1,0:T(8,128)(2,1)} %grad_ref.1, ...), custom_call_target="tpu_custom_call" | custom-call | flops 5000000000 | bytes 8000000 | tf_op jit(solution)/shard_map/attention_backward/pallas_call | solution.py:238
  15.2 20.5 %all-to-all-start = ((bf16[16,2,32,512]{3,2,1,0:T(8,128)(2,1)}), bf16[16,2,32,512]{3,2,1,0:T(8,128)(2,1)S(1)}, u32[]{:S(2)}, u32[]{:S(2)}) async-start(bf16[16,2,32,512]{3,2,1,0:T(8,128)(2,1)} %get-tuple-element.26), calls=%async_computation | async-start | bytes 2097152 | tf_op jit(solution)/shard_map/all_to_all | solution.py:287
  35.8 0.0 copy-start.8
  35.8 3.0 %collective-permute-start.3 = (bf16[32,512]{1,0:T(8,128)(2,1)S(1)}, bf16[32,512]{1,0:T(8,128)(2,1)S(1)}, u32[]{:S(2)}, u32[]{:S(2)}) collective-permute-start(bf16[32,512]{1,0:T(8,128)(2,1)S(1)} %collective-permute-done), channel_id=1, source_target_pairs={{0,384},{16,400},{32,416},{48,432},{64,448},{80,464},{96,480},{112... | collective-permute-start | bytes 98312 | tf_op jit(solution)/shard_map/ppermute | solution.py:343
  38.8 8.8 %collective-permute-start.2 = (bf16[32,512]{1,0:T(8,128)(2,1)S(1)}, bf16[32,512]{1,0:T(8,128)(2,1)S(1)}, u32[]{:S(2)}, u32[]{:S(2)}) collective-permute-start(bf16[32,512]{1,0:T(8,128)(2,1)S(1)} %collective-permute-done), channel_id=1, source_target_pairs={{0,256},{16,272},{32,288},{48,304},{64,320},{80,336},{96,352},{112... | collective-permute-start | bytes 98312 | tf_op jit(solution)/shard_map/ppermute | solution.py:343
  47.6 3.6 %collective-permute-start.1 = (bf16[32,512]{1,0:T(8,128)(2,1)S(1)}, bf16[32,512]{1,0:T(8,128)(2,1)S(1)}, u32[]{:S(2)}, u32[]{:S(2)}) collective-permute-start(bf16[32,512]{1,0:T(8,128)(2,1)S(1)} %collective-permute-done), channel_id=1, source_target_pairs={{0,128},{16,144},{32,160},{48,176},{64,192},{80,208},{96,224},{112... | collective-permute-start | bytes 98312 | tf_op jit(solution)/shard_map/ppermute | solution.py:343
  51.2 1.0 collective-permute-done.2
  52.2 4.4 %collective-permute-done.1 = bf16[32,512]{1,0:T(8,128)(2,1)S(1)} collective-permute-done((bf16[32,512]{1,0:T(8,128)(2,1)S(1)}, bf16[32,512]{1,0:T(8,128)(2,1)S(1)}, u32[]{:S(2)}, u32[]{:S(2)}) %collective-permute-start.1) | collective-permute-done | bytes 32800 | tf_op jit(solution)/shard_map/ppermute | solution.py:343
  56.6 1.2 %lowrank_sum.1 = bf16[16,2,32,512]{3,2,1,0:T(8,128)(2,1)} custom-call(bf16[16,2,32,512]{3,2,1,0:T(8,128)(2,1)S(1)} %all-to-all-done.parts_ref), custom_call_target="tpu_custom_call" | custom-call | tf_op jit(solution)/shard_map/lowrank_sum/pallas_call | solution.py:290
  57.8 6.7 %all-to-all-start.1 = ((bf16[16,2,32,512]{3,2,1,0:T(8,128)(2,1)}), bf16[16,2,32,512]{3,2,1,0:T(8,128)(2,1)S(1)}, u32[]{:S(2)}, u32[]{:S(2)}) async-start(bf16[16,2,32,512]{3,2,1,0:T(8,128)(2,1)} %lowrank_sum.1), calls=%async_computation.1 | async-start | bytes 2097152 | tf_op jit(solution)/shard_map/all_to_all | solution.py:298
  64.4 0.8 pad_maximum_fusion.refs_0_
  65.3 5.2 %collective-permute-start.6 = (bf16[4,32,512]{2,1,0:T(8,128)(2,1)S(1)}, bf16[4,32,512]{2,1,0:T(8,128)(2,1)S(1)}, u32[]{:S(2)}, u32[]{:S(2)}) collective-permute-start(bf16[4,32,512]{2,1,0:T(8,128)(2,1)S(1)} %pad_maximum_fusion.refs_0_), channel_id=1, source_target_pairs={{0,480},{16,496},{32,0},{48,16},{64,32},{80,48},{96,64},{112,80},{... | collective-permute-start | bytes 393224 | tf_op jit(solution)/shard_map/ppermute | solution.py:343
  70.5 1.9 %collective-permute-start.5 = (bf16[4,32,512]{2,1,0:T(8,128)(2,1)S(1)}, bf16[4,32,512]{2,1,0:T(8,128)(2,1)S(1)}, u32[]{:S(2)}, u32[]{:S(2)}) collective-permute-start(bf16[4,32,512]{2,1,0:T(8,128)(2,1)S(1)} %pad_maximum_fusion.refs_0_), channel_id=1, source_target_pairs={{0,64},{16,80},{32,96},{48,112},{64,128},{80,144},{96,160},{112,17... | collective-permute-start | bytes 393224 | tf_op jit(solution)/shard_map/ppermute | solution.py:343
  72.4 2.5 %collective-permute-start.4 = (bf16[4,32,512]{2,1,0:T(8,128)(2,1)S(1)}, bf16[4,32,512]{2,1,0:T(8,128)(2,1)}, u32[]{:S(2)}, u32[]{:S(2)}) collective-permute-start(bf16[4,32,512]{2,1,0:T(8,128)(2,1)S(1)} %pad_maximum_fusion.refs_0_), channel_id=1, source_target_pairs={{0,32},{16,48},{32,64},{48,80},{64,96},{80,112},{96,128},{112,144}... | collective-permute-start | bytes 393224 | tf_op jit(solution)/shard_map/ppermute | solution.py:343
  74.9 4.7 %collective-permute-done.5.refs_2_ = bf16[4,32,512]{2,1,0:T(8,128)(2,1)S(1)} collective-permute-done((bf16[4,32,512]{2,1,0:T(8,128)(2,1)S(1)}, bf16[4,32,512]{2,1,0:T(8,128)(2,1)S(1)}, u32[]{:S(2)}, u32[]{:S(2)}) %collective-permute-start.5) | collective-permute-done | bytes 131104 | tf_op jit(solution)/shard_map/ppermute | solution.py:343
  79.6 0.6 copy-done.6
  80.3 3.0 %collective-permute-done.4.refs_1_ = bf16[4,32,512]{2,1,0:T(8,128)(2,1)} collective-permute-done((bf16[4,32,512]{2,1,0:T(8,128)(2,1)S(1)}, bf16[4,32,512]{2,1,0:T(8,128)(2,1)}, u32[]{:S(2)}, u32[]{:S(2)}) %collective-permute-start.4) | collective-permute-done | bytes 131104 | tf_op jit(solution)/shard_map/ppermute | solution.py:343
  83.4 0.9 copy-done.3
  84.3 0.7 copy-done.10
  85.0 0.7 copy-done.11
  85.7 2.5 %partial_features.1 = bf16[16,128,128]{2,1,0:T(8,128)(2,1)} custom-call(s32[1]{0:T(128)} %bitcast.2.kv_index, bf16[16,2,32,512]{3,2,1,0:T(8,128)(2,1)S(1)} %all-to-all-done.1.lowrank_ref, bf16[2,512,512]{2,1,0:T(8,128)(2,1)S(1)} %copy-done, bf16[2,512,512]{2,1,0:T(8,128)(2,1)S(1)} %copy-done.1, bf16[2,512,128]{2,1,0:T(8,128)(2,1)S(1)} %copy-done.3, ...), custom_call_target="tpu_custom_call" | custom-call | tf_op jit(solution)/shard_map/partial_features/pallas_call | solution.py:303
  88.1 6.5 %all-to-all-start.2 = ((bf16[16,128,128]{2,1,0:T(8,128)(2,1)}), bf16[16,128,128]{2,1,0:T(8,128)(2,1)S(1)}, u32[]{:S(2)}, u32[]{:S(2)}) async-start(bf16[16,128,128]{2,1,0:T(8,128)(2,1)} %partial_features.1), calls=%async_computation.2 | async-start | bytes 1048576 | tf_op jit(solution)/shard_map/all_to_all | solution.py:323
  94.6 4.7 %collective-permute-start.7 = (bf16[4,32,512]{2,1,0:T(8,128)(2,1)S(1)}, bf16[4,32,512]{2,1,0:T(8,128)(2,1)S(1)}, u32[]{:S(2)}, u32[]{:S(2)}) collective-permute-start(bf16[4,32,512]{2,1,0:T(8,128)(2,1)S(1)} %pad_maximum_fusion.refs_0_), channel_id=1, source_target_pairs={{0,16},{16,0},{32,48},{48,32},{64,80},{80,64},{96,112},{112,96},{1... | collective-permute-start | bytes 393224 | tf_op jit(solution)/shard_map/ppermute | solution.py:325
  99.4 1.9 %collective-permute-start.8 = (bf16[4,32,512]{2,1,0:T(8,128)(2,1)}, bf16[4,32,512]{2,1,0:T(8,128)(2,1)S(1)}, u32[]{:S(2)}, u32[]{:S(2)}) collective-permute-start(bf16[4,32,512]{2,1,0:T(8,128)(2,1)} %collective-permute-done.4.refs_1_), channel_id=1, source_target_pairs={{0,16},{16,0},{32,48},{48,32},{64,80},{80,64},{96,112},{112,96},{1... | collective-permute-start | bytes 393224 | tf_op jit(solution)/shard_map/ppermute | solution.py:325
  101.3 2.4 %collective-permute-start.9 = (bf16[4,32,512]{2,1,0:T(8,128)(2,1)}, bf16[4,32,512]{2,1,0:T(8,128)(2,1)S(1)}, u32[]{:S(2)}, u32[]{:S(2)}) collective-permute-start(bf16[4,32,512]{2,1,0:T(8,128)(2,1)} %copy-done.6), channel_id=1, source_target_pairs={{0,16},{16,0},{32,48},{48,32},{64,80},{80,64},{96,112},{112,96},{1... | collective-permute-start | bytes 393224 | tf_op jit(solution)/shard_map/ppermute | solution.py:325
  103.7 1.9 %collective-permute-start.10 = (bf16[4,32,512]{2,1,0:T(8,128)(2,1)}, bf16[4,32,512]{2,1,0:T(8,128)(2,1)S(1)}, u32[]{:S(2)}, u32[]{:S(2)}) collective-permute-start(bf16[4,32,512]{2,1,0:T(8,128)(2,1)} %copy-done.4), channel_id=1, source_target_pairs={{0,16},{16,0},{32,48},{48,32},{64,80},{80,64},{96,112},{112,96},{1... | collective-permute-start | bytes 393224 | tf_op jit(solution)/shard_map/ppermute | solution.py:325
  105.7 0.1 pad_add_fusion.place
  105.7 1.4 %collective-permute-done.10.refs_7_ = bf16[4,32,512]{2,1,0:T(8,128)(2,1)S(1)} collective-permute-done((bf16[4,32,512]{2,1,0:T(8,128)(2,1)}, bf16[4,32,512]{2,1,0:T(8,128)(2,1)S(1)}, u32[]{:S(2)}, u32[]{:S(2)}) %collective-permute-start.10) | collective-permute-done | bytes 131104 | tf_op jit(solution)/shard_map/ppermute | solution.py:325
  107.2 0.9 copy-done.5
  108.1 0.9 copy-done.7
  109.0 2.1 %scores.1 = f32[2,64]{1,0:T(2,128)} custom-call(s32[2]{0:T(128)S(1)} %pad_add_fusion.place, bf16[16,128,128]{2,1,0:T(8,128)(2,1)S(1)} %all-to-all-done.2.parts_ref, bf16[4,32,512]{2,1,0:T(8,128)(2,1)S(1)} %pad_maximum_fusion.refs_0_, bf16[4,32,512]{2,1,0:T(8,128)(2,1)} %collective-permute-done.4.refs_1_, bf16[4,32,512]{2,1,0:T(8,128)(2,1)S(1)} %copy-done.7, ...), custom_call_target="tpu_custom_call" | custom-call | tf_op jit(solution)/shard_map/scores/pallas_call | solution.py:328
  (34 shorter events, 0.1 us)
Async XLA Ops:
  0.0 15.2 %collective-permute-start = (bf16[32,512]{1,0:T(8,128)(2,1)}, bf16[32,512]{1,0:T(8,128)(2,1)S(1)}, u32[]{:S(2)}, u32[]{:S(2)}) collective-permute-start(bf16[32,512]{1,0:T(8,128)(2,1)} %param.31), channel_id=1, source_target_pairs={{0,0},{1,32},{2,64},{3,96},{4,128},{5,160},{6,192},{7,224},{8,256}... | collective-permute-start | bytes 98312 | tf_op jit(solution)/shard_map/ppermute | solution.py:221
  15.2 42.6 %copy-start.12 = (bf16[32,512]{1,0:T(8,128)(2,1)}, bf16[32,512]{1,0:T(8,128)(2,1)S(1)}, u32[]{:S(2)}) copy-start(bf16[32,512]{1,0:T(8,128)(2,1)S(1)} %collective-permute-done) | copy-start | bytes 98308
  15.2 41.4 %all-to-all-start = ((bf16[16,2,32,512]{3,2,1,0:T(8,128)(2,1)}), bf16[16,2,32,512]{3,2,1,0:T(8,128)(2,1)S(1)}, u32[]{:S(2)}, u32[]{:S(2)}) async-start(bf16[16,2,32,512]{3,2,1,0:T(8,128)(2,1)} %get-tuple-element.26), calls=%async_computation | async-start | bytes 2097152 | tf_op jit(solution)/shard_map/all_to_all | solution.py:287
  35.7 47.6 %copy-start = (bf16[2,512,512]{2,1,0:T(8,128)(2,1)S(1)}, bf16[2,512,512]{2,1,0:T(8,128)(2,1)}, u32[]{:S(2)}) copy-start(bf16[2,512,512]{2,1,0:T(8,128)(2,1)} %hidden_ref.3) | copy-start | bytes 3145732
  35.7 47.6 %copy-start.1 = (bf16[2,512,512]{2,1,0:T(8,128)(2,1)S(1)}, bf16[2,512,512]{2,1,0:T(8,128)(2,1)}, u32[]{:S(2)}) copy-start(bf16[2,512,512]{2,1,0:T(8,128)(2,1)} %get-tuple-element.34.query_grad_ref) | copy-start | bytes 3145732
  35.7 47.6 %copy-start.2 = (bf16[8,128,128]{2,1,0:T(8,128)(2,1)S(1)}, bf16[8,128,128]{2,1,0:T(8,128)(2,1)}, u32[]{:S(2)}) copy-start(bf16[8,128,128]{2,1,0:T(8,128)(2,1)} %bank_ref.1) | copy-start | bytes 786436
  35.8 47.6 %copy-start.8 = (s32[3,512]{1,0:T(4,128)S(1)}, s32[3,512]{1,0:T(4,128)}, u32[]{:S(2)}) copy-start(s32[3,512]{1,0:T(4,128)} %block_ref.1) | copy-start | bytes 18436
  35.8 47.6 %copy-start.9 = (s32[3,512]{1,0:T(4,128)S(1)}, s32[3,512]{1,0:T(4,128)}, u32[]{:S(2)}) copy-start(s32[3,512]{1,0:T(4,128)} %tile_ref.1) | copy-start | bytes 18436
  35.8 15.4 %collective-permute-start.3 = (bf16[32,512]{1,0:T(8,128)(2,1)S(1)}, bf16[32,512]{1,0:T(8,128)(2,1)S(1)}, u32[]{:S(2)}, u32[]{:S(2)}) collective-permute-start(bf16[32,512]{1,0:T(8,128)(2,1)S(1)} %collective-permute-done), channel_id=1, source_target_pairs={{0,384},{16,400},{32,416},{48,432},{64,448},{80,464},{96,480},{112... | collective-permute-start | bytes 98312 | tf_op jit(solution)/shard_map/ppermute | solution.py:343
  38.8 13.4 %collective-permute-start.2 = (bf16[32,512]{1,0:T(8,128)(2,1)S(1)}, bf16[32,512]{1,0:T(8,128)(2,1)S(1)}, u32[]{:S(2)}, u32[]{:S(2)}) collective-permute-start(bf16[32,512]{1,0:T(8,128)(2,1)S(1)} %collective-permute-done), channel_id=1, source_target_pairs={{0,256},{16,272},{32,288},{48,304},{64,320},{80,336},{96,352},{112... | collective-permute-start | bytes 98312 | tf_op jit(solution)/shard_map/ppermute | solution.py:343
  47.6 9.0 %collective-permute-start.1 = (bf16[32,512]{1,0:T(8,128)(2,1)S(1)}, bf16[32,512]{1,0:T(8,128)(2,1)S(1)}, u32[]{:S(2)}, u32[]{:S(2)}) collective-permute-start(bf16[32,512]{1,0:T(8,128)(2,1)S(1)} %collective-permute-done), channel_id=1, source_target_pairs={{0,128},{16,144},{32,160},{48,176},{64,192},{80,208},{96,224},{112... | collective-permute-start | bytes 98312 | tf_op jit(solution)/shard_map/ppermute | solution.py:343
  51.2 6.6 %copy-start.13 = (bf16[32,512]{1,0:T(8,128)(2,1)}, bf16[32,512]{1,0:T(8,128)(2,1)S(1)}, u32[]{:S(2)}) copy-start(bf16[32,512]{1,0:T(8,128)(2,1)S(1)} %collective-permute-done.3) | copy-start | bytes 98308
  52.2 5.6 %copy-start.14 = (bf16[32,512]{1,0:T(8,128)(2,1)}, bf16[32,512]{1,0:T(8,128)(2,1)S(1)}, u32[]{:S(2)}) copy-start(bf16[32,512]{1,0:T(8,128)(2,1)S(1)} %collective-permute-done.2) | copy-start | bytes 98308
  56.6 1.2 %copy-start.15 = (bf16[32,512]{1,0:T(8,128)(2,1)}, bf16[32,512]{1,0:T(8,128)(2,1)S(1)}, u32[]{:S(2)}) copy-start(bf16[32,512]{1,0:T(8,128)(2,1)S(1)} %collective-permute-done.1) | copy-start | bytes 98308
  57.8 25.5 %all-to-all-start.1 = ((bf16[16,2,32,512]{3,2,1,0:T(8,128)(2,1)}), bf16[16,2,32,512]{3,2,1,0:T(8,128)(2,1)S(1)}, u32[]{:S(2)}, u32[]{:S(2)}) async-start(bf16[16,2,32,512]{3,2,1,0:T(8,128)(2,1)} %lowrank_sum.1), calls=%async_computation.1 | async-start | bytes 2097152 | tf_op jit(solution)/shard_map/all_to_all | solution.py:298
  65.3 9.6 %collective-permute-start.6 = (bf16[4,32,512]{2,1,0:T(8,128)(2,1)S(1)}, bf16[4,32,512]{2,1,0:T(8,128)(2,1)S(1)}, u32[]{:S(2)}, u32[]{:S(2)}) collective-permute-start(bf16[4,32,512]{2,1,0:T(8,128)(2,1)S(1)} %pad_maximum_fusion.refs_0_), channel_id=1, source_target_pairs={{0,480},{16,496},{32,0},{48,16},{64,32},{80,48},{96,64},{112,80},{... | collective-permute-start | bytes 393224 | tf_op jit(solution)/shard_map/ppermute | solution.py:343
  70.5 9.1 %collective-permute-start.5 = (bf16[4,32,512]{2,1,0:T(8,128)(2,1)S(1)}, bf16[4,32,512]{2,1,0:T(8,128)(2,1)S(1)}, u32[]{:S(2)}, u32[]{:S(2)}) collective-permute-start(bf16[4,32,512]{2,1,0:T(8,128)(2,1)S(1)} %pad_maximum_fusion.refs_0_), channel_id=1, source_target_pairs={{0,64},{16,80},{32,96},{48,112},{64,128},{80,144},{96,160},{112,17... | collective-permute-start | bytes 393224 | tf_op jit(solution)/shard_map/ppermute | solution.py:343
  72.4 10.9 %collective-permute-start.4 = (bf16[4,32,512]{2,1,0:T(8,128)(2,1)S(1)}, bf16[4,32,512]{2,1,0:T(8,128)(2,1)}, u32[]{:S(2)}, u32[]{:S(2)}) collective-permute-start(bf16[4,32,512]{2,1,0:T(8,128)(2,1)S(1)} %pad_maximum_fusion.refs_0_), channel_id=1, source_target_pairs={{0,32},{16,48},{32,64},{48,80},{64,96},{80,112},{96,128},{112,144}... | collective-permute-start | bytes 393224 | tf_op jit(solution)/shard_map/ppermute | solution.py:343
  74.9 4.7 %copy-start.4 = (bf16[4,32,512]{2,1,0:T(8,128)(2,1)}, bf16[4,32,512]{2,1,0:T(8,128)(2,1)S(1)}, u32[]{:S(2)}) copy-start(bf16[4,32,512]{2,1,0:T(8,128)(2,1)S(1)} %collective-permute-done.6.refs_3_) | copy-start | bytes 393220
  79.6 0.7 copy-start.6
  83.3 1.0 copy-start.3
  84.3 0.7 copy-start.10
  85.0 0.7 copy-start.11
  88.1 19.0 %all-to-all-start.2 = ((bf16[16,128,128]{2,1,0:T(8,128)(2,1)}), bf16[16,128,128]{2,1,0:T(8,128)(2,1)S(1)}, u32[]{:S(2)}, u32[]{:S(2)}) async-start(bf16[16,128,128]{2,1,0:T(8,128)(2,1)} %partial_features.1), calls=%async_computation.2 | async-start | bytes 1048576 | tf_op jit(solution)/shard_map/all_to_all | solution.py:323
  94.6 11.1 %collective-permute-start.7 = (bf16[4,32,512]{2,1,0:T(8,128)(2,1)S(1)}, bf16[4,32,512]{2,1,0:T(8,128)(2,1)S(1)}, u32[]{:S(2)}, u32[]{:S(2)}) collective-permute-start(bf16[4,32,512]{2,1,0:T(8,128)(2,1)S(1)} %pad_maximum_fusion.refs_0_), channel_id=1, source_target_pairs={{0,16},{16,0},{32,48},{48,32},{64,80},{80,64},{96,112},{112,96},{1... | collective-permute-start | bytes 393224 | tf_op jit(solution)/shard_map/ppermute | solution.py:325
  99.4 6.4 %collective-permute-start.8 = (bf16[4,32,512]{2,1,0:T(8,128)(2,1)}, bf16[4,32,512]{2,1,0:T(8,128)(2,1)S(1)}, u32[]{:S(2)}, u32[]{:S(2)}) collective-permute-start(bf16[4,32,512]{2,1,0:T(8,128)(2,1)} %collective-permute-done.4.refs_1_), channel_id=1, source_target_pairs={{0,16},{16,0},{32,48},{48,32},{64,80},{80,64},{96,112},{112,96},{1... | collective-permute-start | bytes 393224 | tf_op jit(solution)/shard_map/ppermute | solution.py:325
  101.3 4.4 %collective-permute-start.9 = (bf16[4,32,512]{2,1,0:T(8,128)(2,1)}, bf16[4,32,512]{2,1,0:T(8,128)(2,1)S(1)}, u32[]{:S(2)}, u32[]{:S(2)}) collective-permute-start(bf16[4,32,512]{2,1,0:T(8,128)(2,1)} %copy-done.6), channel_id=1, source_target_pairs={{0,16},{16,0},{32,48},{48,32},{64,80},{80,64},{96,112},{112,96},{1... | collective-permute-start | bytes 393224 | tf_op jit(solution)/shard_map/ppermute | solution.py:325
  103.7 3.5 %collective-permute-start.10 = (bf16[4,32,512]{2,1,0:T(8,128)(2,1)}, bf16[4,32,512]{2,1,0:T(8,128)(2,1)S(1)}, u32[]{:S(2)}, u32[]{:S(2)}) collective-permute-start(bf16[4,32,512]{2,1,0:T(8,128)(2,1)} %copy-done.4), channel_id=1, source_target_pairs={{0,16},{16,0},{32,48},{48,32},{64,80},{80,64},{96,112},{112,96},{1... | collective-permute-start | bytes 393224 | tf_op jit(solution)/shard_map/ppermute | solution.py:325
  107.2 0.9 copy-start.5
  108.1 0.9 copy-start.7

commit v4 on v1

--- a/solution.py
+++ b/solution.py
@@ -216,21 +216,6 @@
             for m in range(model_size)
         ],
     )
-    seed_pair = lax.all_gather(
-        seed_moved,
-        "dp",
-        axis=0,
-        tiled=True,
-        axis_index_groups=[[2 * z, 2 * z + 1] for z in range(data_size // 2)],
-    )
-    seeds_all = lax.all_gather(
-        seed_pair,
-        "dp",
-        axis=0,
-        tiled=False,
-        axis_index_groups=[[2 * z + core for z in range(data_size // 2)] for core in range(2)],
-    )
-
     chunk = 4 * R // model_size
 
     def per_cand(*shape):
@@ -269,7 +254,7 @@
             ],
             scratch_shapes=[pltpu.VMEM((seq_len, DH), F32)],
         ),
-        compiler_params=PARAMS,
+        compiler_params=pltpu.CompilerParams(vmem_limit_bytes=60 << 20),
         cost_estimate=pl.CostEstimate(
             flops=5_000_000_000, bytes_accessed=8_000_000, transcendentals=2_000_000
         ),
@@ -287,6 +272,23 @@
         up_value,
     )
 
+    send, seed_moved = lax.optimization_barrier((send, seed_moved))
+    pairs = data_size // 4
+    seed_pair = lax.all_gather(
+        seed_moved,
+        "dp",
+        axis=0,
+        tiled=True,
+        axis_index_groups=[[4 * i + j for j in range(4)] for i in range(pairs)],
+    )
+    send, seed_pair = lax.optimization_barrier((send, seed_pair))
+    seeds_all = lax.all_gather(
+        seed_pair,
+        "dp",
+        axis=0,
+        tiled=True,
+        axis_index_groups=[[4 * i + j for i in range(pairs)] for j in range(4)],
+    ).reshape(model_size, out_seeds, seed_feats.shape[1])
     received = lax.all_to_all(send, "mp", 0, 0, tiled=True)
     summed = pl.pallas_call(
         sum_kernel,

time: 142 us -> 112 us (0.79)
  the two profiles are of different devices: /device:TPU:2 before, /device:TPU:32 now
where the time goes in v4:
time: 112 us; the launch traced here: 111 us
  waiting for transfers between devices  28.2 us (25%)
  blocking collectives  27.4 us (24%)
  starting transfers between devices  23.1 us (21%)
  Pallas kernels  17.7 us (16%)
  between operations  13.5 us (12%)
  local copies, waits for them, and re-layouts  1.27 us (1%)
    all_to_all x1, blocking collectives, local(): lowrank = lax.all_to_all(summed, 'mp', 0, 0, tiled=True)  19.6 us
    all_to_all x1, waiting for transfers between devices, local(): received = lax.all_to_all(send, 'mp', 0, 0, tiled=True)  17.5 us
    all_to_all x1, starting transfers between devices, local(): received = lax.all_to_all(send, 'mp', 0, 0, tiled=True)  16.5 us
    pallas_call x1, Pallas kernels, local(): pl.pallas_call(attention_kernel, name='attention_backward', out_shape=(ja...  13.8 us
    all_gather x1, blocking collectives, local(): lax.all_gather(seed_moved, 'dp', axis=0, tiled=True, axis_index_groups=[[...  7.8 us
    all_gather x1, waiting for transfers between devices, local(): lax.all_gather(seed_pair, 'dp', axis=0, tiled=True, axis_index_groups=[[4...  6.67 us
    all_to_all x1, starting transfers between devices, local(): feat_all = lax.all_to_all(feat_parts, 'mp', 0, 0, tiled=True)  3.57 us
    all_to_all x1, waiting for transfers between devices, local(): feat_all = lax.all_to_all(feat_parts, 'mp', 0, 0, tiled=True)  3.39 us
  transfers between devices with their start and end apart: 4, of which 3 were waited for; matrix products, arithmetic and copies ran while one was open for 0% of the time, Pallas kernels for 15%

profile of v4, /device:TPU:32, one launch (start us, length us, event | category | flops | bytes accessed | tf_op | source)
XLA Modules:
  0.0 111.2 jit_solution(2101120485331391236)
XLA Ops:
  6.5 3.0 %collective-permute-start = (bf16[32,512]{1,0:T(8,128)(2,1)}, bf16[32,512]{1,0:T(8,128)(2,1)S(1)}, u32[]{:S(2)}, u32[]{:S(2)}) collective-permute-start(bf16[32,512]{1,0:T(8,128)(2,1)} %param.31), channel_id=1, source_target_pairs={{0,0},{1,32},{2,64},{3,96},{4,128},{5,160},{6,192},{7,224},{8,256}... | collective-permute-start | bytes 98312 | tf_op jit(solution)/shard_map/ppermute | solution.py:210
  9.6 13.8 %attention_backward.1 = (bf16[16,2,32,512]{3,2,1,0:T(8,128)(2,1)}, bf16[2,512,512]{2,1,0:T(8,128)(2,1)}, bf16[2,512,128]{2,1,0:T(8,128)(2,1)}) custom-call(s32[1]{0:T(128)} %bitcast.kv_index, bf16[2,512,512]{2,1,0:T(8,128)(2,1)} %hidden_ref.3, bf16[2,512,512]{2,1,0:T(8,128)(2,1)} %query_ref.1, bf16[2,512,512]{2,1,0:T(8,128)(2,1)} %grad_ref.1, ...), custom_call_target="tpu_custom_call" | custom-call | flops 5000000000 | bytes 8000000 | tf_op jit(solution)/shard_map/attention_backward/pallas_call | solution.py:227
  23.4 0.0 collective-permute-done
  23.4 7.8 %all_gather.6 = bf16[128,512]{1,0:T(8,128)(2,1)} all-gather(bf16[32,512]{1,0:T(8,128)(2,1)S(1)} %collective-permute-done), channel_id=1, replica_groups={{0,16,32,48},{64,80,96,112},{128,144,160,176},{192,208,224,240},{256,27..., dimensions={0}, use_global_device_ids=true | all-gather | bytes 163840 | tf_op jit(solution)/shard_map/all_gather | solution.py:277
  31.2 16.5 %all-to-all-start = ((bf16[16,2,32,512]{3,2,1,0:T(8,128)(2,1)}), bf16[16,2,32,512]{3,2,1,0:T(8,128)(2,1)S(1)}, u32[]{:S(2)}, u32[]{:S(2)}) async-start(bf16[16,2,32,512]{3,2,1,0:T(8,128)(2,1)} %get-tuple-element.15), calls=%async_computation | async-start | bytes 2097152 | tf_op jit(solution)/shard_map/all_to_all | solution.py:292
  47.6 0.0 all-gather.2.cloned.1.call-start
  47.7 0.7 all-gather.2.cloned.1.call-update
  48.4 0.0 copy-start
  48.4 0.0 copy-start.1
  48.4 0.0 copy-start.3
  48.4 0.0 copy-start.5
  48.4 0.0 copy-start.6
  48.4 0.0 copy-start.7
  48.5 0.0 copy-start.8
  48.5 17.5 %all-to-all-done.parts_ref = bf16[16,2,32,512]{3,2,1,0:T(8,128)(2,1)S(1)} async-done(((bf16[16,2,32,512]{3,2,1,0:T(8,128)(2,1)}), bf16[16,2,32,512]{3,2,1,0:T(8,128)(2,1)S(1)}, u32[]{:S(2)}, u32[]{:S(2)}) %all-to-all-start) | async-done | bytes 1048608 | tf_op jit(solution)/shard_map/all_to_all | solution.py:292
  65.9 0.0 copy-start.4
  65.9 0.2 lowrank_sum.1
  66.1 19.6 %all_to_all.15.lowrank_ref = bf16[16,2,32,512]{3,2,1,0:T(8,128)(2,1)S(1)} all-to-all(bf16[16,2,32,512]{3,2,1,0:T(8,128)(2,1)S(1)} %lowrank_sum.1), channel_id=1, replica_groups=mesh['dp'=32,'mp'=16] {'mp'}, dimensions={0} | all-to-all | bytes 2097152 | tf_op jit(solution)/shard_map/all_to_all | solution.py:301
  85.7 0.0 copy-done
  85.7 0.0 copy-done.1
  85.7 0.0 copy-done.3
  85.7 0.0 copy-done.5
  85.7 0.0 copy-done.6
  85.7 0.0 copy-done.7
  85.7 0.0 copy-done.8
  85.7 0.0 copy-done.4
  85.7 2.5 %partial_features.1 = bf16[16,128,128]{2,1,0:T(8,128)(2,1)} custom-call(s32[1]{0:T(128)} %bitcast.kv_index, bf16[16,2,32,512]{3,2,1,0:T(8,128)(2,1)S(1)} %all_to_all.15.lowrank_ref, bf16[2,512,512]{2,1,0:T(8,128)(2,1)S(1)} %copy-done, bf16[2,512,512]{2,1,0:T(8,128)(2,1)S(1)} %copy-done.1, bf16[2,512,128]{2,1,0:T(8,128)(2,1)S(1)} %copy-done.4, ...), custom_call_target="tpu_custom_call" | custom-call | tf_op jit(solution)/shard_map/partial_features/pallas_call | solution.py:303
  88.2 3.6 %all-to-all-start.2 = ((bf16[16,128,128]{2,1,0:T(8,128)(2,1)}), bf16[16,128,128]{2,1,0:T(8,128)(2,1)S(1)}, u32[]{:S(2)}, u32[]{:S(2)}) async-start(bf16[16,128,128]{2,1,0:T(8,128)(2,1)} %partial_features.1), calls=%async_computation.2 | async-start | bytes 1048576 | tf_op jit(solution)/shard_map/all_to_all | solution.py:322
  91.8 6.7 %all-gather.2.cloned.1.call-done = bf16[1024,512]{1,0:T(8,128)(2,1)} async-done(((bf16[128,512]{1,0:T(8,128)(2,1)}), bf16[1024,512]{1,0:T(8,128)(2,1)}) %all-gather.2.cloned.1.call-update) | async-done | bytes 1048592 | tf_op jit(solution)/shard_map/all_gather | solution.py:285
  98.5 3.4 %all-to-all-done.2.parts_ref = bf16[16,128,128]{2,1,0:T(8,128)(2,1)S(1)} async-done(((bf16[16,128,128]{2,1,0:T(8,128)(2,1)}), bf16[16,128,128]{2,1,0:T(8,128)(2,1)S(1)}, u32[]{:S(2)}, u32[]{:S(2)}) %all-to-all-start.2) | async-done | bytes 524320 | tf_op jit(solution)/shard_map/all_to_all | solution.py:322
  101.9 1.2 %copy-done.2 = bf16[1024,512]{1,0:T(8,128)(2,1)S(1)} copy-done((bf16[1024,512]{1,0:T(8,128)(2,1)S(1)}, bf16[1024,512]{1,0:T(8,128)(2,1)}, u32[]{:S(2)}) %copy-start.2) | copy-done | bytes 1048600
  103.1 1.2 %scores.1 = f32[2,64]{1,0:T(2,128)} custom-call(bf16[16,128,128]{2,1,0:T(8,128)(2,1)S(1)} %all-to-all-done.2.parts_ref, bf16[16,64,512]{2,1,0:T(8,128)(2,1)S(1)} %bitcast.4), custom_call_target="tpu_custom_call" | custom-call | tf_op jit(solution)/shard_map/scores/pallas_call | solution.py:324
  (1 shorter events, 0.0 us)
Async XLA Ops:
  6.5 16.8 %collective-permute-start = (bf16[32,512]{1,0:T(8,128)(2,1)}, bf16[32,512]{1,0:T(8,128)(2,1)S(1)}, u32[]{:S(2)}, u32[]{:S(2)}) collective-permute-start(bf16[32,512]{1,0:T(8,128)(2,1)} %param.31), channel_id=1, source_target_pairs={{0,0},{1,32},{2,64},{3,96},{4,128},{5,160},{6,192},{7,224},{8,256}... | collective-permute-start | bytes 98312 | tf_op jit(solution)/shard_map/ppermute | solution.py:210
  31.2 34.8 %all-to-all-start = ((bf16[16,2,32,512]{3,2,1,0:T(8,128)(2,1)}), bf16[16,2,32,512]{3,2,1,0:T(8,128)(2,1)S(1)}, u32[]{:S(2)}, u32[]{:S(2)}) async-start(bf16[16,2,32,512]{3,2,1,0:T(8,128)(2,1)} %get-tuple-element.15), calls=%async_computation | async-start | bytes 2097152 | tf_op jit(solution)/shard_map/all_to_all | solution.py:292
  47.6 50.8 %all-gather.2.cloned.1.call-start = ((), (), s32[]{:S(2)}) async-start(), calls=%async_computation.3 | async-start | bytes 1179648 | tf_op jit(solution)/shard_map/all_gather | solution.py:285
  48.4 37.3 %copy-start = (bf16[2,512,512]{2,1,0:T(8,128)(2,1)S(1)}, bf16[2,512,512]{2,1,0:T(8,128)(2,1)}, u32[]{:S(2)}) copy-start(bf16[2,512,512]{2,1,0:T(8,128)(2,1)} %hidden_ref.3) | copy-start | bytes 3145732
  48.4 37.3 %copy-start.1 = (bf16[2,512,512]{2,1,0:T(8,128)(2,1)S(1)}, bf16[2,512,512]{2,1,0:T(8,128)(2,1)}, u32[]{:S(2)}) copy-start(bf16[2,512,512]{2,1,0:T(8,128)(2,1)} %get-tuple-element.16.query_grad_ref) | copy-start | bytes 3145732
  48.4 37.3 %copy-start.3 = (bf16[8,128,128]{2,1,0:T(8,128)(2,1)S(1)}, bf16[8,128,128]{2,1,0:T(8,128)(2,1)}, u32[]{:S(2)}) copy-start(bf16[8,128,128]{2,1,0:T(8,128)(2,1)} %bank_ref.1) | copy-start | bytes 786436
  48.4 37.3 %copy-start.5 = (s32[3,512]{1,0:T(4,128)S(1)}, s32[3,512]{1,0:T(4,128)}, u32[]{:S(2)}) copy-start(s32[3,512]{1,0:T(4,128)} %block_ref.1) | copy-start | bytes 18436
  48.4 37.3 %copy-start.6 = (s32[3,512]{1,0:T(4,128)S(1)}, s32[3,512]{1,0:T(4,128)}, u32[]{:S(2)}) copy-start(s32[3,512]{1,0:T(4,128)} %tile_ref.1) | copy-start | bytes 18436
  48.4 37.3 %copy-start.7 = (s32[1024]{0:T(1024)S(1)}, s32[1024]{0:T(1024)}, u32[]{:S(2)}) copy-start(s32[1024]{0:T(1024)} %param.28) | copy-start | bytes 12292
  48.5 37.3 %copy-start.8 = (s32[1024]{0:T(1024)S(1)}, s32[1024]{0:T(1024)}, u32[]{:S(2)}) copy-start(s32[1024]{0:T(1024)} %param.29) | copy-start | bytes 12292
  65.9 19.8 %copy-start.4 = (bf16[2,512,128]{2,1,0:T(8,128)(2,1)S(1)}, bf16[2,512,128]{2,1,0:T(8,128)(2,1)}, u32[]{:S(2)}) copy-start(bf16[2,512,128]{2,1,0:T(8,128)(2,1)} %get-tuple-element.17.value_grad_ref) | copy-start | bytes 786436
  88.2 13.6 %all-to-all-start.2 = ((bf16[16,128,128]{2,1,0:T(8,128)(2,1)}), bf16[16,128,128]{2,1,0:T(8,128)(2,1)S(1)}, u32[]{:S(2)}, u32[]{:S(2)}) async-start(bf16[16,128,128]{2,1,0:T(8,128)(2,1)} %partial_features.1), calls=%async_computation.2 | async-start | bytes 1048576 | tf_op jit(solution)/shard_map/all_to_all | solution.py:322
  101.9 1.2 %copy-start.2 = (bf16[1024,512]{1,0:T(8,128)(2,1)S(1)}, bf16[1024,512]{1,0:T(8,128)(2,1)}, u32[]{:S(2)}) copy-start(bf16[1024,512]{1,0:T(8,128)(2,1)} %all-gather.2.cloned.1.call-done) | copy-start | bytes 3145732
Sparse Core Ops, SparseCore 0:
  50.6 47.8 all-gather.1

commit v5 on v3

--- a/solution.py
+++ b/solution.py
@@ -156,21 +156,20 @@
 
 
 def score_kernel(place, parts_ref, *refs):
-    mine_refs, other_refs, (out_ref, feats_ref) = refs[:4], refs[4:8], refs[8:]
+    mine_refs, other_refs, (out_ref, feats_ref) = refs[:2], refs[2:4], refs[4:]
     cands = out_ref.shape[0]
-    fours, seeds, depth = mine_refs[0].shape
-    levels = 4 * fours
+    eights, seeds, depth = mine_refs[0].shape
     per_part = depth // PB
     feats_ref[...] = jnp.sum(parts_ref[...].astype(F32), axis=0)
     totals = [[jnp.zeros((seeds, PB), F32) for _ in range(2)] for _ in range(cands)]
-    for at in range(levels):
-        source = (place[1] + (2 * levels - NEAR[at // 4] - 4 * (at % 4))) % levels
+    for at in range(2 * eights):
+        source = place[1] ^ (at % 2 * 8 + at // 2 % 2 * 4 + at // 4 % 2 * 2 + at // 8)
         for part in range(per_part):
             feat = [
                 feats_ref[pl.ds(c * KB + source * per_part + part, 1), :] for c in range(cands)
             ]
-            for half, seeds_ref in enumerate((mine_refs[at // 4], other_refs[at // 4])):
-                seed = seeds_ref[at % 4, :, part * PB : (part + 1) * PB].astype(F32)
+            for half, seeds_ref in enumerate((mine_refs[at // eights], other_refs[at // eights])):
+                seed = seeds_ref[at % eights, :, part * PB : (part + 1) * PB].astype(F32)
                 for c in range(cands):
                     totals[c][half] = totals[c][half] + feat[c] * seed
     first_core = place[0] == 0
@@ -218,15 +217,23 @@
     seeds_dev = seed_feats.shape[0]
     out_seeds = data_size * seeds_dev // model_size
 
-    seed_moved = lax.ppermute(
-        seed_feats,
-        ("dp", "mp"),
-        [
-            (d * model_size + m, (m * 2 + d % 2) * model_size + d // 2)
-            for d in range(data_size)
-            for m in range(model_size)
-        ],
-    )
+    levels = data_size // 2
+
+    def to_column(flip):
+        return lax.ppermute(
+            seed_feats,
+            ("dp", "mp"),
+            [
+                (d * model_size + m, ((m ^ flip) * 2 + d % 2) * model_size + d // 2)
+                for d in range(data_size)
+                for m in range(model_size)
+            ],
+        )
+
+    def from_level(block, flip):
+        return lax.ppermute(block, "dp", [(d, d ^ (2 * flip)) for d in range(data_size)])
+
+    seed_near, seed_far = to_column(0), to_column(levels // 2)
     chunk = 4 * R // model_size
 
     def per_cand(*shape):
@@ -283,10 +290,11 @@
         up_value,
     )
 
-    send, seed_moved = lax.optimization_barrier((send, seed_moved))
+    send, seed_near, seed_far = lax.optimization_barrier((send, seed_near, seed_far))
     received = lax.all_to_all(send, "mp", 0, 0, tiled=True)
-    far = [seed_moved] + [move_z(seed_moved, 4 * j, data_size) for j in range(1, 4)]
-    received, *far = lax.optimization_barrier((received, *far))
+    two = jnp.stack([seed_near, seed_far])
+    two_more = from_level(two, 4)
+    received, two, two_more = lax.optimization_barrier((received, two, two_more))
     summed = pl.pallas_call(
         sum_kernel,
         name="lowrank_sum",
@@ -296,9 +304,11 @@
         compiler_params=PARAMS,
     )(received)
     lowrank = lax.all_to_all(summed, "mp", 0, 0, tiled=True)
-    four = jnp.stack(far)
-    near = [four] + [move_z(four, e, data_size) for e in NEAR[1:]]
-    lowrank, *near = lax.optimization_barrier((lowrank, *near))
+    four = jnp.concatenate([two, two_more])
+    four_more = from_level(four, 2)
+    lowrank, four, four_more = lax.optimization_barrier((lowrank, four, four_more))
+    eight = jnp.concatenate([four, four_more])
+    eight_more = from_level(eight, 1)
 
     feat_parts = pl.pallas_call(
         feature_kernel,
@@ -319,30 +329,21 @@
         tile_value.reshape(KVH, DH),
         tile_bank,
     )
-    feat_parts, *near = lax.optimization_barrier((feat_parts, *near))
+    feat_parts, eight = lax.optimization_barrier((feat_parts, eight))
     feat_all = lax.all_to_all(feat_parts, "mp", 0, 0, tiled=True)
     swap = [(d, d ^ 1) for d in range(data_size)]
-    other = [lax.ppermute(four, "dp", swap) for four in near]
+    other = [lax.ppermute(part, "dp", swap) for part in (eight, eight_more)]
     place = jnp.stack([lax.axis_index("dp") % 2, lax.axis_index("dp") // 2]).astype(jnp.int32)
 
     return pl.pallas_call(
         score_kernel,
         name="scores",
         out_shape=jax.ShapeDtypeStruct((cands, out_seeds), F32),
-        in_specs=[SMEM] + [VMEM] * 9,
+        in_specs=[SMEM] + [VMEM] * 5,
         out_specs=VMEM,
         scratch_shapes=[pltpu.VMEM((cands * KB, PB), F32)],
         compiler_params=PARAMS,
-    )(place, feat_all, *near, *other)
-
-
-NEAR = (0, 1, 2, -1)
-
-
-def move_z(block, steps, data_size):
-    return lax.ppermute(
-        block, "dp", [(d, (d + 2 * steps) % data_size) for d in range(data_size)]
-    )
+    )(place, feat_all, eight, eight_more, *other)
 
 
 def solution(mesh):

time: 112 us -> 107 us (0.955)
  the two profiles are of different devices: /device:TPU:1 before, /device:TPU:32 now
where the time goes in v5:
time: 107 us; the launch traced here: 106 us
  starting transfers between devices  50.7 us (47%)
  waiting for transfers between devices  31.4 us (29%)
  Pallas kernels  19.7 us (18%)
  local copies, waits for them, and re-layouts  3.78 us (4%)
    ppermute x2, starting transfers between devices, to_column(): lax.ppermute(seed_feats, ('dp', 'mp'), [(d * model_size + m, ((m ^ flip)...  18.2 us
    pallas_call x1, Pallas kernels, local(): pl.pallas_call(attention_kernel, name='attention_backward', out_shape=(ja...  13.8 us
    ppermute x3, waiting for transfers between devices, from_level(): lax.ppermute(block, 'dp', [(d, d ^ 2 * flip) for d in range(data_size)])  12.5 us
    all_to_all x1, starting transfers between devices, local(): received = lax.all_to_all(send, 'mp', 0, 0, tiled=True)  10.8 us
    ppermute x3, starting transfers between devices, from_level(): lax.ppermute(block, 'dp', [(d, d ^ 2 * flip) for d in range(data_size)])  10.2 us
    all_to_all x1, waiting for transfers between devices, local(): lowrank = lax.all_to_all(summed, 'mp', 0, 0, tiled=True)  7.23 us
    all_to_all x1, waiting for transfers between devices, local(): received = lax.all_to_all(send, 'mp', 0, 0, tiled=True)  5.98 us
    all_to_all x1, waiting for transfers between devices, local(): feat_all = lax.all_to_all(feat_parts, 'mp', 0, 0, tiled=True)  5.63 us
  transfers between devices with their start and end apart: 10, of which 5 were waited for; matrix products, arithmetic and copies ran while one was open for 0% of the time, Pallas kernels for 15%

profile of v5, /device:TPU:32, one launch (start us, length us, event | category | flops | bytes accessed | tf_op | source)
XLA Modules:
  0.0 105.9 jit_solution(10534986429289145664)
XLA Ops:
  0.0 15.4 %collective-permute-start.1 = (bf16[32,512]{1,0:T(8,128)(2,1)}, bf16[32,512]{1,0:T(8,128)(2,1)S(1)}, u32[]{:S(2)}, u32[]{:S(2)}) collective-permute-start(bf16[32,512]{1,0:T(8,128)(2,1)} %param.31), channel_id=1, source_target_pairs={{0,256},{1,288},{2,320},{3,352},{4,384},{5,416},{6,448},{7,480},{8... | collective-permute-start | bytes 98312 | tf_op jit(solution)/shard_map/ppermute | solution.py:223
  15.4 2.8 %collective-permute-start = (bf16[32,512]{1,0:T(8,128)(2,1)}, bf16[32,512]{1,0:T(8,128)(2,1)S(1)}, u32[]{:S(2)}, u32[]{:S(2)}) collective-permute-start(bf16[32,512]{1,0:T(8,128)(2,1)} %param.31), channel_id=1, source_target_pairs={{0,0},{1,32},{2,64},{3,96},{4,128},{5,160},{6,192},{7,224},{8,256}... | collective-permute-start | bytes 98312 | tf_op jit(solution)/shard_map/ppermute | solution.py:223
  18.2 13.8 %attention_backward.1 = (bf16[16,2,32,512]{3,2,1,0:T(8,128)(2,1)}, bf16[2,512,512]{2,1,0:T(8,128)(2,1)}, bf16[2,512,128]{2,1,0:T(8,128)(2,1)}) custom-call(s32[1]{0:T(128)} %bitcast.2.kv_index, bf16[2,512,512]{2,1,0:T(8,128)(2,1)} %hidden_ref.3, bf16[2,512,512]{2,1,0:T(8,128)(2,1)} %query_ref.1, bf16[2,512,512]{2,1,0:T(8,128)(2,1)} %grad_ref.1, ...), custom_call_target="tpu_custom_call" | custom-call | flops 5000000000 | bytes 8000000 | tf_op jit(solution)/shard_map/attention_backward/pallas_call | solution.py:245
  32.1 0.0 collective-permute-done.1
  32.1 0.0 collective-permute-done
  32.1 10.8 %all-to-all-start = ((bf16[16,2,32,512]{3,2,1,0:T(8,128)(2,1)}), bf16[16,2,32,512]{3,2,1,0:T(8,128)(2,1)S(1)}, u32[]{:S(2)}, u32[]{:S(2)}) async-start(bf16[16,2,32,512]{3,2,1,0:T(8,128)(2,1)} %get-tuple-element.20), calls=%async_computation | async-start | bytes 2097152 | tf_op jit(solution)/shard_map/all_to_all | solution.py:294
  42.9 0.0 copy-start
  42.9 0.0 copy-start.4
  42.9 0.0 copy-start.5
  42.9 0.0 copy-start.6
  42.9 0.0 copy-start.7
  42.9 4.2 %collective-permute-start.2 = (bf16[2,32,512]{2,1,0:T(8,128)(2,1)S(1)}, bf16[2,32,512]{2,1,0:T(8,128)(2,1)S(1)}, u32[]{:S(2)}, u32[]{:S(2)}) collective-permute-start(bf16[2,32,512]{2,1,0:T(8,128)(2,1)S(1)} %pad_maximum_fusion), channel_id=1, source_target_pairs={{0,128},{16,144},{32,160},{48,176},{64,192},{80,208},{96,224},{112... | collective-permute-start | bytes 196616 | tf_op jit(solution)/shard_map/ppermute | solution.py:234
  47.1 6.6 %collective-permute-done.2 = bf16[2,32,512]{2,1,0:T(8,128)(2,1)S(1)} collective-permute-done((bf16[2,32,512]{2,1,0:T(8,128)(2,1)S(1)}, bf16[2,32,512]{2,1,0:T(8,128)(2,1)S(1)}, u32[]{:S(2)}, u32[]{:S(2)}) %collective-permute-start.2) | collective-permute-done | bytes 65568 | tf_op jit(solution)/shard_map/ppermute | solution.py:234
  53.7 6.0 %all-to-all-done.parts_ref = bf16[16,2,32,512]{3,2,1,0:T(8,128)(2,1)S(1)} async-done(((bf16[16,2,32,512]{3,2,1,0:T(8,128)(2,1)}), bf16[16,2,32,512]{3,2,1,0:T(8,128)(2,1)S(1)}, u32[]{:S(2)}, u32[]{:S(2)}) %all-to-all-start) | async-done | bytes 1048608 | tf_op jit(solution)/shard_map/all_to_all | solution.py:294
  59.7 1.2 %lowrank_sum.1 = bf16[16,2,32,512]{3,2,1,0:T(8,128)(2,1)} custom-call(bf16[16,2,32,512]{3,2,1,0:T(8,128)(2,1)S(1)} %all-to-all-done.parts_ref), custom_call_target="tpu_custom_call" | custom-call | tf_op jit(solution)/shard_map/lowrank_sum/pallas_call | solution.py:298
  60.9 3.7 %all-to-all-start.1 = ((bf16[16,2,32,512]{3,2,1,0:T(8,128)(2,1)}), bf16[16,2,32,512]{3,2,1,0:T(8,128)(2,1)S(1)}, u32[]{:S(2)}, u32[]{:S(2)}) async-start(bf16[16,2,32,512]{3,2,1,0:T(8,128)(2,1)} %lowrank_sum.1), calls=%async_computation.1 | async-start | bytes 2097152 | tf_op jit(solution)/shard_map/all_to_all | solution.py:306
  64.6 2.1 %collective-permute-start.3 = (bf16[4,32,512]{2,1,0:T(8,128)(2,1)S(1)}, bf16[4,32,512]{2,1,0:T(8,128)(2,1)}, u32[]{:S(2)}, u32[]{:S(2)}) collective-permute-start(bf16[4,32,512]{2,1,0:T(8,128)(2,1)S(1)} %constant_dynamic-update-slice_fusion), channel_id=1, source_target_pairs={{0,64},{16,80},{32,96},{48,112},{64,0},{80,16},{96,32},{112,48},{1... | collective-permute-start | bytes 393224 | tf_op jit(solution)/shard_map/ppermute | solution.py:234
  66.6 5.9 %collective-permute-done.3 = bf16[4,32,512]{2,1,0:T(8,128)(2,1)} collective-permute-done((bf16[4,32,512]{2,1,0:T(8,128)(2,1)S(1)}, bf16[4,32,512]{2,1,0:T(8,128)(2,1)}, u32[]{:S(2)}, u32[]{:S(2)}) %collective-permute-start.3) | collective-permute-done | bytes 131104 | tf_op jit(solution)/shard_map/ppermute | solution.py:234
  72.5 7.2 %all-to-all-done.1.lowrank_ref = bf16[16,2,32,512]{3,2,1,0:T(8,128)(2,1)S(1)} async-done(((bf16[16,2,32,512]{3,2,1,0:T(8,128)(2,1)}), bf16[16,2,32,512]{3,2,1,0:T(8,128)(2,1)S(1)}, u32[]{:S(2)}, u32[]{:S(2)}) %all-to-all-start.1) | async-done | bytes 1048608 | tf_op jit(solution)/shard_map/all_to_all | solution.py:306
  79.8 0.9 constant_dynamic-update-slice_fusion.3
  80.7 0.9 constant_dynamic-update-slice_fusion.2.refs_0_
  81.6 4.0 %collective-permute-start.4 = (bf16[8,32,512]{2,1,0:T(8,128)(2,1)S(1)}, bf16[8,32,512]{2,1,0:T(8,128)(2,1)}, u32[]{:S(2)}, u32[]{:S(2)}) collective-permute-start(bf16[8,32,512]{2,1,0:T(8,128)(2,1)S(1)} %constant_dynamic-update-slice_fusion.2.refs_0_), channel_id=1, source_target_pairs={{0,32},{16,48},{32,0},{48,16},{64,96},{80,112},{96,64},{112,80},{1... | collective-permute-start | bytes 786440 | tf_op jit(solution)/shard_map/ppermute | solution.py:234
  85.7 0.0 copy-start.2
  85.7 0.9 copy-done.2
  86.6 0.9 copy-done.3
  87.6 2.5 %partial_features.1 = bf16[16,128,128]{2,1,0:T(8,128)(2,1)} custom-call(s32[1]{0:T(128)} %bitcast.2.kv_index, bf16[16,2,32,512]{3,2,1,0:T(8,128)(2,1)S(1)} %all-to-all-done.1.lowrank_ref, bf16[2,512,512]{2,1,0:T(8,128)(2,1)S(1)} %copy-done, bf16[2,512,512]{2,1,0:T(8,128)(2,1)S(1)} %copy-done.1, bf16[2,512,128]{2,1,0:T(8,128)(2,1)S(1)} %copy-done.3, ...), custom_call_target="tpu_custom_call" | custom-call | tf_op jit(solution)/shard_map/partial_features/pallas_call | solution.py:313
  90.0 3.6 %all-to-all-start.2 = ((bf16[16,128,128]{2,1,0:T(8,128)(2,1)}), bf16[16,128,128]{2,1,0:T(8,128)(2,1)S(1)}, u32[]{:S(2)}, u32[]{:S(2)}) async-start(bf16[16,128,128]{2,1,0:T(8,128)(2,1)} %partial_features.1), calls=%async_computation.2 | async-start | bytes 1048576 | tf_op jit(solution)/shard_map/all_to_all | solution.py:333
  93.6 1.9 %collective-permute-start.5 = (bf16[8,32,512]{2,1,0:T(8,128)(2,1)S(1)}, bf16[8,32,512]{2,1,0:T(8,128)(2,1)S(1)}, u32[]{:S(2)}, u32[]{:S(2)}) collective-permute-start(bf16[8,32,512]{2,1,0:T(8,128)(2,1)S(1)} %constant_dynamic-update-slice_fusion.2.refs_0_), channel_id=1, source_target_pairs={{0,16},{16,0},{32,48},{48,32},{64,80},{80,64},{96,112},{112,96},{1... | collective-permute-start | bytes 786440 | tf_op jit(solution)/shard_map/ppermute | solution.py:335
  95.6 2.4 %collective-permute-start.6 = (bf16[8,32,512]{2,1,0:T(8,128)(2,1)}, bf16[8,32,512]{2,1,0:T(8,128)(2,1)S(1)}, u32[]{:S(2)}, u32[]{:S(2)}) collective-permute-start(bf16[8,32,512]{2,1,0:T(8,128)(2,1)} %collective-permute-done.4.refs_1_), channel_id=1, source_target_pairs={{0,16},{16,0},{32,48},{48,32},{64,80},{80,64},{96,112},{112,96},{1... | collective-permute-start | bytes 786440 | tf_op jit(solution)/shard_map/ppermute | solution.py:335
  98.0 0.1 pad_add_fusion.place
  98.1 5.6 %all-to-all-done.2.parts_ref = bf16[16,128,128]{2,1,0:T(8,128)(2,1)S(1)} async-done(((bf16[16,128,128]{2,1,0:T(8,128)(2,1)}), bf16[16,128,128]{2,1,0:T(8,128)(2,1)S(1)}, u32[]{:S(2)}, u32[]{:S(2)}) %all-to-all-start.2) | async-done | bytes 524320 | tf_op jit(solution)/shard_map/all_to_all | solution.py:333
  103.7 2.2 %scores.1 = f32[2,64]{1,0:T(2,128)} custom-call(s32[2]{0:T(128)S(1)} %pad_add_fusion.place, bf16[16,128,128]{2,1,0:T(8,128)(2,1)S(1)} %all-to-all-done.2.parts_ref, bf16[8,32,512]{2,1,0:T(8,128)(2,1)S(1)} %constant_dynamic-update-slice_fusion.2.refs_0_, bf16[8,32,512]{2,1,0:T(8,128)(2,1)} %collective-permute-done.4.refs_1_, ...), custom_call_target="tpu_custom_call" | custom-call | tf_op jit(solution)/shard_map/scores/pallas_call | solution.py:338
  (16 shorter events, 0.1 us)
Async XLA Ops:
  0.0 32.1 %collective-permute-start.1 = (bf16[32,512]{1,0:T(8,128)(2,1)}, bf16[32,512]{1,0:T(8,128)(2,1)S(1)}, u32[]{:S(2)}, u32[]{:S(2)}) collective-permute-start(bf16[32,512]{1,0:T(8,128)(2,1)} %param.31), channel_id=1, source_target_pairs={{0,256},{1,288},{2,320},{3,352},{4,384},{5,416},{6,448},{7,480},{8... | collective-permute-start | bytes 98312 | tf_op jit(solution)/shard_map/ppermute | solution.py:223
  15.4 16.7 %collective-permute-start = (bf16[32,512]{1,0:T(8,128)(2,1)}, bf16[32,512]{1,0:T(8,128)(2,1)S(1)}, u32[]{:S(2)}, u32[]{:S(2)}) collective-permute-start(bf16[32,512]{1,0:T(8,128)(2,1)} %param.31), channel_id=1, source_target_pairs={{0,0},{1,32},{2,64},{3,96},{4,128},{5,160},{6,192},{7,224},{8,256}... | collective-permute-start | bytes 98312 | tf_op jit(solution)/shard_map/ppermute | solution.py:223
  32.1 27.6 %all-to-all-start = ((bf16[16,2,32,512]{3,2,1,0:T(8,128)(2,1)}), bf16[16,2,32,512]{3,2,1,0:T(8,128)(2,1)S(1)}, u32[]{:S(2)}, u32[]{:S(2)}) async-start(bf16[16,2,32,512]{3,2,1,0:T(8,128)(2,1)} %get-tuple-element.20), calls=%async_computation | async-start | bytes 2097152 | tf_op jit(solution)/shard_map/all_to_all | solution.py:294
  42.9 42.7 %copy-start = (bf16[2,512,512]{2,1,0:T(8,128)(2,1)S(1)}, bf16[2,512,512]{2,1,0:T(8,128)(2,1)}, u32[]{:S(2)}) copy-start(bf16[2,512,512]{2,1,0:T(8,128)(2,1)} %hidden_ref.3) | copy-start | bytes 3145732
  42.9 42.7 %copy-start.1 = (bf16[2,512,512]{2,1,0:T(8,128)(2,1)S(1)}, bf16[2,512,512]{2,1,0:T(8,128)(2,1)}, u32[]{:S(2)}) copy-start(bf16[2,512,512]{2,1,0:T(8,128)(2,1)} %get-tuple-element.27.query_grad_ref) | copy-start | bytes 3145732
  42.9 42.7 %copy-start.4 = (s32[3,512]{1,0:T(4,128)S(1)}, s32[3,512]{1,0:T(4,128)}, u32[]{:S(2)}) copy-start(s32[3,512]{1,0:T(4,128)} %block_ref.1) | copy-start | bytes 18436
  42.9 42.7 %copy-start.5 = (s32[3,512]{1,0:T(4,128)S(1)}, s32[3,512]{1,0:T(4,128)}, u32[]{:S(2)}) copy-start(s32[3,512]{1,0:T(4,128)} %tile_ref.1) | copy-start | bytes 18436
  42.9 42.7 %copy-start.6 = (s32[1024]{0:T(1024)S(1)}, s32[1024]{0:T(1024)}, u32[]{:S(2)}) copy-start(s32[1024]{0:T(1024)} %param.28) | copy-start | bytes 12292
  42.9 42.7 %copy-start.7 = (s32[1024]{0:T(1024)S(1)}, s32[1024]{0:T(1024)}, u32[]{:S(2)}) copy-start(s32[1024]{0:T(1024)} %param.29) | copy-start | bytes 12292
  42.9 10.8 %collective-permute-start.2 = (bf16[2,32,512]{2,1,0:T(8,128)(2,1)S(1)}, bf16[2,32,512]{2,1,0:T(8,128)(2,1)S(1)}, u32[]{:S(2)}, u32[]{:S(2)}) collective-permute-start(bf16[2,32,512]{2,1,0:T(8,128)(2,1)S(1)} %pad_maximum_fusion), channel_id=1, source_target_pairs={{0,128},{16,144},{32,160},{48,176},{64,192},{80,208},{96,224},{112... | collective-permute-start | bytes 196616 | tf_op jit(solution)/shard_map/ppermute | solution.py:234
  60.9 18.9 %all-to-all-start.1 = ((bf16[16,2,32,512]{3,2,1,0:T(8,128)(2,1)}), bf16[16,2,32,512]{3,2,1,0:T(8,128)(2,1)S(1)}, u32[]{:S(2)}, u32[]{:S(2)}) async-start(bf16[16,2,32,512]{3,2,1,0:T(8,128)(2,1)} %lowrank_sum.1), calls=%async_computation.1 | async-start | bytes 2097152 | tf_op jit(solution)/shard_map/all_to_all | solution.py:306
  64.5 8.0 %copy-start.8 = (bf16[4,32,512]{2,1,0:T(8,128)(2,1)}, bf16[4,32,512]{2,1,0:T(8,128)(2,1)S(1)}, u32[]{:S(2)}) copy-start(bf16[4,32,512]{2,1,0:T(8,128)(2,1)S(1)} %constant_dynamic-update-slice_fusion) | copy-start | bytes 393220
  64.6 8.0 %collective-permute-start.3 = (bf16[4,32,512]{2,1,0:T(8,128)(2,1)S(1)}, bf16[4,32,512]{2,1,0:T(8,128)(2,1)}, u32[]{:S(2)}, u32[]{:S(2)}) collective-permute-start(bf16[4,32,512]{2,1,0:T(8,128)(2,1)S(1)} %constant_dynamic-update-slice_fusion), channel_id=1, source_target_pairs={{0,64},{16,80},{32,96},{48,112},{64,0},{80,16},{96,32},{112,48},{1... | collective-permute-start | bytes 393224 | tf_op jit(solution)/shard_map/ppermute | solution.py:234
  81.6 14.0 %collective-permute-start.4 = (bf16[8,32,512]{2,1,0:T(8,128)(2,1)S(1)}, bf16[8,32,512]{2,1,0:T(8,128)(2,1)}, u32[]{:S(2)}, u32[]{:S(2)}) collective-permute-start(bf16[8,32,512]{2,1,0:T(8,128)(2,1)S(1)} %constant_dynamic-update-slice_fusion.2.refs_0_), channel_id=1, source_target_pairs={{0,32},{16,48},{32,0},{48,16},{64,96},{80,112},{96,64},{112,80},{1... | collective-permute-start | bytes 786440 | tf_op jit(solution)/shard_map/ppermute | solution.py:234
  85.7 1.0 copy-start.2
  86.6 0.9 copy-start.3
  90.0 13.7 %all-to-all-start.2 = ((bf16[16,128,128]{2,1,0:T(8,128)(2,1)}), bf16[16,128,128]{2,1,0:T(8,128)(2,1)S(1)}, u32[]{:S(2)}, u32[]{:S(2)}) async-start(bf16[16,128,128]{2,1,0:T(8,128)(2,1)} %partial_features.1), calls=%async_computation.2 | async-start | bytes 1048576 | tf_op jit(solution)/shard_map/all_to_all | solution.py:333
  93.6 4.5 %collective-permute-start.5 = (bf16[8,32,512]{2,1,0:T(8,128)(2,1)S(1)}, bf16[8,32,512]{2,1,0:T(8,128)(2,1)S(1)}, u32[]{:S(2)}, u32[]{:S(2)}) collective-permute-start(bf16[8,32,512]{2,1,0:T(8,128)(2,1)S(1)} %constant_dynamic-update-slice_fusion.2.refs_0_), channel_id=1, source_target_pairs={{0,16},{16,0},{32,48},{48,32},{64,80},{80,64},{96,112},{112,96},{1... | collective-permute-start | bytes 786440 | tf_op jit(solution)/shard_map/ppermute | solution.py:335
  95.6 8.1 %collective-permute-start.6 = (bf16[8,32,512]{2,1,0:T(8,128)(2,1)}, bf16[8,32,512]{2,1,0:T(8,128)(2,1)S(1)}, u32[]{:S(2)}, u32[]{:S(2)}) collective-permute-start(bf16[8,32,512]{2,1,0:T(8,128)(2,1)} %collective-permute-done.4.refs_1_), channel_id=1, source_target_pairs={{0,16},{16,0},{32,48},{48,32},{64,80},{80,64},{96,112},{112,96},{1... | collective-permute-start | bytes 786440 | tf_op jit(solution)/shard_map/ppermute | solution.py:335

commit v6 on v5

--- a/solution.py
+++ b/solution.py
@@ -19,6 +19,7 @@
 EPS = 1e-06
 LONGEST = 256
 ROWS = 128
+CHUNK = 32
 F32 = jnp.float32
 BF16 = jnp.bfloat16
 
@@ -44,9 +45,14 @@
     up_query_ref,
     up_value_ref,
     send_ref,
-    query_grad_ref,
-    value_grad_ref,
+    head_grad_ref,
     value_sum,
+    down_t,
+    bias_ref,
+    logit_ref,
+    prob_grad_ref,
+    prob_ref,
+    logit_grad_ref,
 ):
     cand = pl.program_id(0)
     parts = send_ref.shape[0]
@@ -56,15 +62,17 @@
     score_scale = 1.0 / math.sqrt(DH)
     exp_scale = score_scale * math.log2(math.e)
 
-    down = jnp.concatenate([down_query_ref[...].T, down_value_ref[...].T], axis=0)
-    lowrank_in = dot_nt(down, hidden_ref[0])
+    @pl.when(cand == 0)
+    def _():
+        down_t[:R] = down_query_ref[...].T
+        down_t[R:] = down_value_ref[...].T
+
+    lowrank_in = dot_nt(down_t[...], hidden_ref[0])
     send_ref[0 : 2 * quarter, 0] = lowrank_in.astype(BF16).reshape(2 * quarter, chunk, S)
 
     segment_row = segment_ref[pl.ds(cand, 1), :].astype(F32)
     segment_col = jnp.broadcast_to(segment_row, (8, S)).T[:, 0:1]
-    key = key_ref[0]
-    value = value_ref[0]
-    key_t = key.T
+    key_t = key_ref[0].T
     value_sum[...] = jnp.zeros_like(value_sum)
 
     for block in range(S // ROWS):
@@ -72,30 +80,66 @@
         low = max(0, (first - LONGEST + 1) // ROWS * ROWS)
         high = first + ROWS
         width = high - low
-        key_pos = low + lax.broadcasted_iota(jnp.int32, (width, ROWS), 0)
-        row_pos = first + lax.broadcasted_iota(jnp.int32, (width, ROWS), 1)
-        allowed = (key_pos <= row_pos) & (
-            segment_col[low:high] == segment_row[:, first:high]
-        )
-        bias = jnp.where(allowed, 0.0, -1e30)
-        for head in range(heads):
-            cols = slice(head * DH, (head + 1) * DH)
-            grad = grad_ref[0, first:high, cols]
-            logits = dot_nt(key[low:high], query_ref[0, first:high, cols]) + bias
-            row_top = jnp.max(logits, axis=0, keepdims=True)
-            exp_terms = jnp.exp2((logits - row_top) * exp_scale)
-            probs = exp_terms * (1.0 / jnp.sum(exp_terms, axis=0, keepdims=True))
-            prob_grad = dot_nt(value[low:high], grad)
-            row_delta = jnp.sum(probs * prob_grad, axis=0, keepdims=True)
-            logit_grad = (probs * (prob_grad - row_delta)).astype(BF16)
-            value_sum[low:high] += dot_nn(probs.astype(BF16), grad)
-            query_grad = dot_nn(key_t[:, low:high], logit_grad) * score_scale
-            query_grad_ref[0, cols, first:high] = query_grad.astype(BF16)
-
-    value_grad = value_sum[...].astype(BF16)
-    value_grad_ref[0] = value_grad
-    back_query = dot_nn(up_query_ref[...], query_grad_ref[0])
-    back_value = dot_nt(up_value_ref[...], value_grad)
+        for at in range(0, width, ROWS):
+            allowed = segment_col[low + at : low + at + ROWS] == segment_row[:, first:high]
+            if low + at == first:
+                key_pos = lax.broadcasted_iota(jnp.int32, (ROWS, ROWS), 0)
+                row_pos = lax.broadcasted_iota(jnp.int32, (ROWS, ROWS), 1)
+                allowed = allowed & (key_pos <= row_pos)
+            bias_ref[block, at : at + ROWS] = jnp.where(allowed, 0.0, -1e30)
+    for block in range(S // ROWS):
+        first = block * ROWS
+        low = max(0, (first - LONGEST + 1) // ROWS * ROWS)
+        high = first + ROWS
+        width = high - low
+        slot = block % 2
+
+        def stacked(ref):
+            return jnp.concatenate(
+                [ref[0, first:high, h * DH : (h + 1) * DH] for h in range(heads)], axis=0
+            )
+
+        grad = stacked(grad_ref)
+        logit_ref[slot, :width] = dot_nt(key_ref[0, low:high], stacked(query_ref))
+        prob_grad_ref[slot, :width] = dot_nt(value_ref[0, low:high], grad)
+
+        def logits(at):
+            bias = bias_ref[block, at : at + CHUNK]
+            return logit_ref[slot, at : at + CHUNK] + jnp.concatenate([bias] * heads, axis=1)
+
+        lanes = heads * ROWS
+        top = jnp.full((8, lanes), -3e38, F32)
+        for at in range(0, width, CHUNK):
+            top = jnp.maximum(top, jnp.max(logits(at).reshape(CHUNK // 8, 8, lanes), axis=0))
+        row_top = jnp.max(top, axis=0, keepdims=True)
+        total = jnp.zeros((8, lanes), F32)
+        delta = jnp.zeros((8, lanes), F32)
+        for at in range(0, width, CHUNK):
+            terms = jnp.exp2((logits(at) - row_top) * exp_scale)
+            total = total + jnp.sum(terms.reshape(CHUNK // 8, 8, lanes), axis=0)
+            weighted = terms * prob_grad_ref[slot, at : at + CHUNK]
+            delta = delta + jnp.sum(weighted.reshape(CHUNK // 8, 8, lanes), axis=0)
+            logit_ref[slot, at : at + CHUNK] = terms
+        inverse = 1.0 / jnp.sum(total, axis=0, keepdims=True)
+        row_delta = jnp.sum(delta, axis=0, keepdims=True) * inverse
+        for at in range(0, width, CHUNK):
+            probs = logit_ref[slot, at : at + CHUNK] * inverse
+            prob_ref[slot, at : at + CHUNK] = probs.astype(BF16)
+            logit_grad_ref[slot, at : at + CHUNK] = (
+                probs * (prob_grad_ref[slot, at : at + CHUNK] - row_delta)
+            ).astype(BF16)
+        value_sum[low:high] += dot_nn(prob_ref[slot, :width], grad)
+        query_grad = dot_nn(key_t[:, low:high], logit_grad_ref[slot, :width]) * score_scale
+        query_grad = query_grad.astype(BF16)
+        for h in range(heads):
+            head_grad_ref[0, h * DH : (h + 1) * DH, first:high] = query_grad[
+                :, h * ROWS : (h + 1) * ROWS
+            ]
+
+    value_grad = value_sum[...].T.astype(BF16)
+    head_grad_ref[0, heads * DH :] = value_grad
+    back_query = dot_nn(up_query_ref[...], head_grad_ref[0, : heads * DH])
+    back_value = dot_nn(up_value_ref[...], value_grad)
     send_ref[2 * quarter : 3 * quarter, 0] = back_query.astype(BF16).reshape(quarter, chunk, S)
     send_ref[3 * quarter : parts, 0] = back_value.astype(BF16).reshape(quarter, chunk, S)
 
@@ -109,16 +153,20 @@
     kv_index,
     lowrank_ref,
     hidden_ref,
-    query_grad_ref,
-    value_grad_ref,
+    head_grad_ref,
     block_ref,
     tile_ref,
     block_value_ref,
     tile_value_ref,
+    bank_hbm,
+    out_ref,
     bank_ref,
-    out_ref,
+    bank_sem,
 ):
+    bank_copy = pltpu.make_async_copy(bank_hbm, bank_ref, bank_sem)
+    bank_copy.start()
     cands = hidden_ref.shape[0]
+    width = head_grad_ref.shape[1] - DH
     kv = kv_index[0]
     pieces = [[], [], [], []]
     for cand in range(cands):
@@ -126,8 +174,8 @@
         down = dot_nn(lowrank[2 * R :], hidden_ref[cand])
         pieces[0].append(down[:R])
         pieces[1].append(down[R:])
-        pieces[2].append(dot_nt(lowrank[:R], query_grad_ref[cand]))
-        pieces[3].append(dot_nn(lowrank[R : 2 * R], value_grad_ref[cand]))
+        pieces[2].append(dot_nt(lowrank[:R], head_grad_ref[cand, :width]))
+        pieces[3].append(dot_nt(lowrank[R : 2 * R], head_grad_ref[cand, width:]))
     buckets = KB * NT
     sums = jnp.zeros((buckets, cands * R), F32)
     for kind in range(4):
@@ -150,26 +198,27 @@
     )
     high = wide.astype(BF16)
     low = (wide - high.astype(F32)).astype(BF16)
+    bank_copy.wait()
     bank = bank_ref[...].reshape(NT * R, PB)
     feats = dot_nn(high, bank) + dot_nn(low, bank)
     out_ref[...] = jnp.broadcast_to(feats.astype(BF16)[None], out_ref.shape)
 
 
 def score_kernel(place, parts_ref, *refs):
-    mine_refs, other_refs, (out_ref, feats_ref) = refs[:2], refs[2:4], refs[4:]
+    mine_refs, other_refs, (out_ref, feats_ref) = refs[:4], refs[4:8], refs[8:]
     cands = out_ref.shape[0]
-    eights, seeds, depth = mine_refs[0].shape
+    fours, seeds, depth = mine_refs[0].shape
     per_part = depth // PB
     feats_ref[...] = jnp.sum(parts_ref[...].astype(F32), axis=0)
     totals = [[jnp.zeros((seeds, PB), F32) for _ in range(2)] for _ in range(cands)]
-    for at in range(2 * eights):
+    for at in range(4 * fours):
         source = place[1] ^ (at % 2 * 8 + at // 2 % 2 * 4 + at // 4 % 2 * 2 + at // 8)
         for part in range(per_part):
             feat = [
                 feats_ref[pl.ds(c * KB + source * per_part + part, 1), :] for c in range(cands)
             ]
-            for half, seeds_ref in enumerate((mine_refs[at // eights], other_refs[at // eights])):
-                seed = seeds_ref[at % eights, :, part * PB : (part + 1) * PB].astype(F32)
+            for half, seeds_ref in enumerate((mine_refs[at // fours], other_refs[at // fours])):
+                seed = seeds_ref[at % fours, :, part * PB : (part + 1) * PB].astype(F32)
                 for c in range(cands):
                     totals[c][half] = totals[c][half] + feat[c] * seed
     first_core = place[0] == 0
@@ -186,7 +235,7 @@
 
 VMEM = pl.BlockSpec(memory_space=pltpu.VMEM)
 SMEM = pl.BlockSpec(memory_space=pltpu.SMEM)
-PARAMS = pltpu.CompilerParams(vmem_limit_bytes=40 << 20)
+PARAMS = pltpu.CompilerParams(vmem_limit_bytes=24 << 20)
 
 
 def local(
@@ -233,8 +282,12 @@
     def from_level(block, flip):
         return lax.ppermute(block, "dp", [(d, d ^ (2 * flip)) for d in range(data_size)])
 
+    def from_core(block):
+        return lax.ppermute(block, "dp", [(d, d ^ 1) for d in range(data_size)])
+
     seed_near, seed_far = to_column(0), to_column(levels // 2)
     chunk = 4 * R // model_size
+    span = LONGEST + ROWS
 
     def per_cand(*shape):
         return pl.BlockSpec((1, *shape), lambda c, kv_ref: (c, 0, 0))
@@ -242,13 +295,12 @@
     def whole(*shape):
         return pl.BlockSpec(shape, lambda c, kv_ref: (0,) * len(shape))
 
-    send, query_grad, value_grad = pl.pallas_call(
+    send, head_grad = pl.pallas_call(
         attention_kernel,
         name="attention_backward",
         out_shape=(
             jax.ShapeDtypeStruct((model_size, cands, chunk, seq_len), BF16),
-            jax.ShapeDtypeStruct((cands, width, seq_len), BF16),
-            jax.ShapeDtypeStruct((cands, seq_len, DH), BF16),
+            jax.ShapeDtypeStruct((cands, width + DH, seq_len), BF16),
         ),
         grid_spec=pltpu.PrefetchScalarGridSpec(
             num_scalar_prefetch=1,
@@ -267,10 +319,17 @@
             ],
             out_specs=[
                 pl.BlockSpec((model_size, 1, chunk, seq_len), lambda c, kv_ref: (0, c, 0, 0)),
-                per_cand(width, seq_len),
-                per_cand(seq_len, DH),
+                per_cand(width + DH, seq_len),
             ],
-            scratch_shapes=[pltpu.VMEM((seq_len, DH), F32)],
+            scratch_shapes=[
+                pltpu.VMEM((seq_len, DH), F32),
+                pltpu.VMEM((2 * R, hidden_in.shape[2]), BF16),
+                pltpu.VMEM((seq_len // ROWS, span, ROWS), F32),
+                pltpu.VMEM((2, span, heads * ROWS), F32),
+                pltpu.VMEM((2, span, heads * ROWS), F32),
+                pltpu.VMEM((2, span, heads * ROWS), BF16),
+                pltpu.VMEM((2, span, heads * ROWS), BF16),
+            ],
         ),
         compiler_params=pltpu.CompilerParams(vmem_limit_bytes=60 << 20),
         cost_estimate=pl.CostEstimate(
@@ -305,45 +364,45 @@
     )(received)
     lowrank = lax.all_to_all(summed, "mp", 0, 0, tiled=True)
     four = jnp.concatenate([two, two_more])
-    four_more = from_level(four, 2)
-    lowrank, four, four_more = lax.optimization_barrier((lowrank, four, four_more))
-    eight = jnp.concatenate([four, four_more])
-    eight_more = from_level(eight, 1)
+    fours = [four, from_level(four, 2), from_level(four, 1)]
+    others = [from_core(four)]
+    lowrank, *both = lax.optimization_barrier((lowrank, *fours, *others))
+    fours, others = both[:3], both[3:]
+    fours.append(from_level(fours[1], 1))
 
     feat_parts = pl.pallas_call(
         feature_kernel,
         name="partial_features",
         out_shape=jax.ShapeDtypeStruct((model_size, cands * KB, PB), BF16),
-        in_specs=[SMEM] + [VMEM] * 9,
+        in_specs=[SMEM] + [VMEM] * 7 + [pl.BlockSpec(memory_space=pltpu.HBM)],
         out_specs=VMEM,
+        scratch_shapes=[pltpu.VMEM(tile_bank.shape, BF16), pltpu.SemaphoreType.DMA],
         compiler_params=PARAMS,
     )(
         kv_index,
         lowrank,
         hidden_in,
-        query_grad,
-        value_grad,
+        head_grad,
         block_rows,
         tile_rows,
         block_value.reshape(KVH, DH),
         tile_value.reshape(KVH, DH),
         tile_bank,
     )
-    feat_parts, eight = lax.optimization_barrier((feat_parts, eight))
+    feat_parts, *fours[1:3] = lax.optimization_barrier((feat_parts, *fours[1:3]))
     feat_all = lax.all_to_all(feat_parts, "mp", 0, 0, tiled=True)
-    swap = [(d, d ^ 1) for d in range(data_size)]
-    other = [lax.ppermute(part, "dp", swap) for part in (eight, eight_more)]
+    others += [from_core(part) for part in fours[1:]]
     place = jnp.stack([lax.axis_index("dp") % 2, lax.axis_index("dp") // 2]).astype(jnp.int32)
 
     return pl.pallas_call(
         score_kernel,
         name="scores",
         out_shape=jax.ShapeDtypeStruct((cands, out_seeds), F32),
-        in_specs=[SMEM] + [VMEM] * 5,
+        in_specs=[SMEM] + [VMEM] * 9,
         out_specs=VMEM,
         scratch_shapes=[pltpu.VMEM((cands * KB, PB), F32)],
         compiler_params=PARAMS,
-    )(place, feat_all, eight, eight_more, *other)
+    )(place, feat_all, *fours, *others)
 
 
 def solution(mesh):

time: 107 us -> 107 us (level)
  the two profiles are of different devices: /device:TPU:32 before, /device:TPU:1 now
where the time goes in v6:
time: 107 us; the launch traced here: 106 us
  starting transfers between devices  64.2 us (60%)
  waiting for transfers between devices  19.4 us (18%)
  Pallas kernels  14.6 us (14%)
  local copies, waits for them, and re-layouts  7.15 us (7%)
    ppermute x2, starting transfers between devices, to_column(): lax.ppermute(seed_feats, ('dp', 'mp'), [(d * model_size + m, ((m ^ flip)...  17.7 us
    ppermute x4, waiting for transfers between devices, from_level(): lax.ppermute(block, 'dp', [(d, d ^ 2 * flip) for d in range(data_size)])  16.9 us
    all_to_all x1, starting transfers between devices, local(): received = lax.all_to_all(send, 'mp', 0, 0, tiled=True)  12.4 us
    ppermute x4, starting transfers between devices, from_core(): return lax.ppermute(block, 'dp', [(d, d ^ 1) for d in range(data_size)])  12.1 us
    ppermute x4, starting transfers between devices, from_level(): lax.ppermute(block, 'dp', [(d, d ^ 2 * flip) for d in range(data_size)])  10.2 us
    pallas_call x1, Pallas kernels, local(): pl.pallas_call(attention_kernel, name='attention_backward', out_shape=(ja...  8.6 us
    all_to_all x1, starting transfers between devices, local(): feat_all = lax.all_to_all(feat_parts, 'mp', 0, 0, tiled=True)  6.88 us
    unnamed x25, local copies, waits for them, and re-layouts  6.31 us
  transfers between devices with their start and end apart: 13, of which 5 were waited for; matrix products, arithmetic and copies ran while one was open for 2% of the time, Pallas kernels for 8%

profile of v6, /device:TPU:1, one launch (start us, length us, event | category | flops | bytes accessed | tf_op | source)
XLA Modules:
  0.0 105.7 jit_solution(14870360471206861052)
XLA Ops:
  0.0 16.3 %collective-permute-start.1 = (bf16[32,512]{1,0:T(8,128)(2,1)}, bf16[32,512]{1,0:T(8,128)(2,1)S(1)}, u32[]{:S(2)}, u32[]{:S(2)}) collective-permute-start(bf16[32,512]{1,0:T(8,128)(2,1)} %param.31), channel_id=1, source_target_pairs={{0,256},{1,288},{2,320},{3,352},{4,384},{5,416},{6,448},{7,480},{8... | collective-permute-start | bytes 98312 | tf_op jit(solution)/shard_map/ppermute | solution.py:272
  16.3 1.4 %collective-permute-start = (bf16[32,512]{1,0:T(8,128)(2,1)}, bf16[32,512]{1,0:T(8,128)(2,1)S(1)}, u32[]{:S(2)}, u32[]{:S(2)}) collective-permute-start(bf16[32,512]{1,0:T(8,128)(2,1)} %param.31), channel_id=1, source_target_pairs={{0,0},{1,32},{2,64},{3,96},{4,128},{5,160},{6,192},{7,224},{8,256}... | collective-permute-start | bytes 98312 | tf_op jit(solution)/shard_map/ppermute | solution.py:272
  17.7 8.6 %attention_backward.1 = (bf16[16,2,32,512]{3,2,1,0:T(8,128)(2,1)}, bf16[2,640,512]{2,1,0:T(8,128)(2,1)}) custom-call(s32[1]{0:T(128)} %bitcast.2.kv_index, bf16[2,512,512]{2,1,0:T(8,128)(2,1)} %hidden_ref.3, bf16[2,512,512]{2,1,0:T(8,128)(2,1)} %query_ref.1, bf16[2,512,512]{2,1,0:T(8,128)(2,1)} %grad_ref.1, bf16[2,512,1024]{2,1,0:T(8,128)(2,1)} %key_ref.1, ...), custom_call_target="tpu_custom_call" | custom-call | flops 5000000000 | bytes 8000000 | tf_op jit(solution)/shard_map/attention_backward/pallas_call | solution.py:298
  26.3 12.4 %all-to-all-start = ((bf16[16,2,32,512]{3,2,1,0:T(8,128)(2,1)}), bf16[16,2,32,512]{3,2,1,0:T(8,128)(2,1)S(1)}, u32[]{:S(2)}, u32[]{:S(2)}) async-start(bf16[16,2,32,512]{3,2,1,0:T(8,128)(2,1)} %get-tuple-element.22), calls=%async_computation | async-start | bytes 2097152 | tf_op jit(solution)/shard_map/all_to_all | solution.py:353
  38.8 3.9 %collective-permute-start.2 = (bf16[2,32,512]{2,1,0:T(8,128)(2,1)S(1)}, bf16[2,32,512]{2,1,0:T(8,128)(2,1)}, u32[]{:S(2)}, u32[]{:S(2)}) collective-permute-start(bf16[2,32,512]{2,1,0:T(8,128)(2,1)S(1)} %pad_maximum_fusion), channel_id=1, source_target_pairs={{0,128},{16,144},{32,160},{48,176},{64,192},{80,208},{96,224},{112... | collective-permute-start | bytes 196616 | tf_op jit(solution)/shard_map/ppermute | solution.py:283
  42.7 9.6 %collective-permute-done.2 = bf16[2,32,512]{2,1,0:T(8,128)(2,1)} collective-permute-done((bf16[2,32,512]{2,1,0:T(8,128)(2,1)S(1)}, bf16[2,32,512]{2,1,0:T(8,128)(2,1)}, u32[]{:S(2)}, u32[]{:S(2)}) %collective-permute-start.2) | collective-permute-done | bytes 65568 | tf_op jit(solution)/shard_map/ppermute | solution.py:283
  52.3 1.6 %all-to-all-done.parts_ref = bf16[16,2,32,512]{3,2,1,0:T(8,128)(2,1)S(1)} async-done(((bf16[16,2,32,512]{3,2,1,0:T(8,128)(2,1)}), bf16[16,2,32,512]{3,2,1,0:T(8,128)(2,1)S(1)}, u32[]{:S(2)}, u32[]{:S(2)}) %all-to-all-start) | async-done | bytes 1048608 | tf_op jit(solution)/shard_map/all_to_all | solution.py:353
  53.9 1.2 %lowrank_sum.1 = bf16[16,2,32,512]{3,2,1,0:T(8,128)(2,1)} custom-call(bf16[16,2,32,512]{3,2,1,0:T(8,128)(2,1)S(1)} %all-to-all-done.parts_ref), custom_call_target="tpu_custom_call" | custom-call | tf_op jit(solution)/shard_map/lowrank_sum/pallas_call | solution.py:357
  55.1 5.0 %all-to-all-start.1 = ((bf16[16,2,32,512]{3,2,1,0:T(8,128)(2,1)}), bf16[16,2,32,512]{3,2,1,0:T(8,128)(2,1)S(1)}, u32[]{:S(2)}, u32[]{:S(2)}) async-start(bf16[16,2,32,512]{3,2,1,0:T(8,128)(2,1)} %lowrank_sum.1), calls=%async_computation.1 | async-start | bytes 2097152 | tf_op jit(solution)/shard_map/all_to_all | solution.py:365
  60.1 0.8 constant_dynamic-update-slice_fusion.1
  60.9 0.8 constant_dynamic-update-slice_fusion.refs_0_
  61.8 3.7 %collective-permute-start.5 = (bf16[4,32,512]{2,1,0:T(8,128)(2,1)S(1)}, bf16[4,32,512]{2,1,0:T(8,128)(2,1)S(1)}, u32[]{:S(2)}, u32[]{:S(2)}) collective-permute-start(bf16[4,32,512]{2,1,0:T(8,128)(2,1)S(1)} %constant_dynamic-update-slice_fusion.refs_0_), channel_id=1, source_target_pairs={{0,16},{16,0},{32,48},{48,32},{64,80},{80,64},{96,112},{112,96},{1... | collective-permute-start | bytes 393224 | tf_op jit(solution)/shard_map/ppermute | solution.py:286
  65.5 2.5 %collective-permute-start.4 = (bf16[4,32,512]{2,1,0:T(8,128)(2,1)S(1)}, bf16[4,32,512]{2,1,0:T(8,128)(2,1)S(1)}, u32[]{:S(2)}, u32[]{:S(2)}) collective-permute-start(bf16[4,32,512]{2,1,0:T(8,128)(2,1)S(1)} %constant_dynamic-update-slice_fusion.refs_0_), channel_id=1, source_target_pairs={{0,32},{16,48},{32,0},{48,16},{64,96},{80,112},{96,64},{112,80},{1... | collective-permute-start | bytes 393224 | tf_op jit(solution)/shard_map/ppermute | solution.py:283
  68.0 1.9 %collective-permute-start.3 = (bf16[4,32,512]{2,1,0:T(8,128)(2,1)S(1)}, bf16[4,32,512]{2,1,0:T(8,128)(2,1)}, u32[]{:S(2)}, u32[]{:S(2)}) collective-permute-start(bf16[4,32,512]{2,1,0:T(8,128)(2,1)S(1)} %constant_dynamic-update-slice_fusion.refs_0_), channel_id=1, source_target_pairs={{0,64},{16,80},{32,96},{48,112},{64,0},{80,16},{96,32},{112,48},{1... | collective-permute-start | bytes 393224 | tf_op jit(solution)/shard_map/ppermute | solution.py:283
  69.9 0.7 copy-done.3
  70.6 1.9 %collective-permute-done.4.refs_2_ = bf16[4,32,512]{2,1,0:T(8,128)(2,1)S(1)} collective-permute-done((bf16[4,32,512]{2,1,0:T(8,128)(2,1)S(1)}, bf16[4,32,512]{2,1,0:T(8,128)(2,1)S(1)}, u32[]{:S(2)}, u32[]{:S(2)}) %collective-permute-start.4) | collective-permute-done | bytes 131104 | tf_op jit(solution)/shard_map/ppermute | solution.py:283
  72.5 0.7 copy-done.5
  73.2 5.4 %collective-permute-done.3.refs_1_ = bf16[4,32,512]{2,1,0:T(8,128)(2,1)} collective-permute-done((bf16[4,32,512]{2,1,0:T(8,128)(2,1)S(1)}, bf16[4,32,512]{2,1,0:T(8,128)(2,1)}, u32[]{:S(2)}, u32[]{:S(2)}) %collective-permute-start.3) | collective-permute-done | bytes 131104 | tf_op jit(solution)/shard_map/ppermute | solution.py:283
  78.6 0.9 copy-done.2
  79.5 0.7 copy-done.9
  80.2 0.7 copy-done.10
  80.9 2.7 %partial_features.1 = bf16[16,128,128]{2,1,0:T(8,128)(2,1)} custom-call(s32[1]{0:T(128)} %bitcast.2.kv_index, bf16[16,2,32,512]{3,2,1,0:T(8,128)(2,1)S(1)} %all-to-all-done.1.lowrank_ref, bf16[2,512,512]{2,1,0:T(8,128)(2,1)S(1)} %copy-done.1, bf16[2,640,512]{2,1,0:T(8,128)(2,1)S(1)} %copy-done, s32[3,512]{1,0:T(4,128)S(1)} %copy-done.7, ...), custom_call_target="tpu_custom_call" | custom-call | tf_op jit(solution)/shard_map/partial_features/pallas_call | solution.py:373
  83.6 6.9 %all-to-all-start.2 = ((bf16[16,128,128]{2,1,0:T(8,128)(2,1)}), bf16[16,128,128]{2,1,0:T(8,128)(2,1)S(1)}, u32[]{:S(2)}, u32[]{:S(2)}) async-start(bf16[16,128,128]{2,1,0:T(8,128)(2,1)} %partial_features.1), calls=%async_computation.2 | async-start | bytes 1048576 | tf_op jit(solution)/shard_map/all_to_all | solution.py:393
  90.5 1.9 %collective-permute-start.6 = (bf16[4,32,512]{2,1,0:T(8,128)(2,1)}, bf16[4,32,512]{2,1,0:T(8,128)(2,1)S(1)}, u32[]{:S(2)}, u32[]{:S(2)}) collective-permute-start(bf16[4,32,512]{2,1,0:T(8,128)(2,1)} %collective-permute-done.3.refs_1_), channel_id=1, source_target_pairs={{0,32},{16,48},{32,0},{48,16},{64,96},{80,112},{96,64},{112,80},{1... | collective-permute-start | bytes 393224 | tf_op jit(solution)/shard_map/ppermute | solution.py:283
  92.4 3.3 %collective-permute-start.7 = (bf16[4,32,512]{2,1,0:T(8,128)(2,1)}, bf16[4,32,512]{2,1,0:T(8,128)(2,1)S(1)}, u32[]{:S(2)}, u32[]{:S(2)}) collective-permute-start(bf16[4,32,512]{2,1,0:T(8,128)(2,1)} %collective-permute-done.3.refs_1_), channel_id=1, source_target_pairs={{0,16},{16,0},{32,48},{48,32},{64,80},{80,64},{96,112},{112,96},{1... | collective-permute-start | bytes 393224 | tf_op jit(solution)/shard_map/ppermute | solution.py:286
  95.6 1.9 %collective-permute-start.8 = (bf16[4,32,512]{2,1,0:T(8,128)(2,1)}, bf16[4,32,512]{2,1,0:T(8,128)(2,1)S(1)}, u32[]{:S(2)}, u32[]{:S(2)}) collective-permute-start(bf16[4,32,512]{2,1,0:T(8,128)(2,1)} %copy-done.5), channel_id=1, source_target_pairs={{0,16},{16,0},{32,48},{48,32},{64,80},{80,64},{96,112},{112,96},{1... | collective-permute-start | bytes 393224 | tf_op jit(solution)/shard_map/ppermute | solution.py:286
  97.6 3.2 %collective-permute-start.9 = (bf16[4,32,512]{2,1,0:T(8,128)(2,1)S(1)}, bf16[4,32,512]{2,1,0:T(8,128)(2,1)S(1)}, u32[]{:S(2)}, u32[]{:S(2)}) collective-permute-start(bf16[4,32,512]{2,1,0:T(8,128)(2,1)S(1)} %collective-permute-done.6.refs_3_), channel_id=1, source_target_pairs={{0,16},{16,0},{32,48},{48,32},{64,80},{80,64},{96,112},{112,96},{1... | collective-permute-start | bytes 393224 | tf_op jit(solution)/shard_map/ppermute | solution.py:286
  100.8 0.1 pad_add_fusion.place
  100.9 0.9 collective-permute-done.9.refs_7_
  101.8 0.9 copy-done.4
  102.7 0.9 copy-done.6
  103.6 2.1 %scores.1 = f32[2,64]{1,0:T(2,128)} custom-call(s32[2]{0:T(128)S(1)} %pad_add_fusion.place, bf16[16,128,128]{2,1,0:T(8,128)(2,1)S(1)} %all-to-all-done.2.parts_ref, bf16[4,32,512]{2,1,0:T(8,128)(2,1)S(1)} %constant_dynamic-update-slice_fusion.refs_0_, bf16[4,32,512]{2,1,0:T(8,128)(2,1)} %collective-permute-done.3.refs_1_, bf16[4,32,512]{2,1,0:T(8,128)(2,1)S(1)} %copy-done.6, ...), custom_call_target="tpu_custom_call" | custom-call | tf_op jit(solution)/shard_map/scores/pallas_call | solution.py:397
  (26 shorter events, 0.1 us)
Async XLA Ops:
  0.0 26.3 %collective-permute-start.1 = (bf16[32,512]{1,0:T(8,128)(2,1)}, bf16[32,512]{1,0:T(8,128)(2,1)S(1)}, u32[]{:S(2)}, u32[]{:S(2)}) collective-permute-start(bf16[32,512]{1,0:T(8,128)(2,1)} %param.31), channel_id=1, source_target_pairs={{0,256},{1,288},{2,320},{3,352},{4,384},{5,416},{6,448},{7,480},{8... | collective-permute-start | bytes 98312 | tf_op jit(solution)/shard_map/ppermute | solution.py:272
  16.3 10.0 %collective-permute-start = (bf16[32,512]{1,0:T(8,128)(2,1)}, bf16[32,512]{1,0:T(8,128)(2,1)S(1)}, u32[]{:S(2)}, u32[]{:S(2)}) collective-permute-start(bf16[32,512]{1,0:T(8,128)(2,1)} %param.31), channel_id=1, source_target_pairs={{0,0},{1,32},{2,64},{3,96},{4,128},{5,160},{6,192},{7,224},{8,256}... | collective-permute-start | bytes 98312 | tf_op jit(solution)/shard_map/ppermute | solution.py:272
  26.3 27.6 %all-to-all-start = ((bf16[16,2,32,512]{3,2,1,0:T(8,128)(2,1)}), bf16[16,2,32,512]{3,2,1,0:T(8,128)(2,1)S(1)}, u32[]{:S(2)}, u32[]{:S(2)}) async-start(bf16[16,2,32,512]{3,2,1,0:T(8,128)(2,1)} %get-tuple-element.22), calls=%async_computation | async-start | bytes 2097152 | tf_op jit(solution)/shard_map/all_to_all | solution.py:353
  38.7 3.9 %copy-start.11 = (bf16[2,32,512]{2,1,0:T(8,128)(2,1)}, bf16[2,32,512]{2,1,0:T(8,128)(2,1)S(1)}, u32[]{:S(2)}) copy-start(bf16[2,32,512]{2,1,0:T(8,128)(2,1)S(1)} %pad_maximum_fusion) | copy-start | bytes 196612
  38.7 39.8 %copy-start = (bf16[2,640,512]{2,1,0:T(8,128)(2,1)S(1)}, bf16[2,640,512]{2,1,0:T(8,128)(2,1)}, u32[]{:S(2)}) copy-start(bf16[2,640,512]{2,1,0:T(8,128)(2,1)} %get-tuple-element.29.head_grad_ref) | copy-start | bytes 3932164
  38.7 39.8 %copy-start.1 = (bf16[2,512,512]{2,1,0:T(8,128)(2,1)S(1)}, bf16[2,512,512]{2,1,0:T(8,128)(2,1)}, u32[]{:S(2)}) copy-start(bf16[2,512,512]{2,1,0:T(8,128)(2,1)} %hidden_ref.3) | copy-start | bytes 3145732
  38.8 39.8 %copy-start.7 = (s32[3,512]{1,0:T(4,128)S(1)}, s32[3,512]{1,0:T(4,128)}, u32[]{:S(2)}) copy-start(s32[3,512]{1,0:T(4,128)} %block_ref.1) | copy-start | bytes 18436
  38.8 39.8 %copy-start.8 = (s32[3,512]{1,0:T(4,128)S(1)}, s32[3,512]{1,0:T(4,128)}, u32[]{:S(2)}) copy-start(s32[3,512]{1,0:T(4,128)} %tile_ref.1) | copy-start | bytes 18436
  38.8 13.5 %collective-permute-start.2 = (bf16[2,32,512]{2,1,0:T(8,128)(2,1)S(1)}, bf16[2,32,512]{2,1,0:T(8,128)(2,1)}, u32[]{:S(2)}, u32[]{:S(2)}) collective-permute-start(bf16[2,32,512]{2,1,0:T(8,128)(2,1)S(1)} %pad_maximum_fusion), channel_id=1, source_target_pairs={{0,128},{16,144},{32,160},{48,176},{64,192},{80,208},{96,224},{112... | collective-permute-start | bytes 196616 | tf_op jit(solution)/shard_map/ppermute | solution.py:283
  55.1 23.4 %all-to-all-start.1 = ((bf16[16,2,32,512]{3,2,1,0:T(8,128)(2,1)}), bf16[16,2,32,512]{3,2,1,0:T(8,128)(2,1)S(1)}, u32[]{:S(2)}, u32[]{:S(2)}) async-start(bf16[16,2,32,512]{3,2,1,0:T(8,128)(2,1)} %lowrank_sum.1), calls=%async_computation.1 | async-start | bytes 2097152 | tf_op jit(solution)/shard_map/all_to_all | solution.py:365
  61.8 8.2 %collective-permute-start.5 = (bf16[4,32,512]{2,1,0:T(8,128)(2,1)S(1)}, bf16[4,32,512]{2,1,0:T(8,128)(2,1)S(1)}, u32[]{:S(2)}, u32[]{:S(2)}) collective-permute-start(bf16[4,32,512]{2,1,0:T(8,128)(2,1)S(1)} %constant_dynamic-update-slice_fusion.refs_0_), channel_id=1, source_target_pairs={{0,16},{16,0},{32,48},{48,32},{64,80},{80,64},{96,112},{112,96},{1... | collective-permute-start | bytes 393224 | tf_op jit(solution)/shard_map/ppermute | solution.py:286
  65.5 7.0 %collective-permute-start.4 = (bf16[4,32,512]{2,1,0:T(8,128)(2,1)S(1)}, bf16[4,32,512]{2,1,0:T(8,128)(2,1)S(1)}, u32[]{:S(2)}, u32[]{:S(2)}) collective-permute-start(bf16[4,32,512]{2,1,0:T(8,128)(2,1)S(1)} %constant_dynamic-update-slice_fusion.refs_0_), channel_id=1, source_target_pairs={{0,32},{16,48},{32,0},{48,16},{64,96},{80,112},{96,64},{112,80},{1... | collective-permute-start | bytes 393224 | tf_op jit(solution)/shard_map/ppermute | solution.py:283
  68.0 10.6 %collective-permute-start.3 = (bf16[4,32,512]{2,1,0:T(8,128)(2,1)S(1)}, bf16[4,32,512]{2,1,0:T(8,128)(2,1)}, u32[]{:S(2)}, u32[]{:S(2)}) collective-permute-start(bf16[4,32,512]{2,1,0:T(8,128)(2,1)S(1)} %constant_dynamic-update-slice_fusion.refs_0_), channel_id=1, source_target_pairs={{0,64},{16,80},{32,96},{48,112},{64,0},{80,16},{96,32},{112,48},{1... | collective-permute-start | bytes 393224 | tf_op jit(solution)/shard_map/ppermute | solution.py:283
  69.9 0.7 copy-start.3
  72.5 0.7 copy-start.5
  78.6 1.0 copy-start.2
  79.5 0.7 copy-start.9
  80.2 0.7 copy-start.10
  83.6 18.2 %all-to-all-start.2 = ((bf16[16,128,128]{2,1,0:T(8,128)(2,1)}), bf16[16,128,128]{2,1,0:T(8,128)(2,1)S(1)}, u32[]{:S(2)}, u32[]{:S(2)}) async-start(bf16[16,128,128]{2,1,0:T(8,128)(2,1)} %partial_features.1), calls=%async_computation.2 | async-start | bytes 1048576 | tf_op jit(solution)/shard_map/all_to_all | solution.py:393
  90.5 7.1 %collective-permute-start.6 = (bf16[4,32,512]{2,1,0:T(8,128)(2,1)}, bf16[4,32,512]{2,1,0:T(8,128)(2,1)S(1)}, u32[]{:S(2)}, u32[]{:S(2)}) collective-permute-start(bf16[4,32,512]{2,1,0:T(8,128)(2,1)} %collective-permute-done.3.refs_1_), channel_id=1, source_target_pairs={{0,32},{16,48},{32,0},{48,16},{64,96},{80,112},{96,64},{112,80},{1... | collective-permute-start | bytes 393224 | tf_op jit(solution)/shard_map/ppermute | solution.py:283
  92.4 8.5 %collective-permute-start.7 = (bf16[4,32,512]{2,1,0:T(8,128)(2,1)}, bf16[4,32,512]{2,1,0:T(8,128)(2,1)S(1)}, u32[]{:S(2)}, u32[]{:S(2)}) collective-permute-start(bf16[4,32,512]{2,1,0:T(8,128)(2,1)} %collective-permute-done.3.refs_1_), channel_id=1, source_target_pairs={{0,16},{16,0},{32,48},{48,32},{64,80},{80,64},{96,112},{112,96},{1... | collective-permute-start | bytes 393224 | tf_op jit(solution)/shard_map/ppermute | solution.py:286
  95.6 5.2 %collective-permute-start.8 = (bf16[4,32,512]{2,1,0:T(8,128)(2,1)}, bf16[4,32,512]{2,1,0:T(8,128)(2,1)S(1)}, u32[]{:S(2)}, u32[]{:S(2)}) collective-permute-start(bf16[4,32,512]{2,1,0:T(8,128)(2,1)} %copy-done.5), channel_id=1, source_target_pairs={{0,16},{16,0},{32,48},{48,32},{64,80},{80,64},{96,112},{112,96},{1... | collective-permute-start | bytes 393224 | tf_op jit(solution)/shard_map/ppermute | solution.py:286
  97.6 4.2 %collective-permute-start.9 = (bf16[4,32,512]{2,1,0:T(8,128)(2,1)S(1)}, bf16[4,32,512]{2,1,0:T(8,128)(2,1)S(1)}, u32[]{:S(2)}, u32[]{:S(2)}) collective-permute-start(bf16[4,32,512]{2,1,0:T(8,128)(2,1)S(1)} %collective-permute-done.6.refs_3_), channel_id=1, source_target_pairs={{0,16},{16,0},{32,48},{48,32},{64,80},{80,64},{96,112},{112,96},{1... | collective-permute-start | bytes 393224 | tf_op jit(solution)/shard_map/ppermute | solution.py:286
  101.7 0.9 copy-start.4
  102.7 0.9 copy-start.6

commit v7 on v6

--- a/solution.py
+++ b/solution.py
@@ -44,8 +44,13 @@
     down_value_ref,
     up_query_ref,
     up_value_ref,
+    block_ref,
+    tile_ref,
+    block_value_ref,
+    tile_value_ref,
+    bank_ref,
     send_ref,
-    head_grad_ref,
+    packed_ref,
     value_sum,
     down_t,
     bias_ref,
@@ -67,6 +72,20 @@
         down_t[:R] = down_query_ref[...].T
         down_t[R:] = down_value_ref[...].T
 
+    width = heads * DH
+    kv = kv_index[0]
+    for tile in range(bank_ref.shape[0]):
+        packed_ref[0, width + DH : width + 2 * DH, tile * PB : (tile + 1) * PB] = bank_ref[tile]
+    ids = [
+        block_ref[...],
+        jnp.concatenate([block_value_ref[pl.ds(kv, 1), :]] * heads, axis=1),
+        tile_ref[...],
+        jnp.concatenate([tile_value_ref[pl.ds(kv, 1), :]] * heads, axis=1),
+        jnp.zeros((8, width), jnp.int32),
+    ]
+    ids = jnp.concatenate(ids, axis=0).astype(F32).astype(BF16)
+    packed_ref[0, width + 2 * DH :] = ids
+
     lowrank_in = dot_nt(down_t[...], hidden_ref[0])
     send_ref[0 : 2 * quarter, 0] = lowrank_in.astype(BF16).reshape(2 * quarter, chunk, S)
 
@@ -79,8 +98,8 @@
         first = block * ROWS
         low = max(0, (first - LONGEST + 1) // ROWS * ROWS)
         high = first + ROWS
-        width = high - low
-        for at in range(0, width, ROWS):
+        reach = high - low
+        for at in range(0, reach, ROWS):
             allowed = segment_col[low + at : low + at + ROWS] == segment_row[:, first:high]
             if low + at == first:
                 key_pos = lax.broadcasted_iota(jnp.int32, (ROWS, ROWS), 0)
@@ -91,7 +110,7 @@
         first = block * ROWS
         low = max(0, (first - LONGEST + 1) // ROWS * ROWS)
         high = first + ROWS
-        width = high - low
+        reach = high - low
         slot = block % 2
 
         def stacked(ref):
@@ -100,8 +119,8 @@
             )
 
         grad = stacked(grad_ref)
-        logit_ref[slot, :width] = dot_nt(key_ref[0, low:high], stacked(query_ref))
-        prob_grad_ref[slot, :width] = dot_nt(value_ref[0, low:high], grad)
+        logit_ref[slot, :reach] = dot_nt(key_ref[0, low:high], stacked(query_ref))
+        prob_grad_ref[slot, :reach] = dot_nt(value_ref[0, low:high], grad)
 
         def logits(at):
             bias = bias_ref[block, at : at + CHUNK]
@@ -109,12 +128,12 @@
 
         lanes = heads * ROWS
         top = jnp.full((8, lanes), -3e38, F32)
-        for at in range(0, width, CHUNK):
+        for at in range(0, reach, CHUNK):
             top = jnp.maximum(top, jnp.max(logits(at).reshape(CHUNK // 8, 8, lanes), axis=0))
         row_top = jnp.max(top, axis=0, keepdims=True)
         total = jnp.zeros((8, lanes), F32)
         delta = jnp.zeros((8, lanes), F32)
-        for at in range(0, width, CHUNK):
+        for at in range(0, reach, CHUNK):
             terms = jnp.exp2((logits(at) - row_top) * exp_scale)
             total = total + jnp.sum(terms.reshape(CHUNK // 8, 8, lanes), axis=0)
             weighted = terms * prob_grad_ref[slot, at : at + CHUNK]
@@ -122,23 +141,23 @@
             logit_ref[slot, at : at + CHUNK] = terms
         inverse = 1.0 / jnp.sum(total, axis=0, keepdims=True)
         row_delta = jnp.sum(delta, axis=0, keepdims=True) * inverse
-        for at in range(0, width, CHUNK):
+        for at in range(0, reach, CHUNK):
             probs = logit_ref[slot, at : at + CHUNK] * inverse
             prob_ref[slot, at : at + CHUNK] = probs.astype(BF16)
             logit_grad_ref[slot, at : at + CHUNK] = (
                 probs * (prob_grad_ref[slot, at : at + CHUNK] - row_delta)
             ).astype(BF16)
-        value_sum[low:high] += dot_nn(prob_ref[slot, :width], grad)
-        query_grad = dot_nn(key_t[:, low:high], logit_grad_ref[slot, :width]) * score_scale
+        value_sum[low:high] += dot_nn(prob_ref[slot, :reach], grad)
+        query_grad = dot_nn(key_t[:, low:high], logit_grad_ref[slot, :reach]) * score_scale
         query_grad = query_grad.astype(BF16)
         for h in range(heads):
-            head_grad_ref[0, h * DH : (h + 1) * DH, first:high] = query_grad[
+            packed_ref[0, h * DH : (h + 1) * DH, first:high] = query_grad[
                 :, h * ROWS : (h + 1) * ROWS
             ]
 
     value_grad = value_sum[...].T.astype(BF16)
-    head_grad_ref[0, heads * DH :] = value_grad
-    back_query = dot_nn(up_query_ref[...], head_grad_ref[0, : heads * DH])
+    packed_ref[0, width : width + DH] = value_grad
+    back_query = dot_nn(up_query_ref[...], packed_ref[0, :width])
     back_value = dot_nn(up_value_ref[...], value_grad)
     send_ref[2 * quarter : 3 * quarter, 0] = back_query.astype(BF16).reshape(quarter, chunk, S)
     send_ref[3 * quarter : parts, 0] = back_value.astype(BF16).reshape(quarter, chunk, S)
@@ -149,43 +168,28 @@
     out_ref[...] = jnp.broadcast_to(total.astype(BF16)[None], out_ref.shape)
 
 
-def feature_kernel(
-    kv_index,
-    lowrank_ref,
-    hidden_ref,
-    head_grad_ref,
-    block_ref,
-    tile_ref,
-    block_value_ref,
-    tile_value_ref,
-    bank_hbm,
-    out_ref,
-    bank_ref,
-    bank_sem,
-):
-    bank_copy = pltpu.make_async_copy(bank_hbm, bank_ref, bank_sem)
-    bank_copy.start()
+def feature_kernel(lowrank_ref, hidden_ref, packed_ref, out_ref):
     cands = hidden_ref.shape[0]
-    width = head_grad_ref.shape[1] - DH
-    kv = kv_index[0]
+    width = hidden_ref.shape[2]
+    values = slice(width, width + DH)
+    tile_rows = slice(width + DH, width + 2 * DH)
     pieces = [[], [], [], []]
     for cand in range(cands):
         lowrank = lowrank_ref[:, cand].reshape(4 * R, S)
         down = dot_nn(lowrank[2 * R :], hidden_ref[cand])
         pieces[0].append(down[:R])
         pieces[1].append(down[R:])
-        pieces[2].append(dot_nt(lowrank[:R], head_grad_ref[cand, :width]))
-        pieces[3].append(dot_nt(lowrank[R : 2 * R], head_grad_ref[cand, width:]))
+        pieces[2].append(dot_nt(lowrank[:R], packed_ref[cand, :width]))
+        pieces[3].append(dot_nt(lowrank[R : 2 * R], packed_ref[cand, values]))
     buckets = KB * NT
+    ids = packed_ref[0, width + 2 * DH :].astype(F32)
+    ids = (ids[4:8] * KB + ids[0:4]).astype(jnp.int32)
     sums = jnp.zeros((buckets, cands * R), F32)
     for kind in range(4):
-        if kind < 3:
-            ids = tile_ref[kind : kind + 1, :] * KB + block_ref[kind : kind + 1, :]
-        else:
-            ids = tile_value_ref[pl.ds(kv, 1), :] * KB + block_value_ref[pl.ds(kv, 1), :]
         rows = jnp.concatenate(pieces[kind], axis=0).astype(BF16)
-        where = lax.broadcasted_iota(jnp.int32, (buckets, rows.shape[1]), 0)
-        chosen = jnp.where(where == ids, 1.0, 0.0).astype(BF16)
+        count = rows.shape[1]
+        where = lax.broadcasted_iota(jnp.int32, (buckets, count), 0)
+        chosen = jnp.where(where == ids[kind : kind + 1, :count], 1.0, 0.0).astype(BF16)
         sums = sums + dot_nt(chosen, rows)
     wide = jnp.concatenate(
         [
@@ -198,27 +202,34 @@
     )
     high = wide.astype(BF16)
     low = (wide - high.astype(F32)).astype(BF16)
-    bank_copy.wait()
-    bank = bank_ref[...].reshape(NT * R, PB)
+    tiles = NT // cands
+    bank = jnp.concatenate(
+        [
+            packed_ref[c, tile_rows, t * PB : (t + 1) * PB]
+            for c in range(cands)
+            for t in range(tiles)
+        ],
+        axis=0,
+    )
     feats = dot_nn(high, bank) + dot_nn(low, bank)
     out_ref[...] = jnp.broadcast_to(feats.astype(BF16)[None], out_ref.shape)
 
 
 def score_kernel(place, parts_ref, *refs):
-    mine_refs, other_refs, (out_ref, feats_ref) = refs[:4], refs[4:8], refs[8:]
+    mine_refs, other_refs, (out_ref, feats_ref) = refs[:2], refs[2:4], refs[4:]
     cands = out_ref.shape[0]
-    fours, seeds, depth = mine_refs[0].shape
+    eights, seeds, depth = mine_refs[0].shape
     per_part = depth // PB
     feats_ref[...] = jnp.sum(parts_ref[...].astype(F32), axis=0)
     totals = [[jnp.zeros((seeds, PB), F32) for _ in range(2)] for _ in range(cands)]
-    for at in range(4 * fours):
+    for at in range(2 * eights):
         source = place[1] ^ (at % 2 * 8 + at // 2 % 2 * 4 + at // 4 % 2 * 2 + at // 8)
         for part in range(per_part):
             feat = [
                 feats_ref[pl.ds(c * KB + source * per_part + part, 1), :] for c in range(cands)
             ]
-            for half, seeds_ref in enumerate((mine_refs[at // fours], other_refs[at // fours])):
-                seed = seeds_ref[at % fours, :, part * PB : (part + 1) * PB].astype(F32)
+            for half, seeds_ref in enumerate((mine_refs[at // eights], other_refs[at // eights])):
+                seed = seeds_ref[at % eights, :, part * PB : (part + 1) * PB].astype(F32)
                 for c in range(cands):
                     totals[c][half] = totals[c][half] + feat[c] * seed
     first_core = place[0] == 0
@@ -235,7 +246,7 @@
 
 VMEM = pl.BlockSpec(memory_space=pltpu.VMEM)
 SMEM = pl.BlockSpec(memory_space=pltpu.SMEM)
-PARAMS = pltpu.CompilerParams(vmem_limit_bytes=24 << 20)
+PARAMS = pltpu.CompilerParams(vmem_limit_bytes=40 << 20)
 
 
 def local(
@@ -288,6 +299,8 @@
     seed_near, seed_far = to_column(0), to_column(levels // 2)
     chunk = 4 * R // model_size
     span = LONGEST + ROWS
+    packed_rows = width + 2 * DH + 16
+    tiles = NT // cands
 
     def per_cand(*shape):
         return pl.BlockSpec((1, *shape), lambda c, kv_ref: (c, 0, 0))
@@ -295,12 +308,12 @@
     def whole(*shape):
         return pl.BlockSpec(shape, lambda c, kv_ref: (0,) * len(shape))
 
-    send, head_grad = pl.pallas_call(
+    send, packed = pl.pallas_call(
         attention_kernel,
         name="attention_backward",
         out_shape=(
             jax.ShapeDtypeStruct((model_size, cands, chunk, seq_len), BF16),
-            jax.ShapeDtypeStruct((cands, width + DH, seq_len), BF16),
+            jax.ShapeDtypeStruct((cands, packed_rows, seq_len), BF16),
         ),
         grid_spec=pltpu.PrefetchScalarGridSpec(
             num_scalar_prefetch=1,
@@ -316,10 +329,15 @@
                 whole(*down_value.shape),
                 whole(*up_query.shape),
                 pl.BlockSpec((R, DH), lambda c, kv_ref: (0, kv_ref[0])),
+                whole(*block_rows.shape),
+                whole(*tile_rows.shape),
+                whole(KVH, DH),
+                whole(KVH, DH),
+                pl.BlockSpec((tiles, R, PB), lambda c, kv_ref: (c, 0, 0)),
             ],
             out_specs=[
                 pl.BlockSpec((model_size, 1, chunk, seq_len), lambda c, kv_ref: (0, c, 0, 0)),
-                per_cand(width + DH, seq_len),
+                per_cand(packed_rows, seq_len),
             ],
             scratch_shapes=[
                 pltpu.VMEM((seq_len, DH), F32),
@@ -347,6 +365,11 @@
         down_value,
         up_query,
         up_value,
+        block_rows,
+        tile_rows,
+        block_value.reshape(KVH, DH),
+        tile_value.reshape(KVH, DH),
+        tile_bank,
     )
 
     send, seed_near, seed_far = lax.optimization_barrier((send, seed_near, seed_far))
@@ -364,45 +387,33 @@
     )(received)
     lowrank = lax.all_to_all(summed, "mp", 0, 0, tiled=True)
     four = jnp.concatenate([two, two_more])
-    fours = [four, from_level(four, 2), from_level(four, 1)]
-    others = [from_core(four)]
-    lowrank, *both = lax.optimization_barrier((lowrank, *fours, *others))
-    fours, others = both[:3], both[3:]
-    fours.append(from_level(fours[1], 1))
+    four_more = from_level(four, 2)
+    lowrank, four, four_more = lax.optimization_barrier((lowrank, four, four_more))
+    eight = jnp.concatenate([four, four_more])
+    eight_more = from_level(eight, 1)
 
     feat_parts = pl.pallas_call(
         feature_kernel,
         name="partial_features",
         out_shape=jax.ShapeDtypeStruct((model_size, cands * KB, PB), BF16),
-        in_specs=[SMEM] + [VMEM] * 7 + [pl.BlockSpec(memory_space=pltpu.HBM)],
+        in_specs=[VMEM] * 3,
         out_specs=VMEM,
-        scratch_shapes=[pltpu.VMEM(tile_bank.shape, BF16), pltpu.SemaphoreType.DMA],
         compiler_params=PARAMS,
-    )(
-        kv_index,
-        lowrank,
-        hidden_in,
-        head_grad,
-        block_rows,
-        tile_rows,
-        block_value.reshape(KVH, DH),
-        tile_value.reshape(KVH, DH),
-        tile_bank,
-    )
-    feat_parts, *fours[1:3] = lax.optimization_barrier((feat_parts, *fours[1:3]))
+    )(lowrank, hidden_in, packed)
+    feat_parts, eight = lax.optimization_barrier((feat_parts, eight))
     feat_all = lax.all_to_all(feat_parts, "mp", 0, 0, tiled=True)
-    others += [from_core(part) for part in fours[1:]]
+    other = [from_core(part) for part in (eight, eight_more)]
     place = jnp.stack([lax.axis_index("dp") % 2, lax.axis_index("dp") // 2]).astype(jnp.int32)
 
     return pl.pallas_call(
         score_kernel,
         name="scores",
         out_shape=jax.ShapeDtypeStruct((cands, out_seeds), F32),
-        in_specs=[SMEM] + [VMEM] * 9,
+        in_specs=[SMEM] + [VMEM] * 5,
         out_specs=VMEM,
         scratch_shapes=[pltpu.VMEM((cands * KB, PB), F32)],
         compiler_params=PARAMS,
-    )(place, feat_all, *fours, *others)
+    )(place, feat_all, eight, eight_more, *other)
 
 
 def solution(mesh):

time: 107 us -> 98.5 us (0.921)
  the two profiles are of different devices: /device:TPU:1 before, /device:TPU:32 now
where the time goes in v7:
time: 98.5 us; the launch traced here: 97.9 us
  starting transfers between devices  50.7 us (51%)
  waiting for transfers between devices  31.5 us (32%)
  Pallas kernels  14.2 us (14%)
  local copies, waits for them, and re-layouts  1.26 us (1%)
    ppermute x2, starting transfers between devices, to_column(): lax.ppermute(seed_feats, ('dp', 'mp'), [(d * model_size + m, ((m ^ flip)...  18.2 us
    ppermute x3, waiting for transfers between devices, from_level(): lax.ppermute(block, 'dp', [(d, d ^ 2 * flip) for d in range(data_size)])  12.4 us
    all_to_all x1, starting transfers between devices, local(): received = lax.all_to_all(send, 'mp', 0, 0, tiled=True)  10.8 us
    ppermute x3, starting transfers between devices, from_level(): lax.ppermute(block, 'dp', [(d, d ^ 2 * flip) for d in range(data_size)])  10.1 us
    pallas_call x1, Pallas kernels, local(): pl.pallas_call(attention_kernel, name='attention_backward', out_shape=(ja...  8.77 us
    all_to_all x1, waiting for transfers between devices, local(): lowrank = lax.all_to_all(summed, 'mp', 0, 0, tiled=True)  7.36 us
    all_to_all x1, waiting for transfers between devices, local(): received = lax.all_to_all(send, 'mp', 0, 0, tiled=True)  6.04 us
    all_to_all x1, waiting for transfers between devices, local(): feat_all = lax.all_to_all(feat_parts, 'mp', 0, 0, tiled=True)  5.64 us
  transfers between devices with their start and end apart: 10, of which 5 were waited for; matrix products, arithmetic and copies ran while one was open for 0% of the time, Pallas kernels for 11%

profile of v7, /device:TPU:32, one launch (start us, length us, event | category | flops | bytes accessed | tf_op | source)
XLA Modules:
  0.0 97.9 jit_solution(14246402792069449917)
XLA Ops:
  0.0 15.4 %collective-permute-start.1 = (bf16[32,512]{1,0:T(8,128)(2,1)}, bf16[32,512]{1,0:T(8,128)(2,1)S(1)}, u32[]{:S(2)}, u32[]{:S(2)}) collective-permute-start(bf16[32,512]{1,0:T(8,128)(2,1)} %param.31), channel_id=1, source_target_pairs={{0,256},{1,288},{2,320},{3,352},{4,384},{5,416},{6,448},{7,480},{8... | collective-permute-start | bytes 98312 | tf_op jit(solution)/shard_map/ppermute | solution.py:283
  15.4 2.8 %collective-permute-start = (bf16[32,512]{1,0:T(8,128)(2,1)}, bf16[32,512]{1,0:T(8,128)(2,1)S(1)}, u32[]{:S(2)}, u32[]{:S(2)}) collective-permute-start(bf16[32,512]{1,0:T(8,128)(2,1)} %param.31), channel_id=1, source_target_pairs={{0,0},{1,32},{2,64},{3,96},{4,128},{5,160},{6,192},{7,224},{8,256}... | collective-permute-start | bytes 98312 | tf_op jit(solution)/shard_map/ppermute | solution.py:283
  18.2 8.8 %attention_backward.1 = (bf16[16,2,32,512]{3,2,1,0:T(8,128)(2,1)}, bf16[2,784,512]{2,1,0:T(8,128)(2,1)}) custom-call(s32[1]{0:T(128)} %bitcast.2.kv_index, bf16[2,512,512]{2,1,0:T(8,128)(2,1)} %hidden_ref.3, bf16[2,512,512]{2,1,0:T(8,128)(2,1)} %query_ref.1, bf16[2,512,512]{2,1,0:T(8,128)(2,1)} %grad_ref.1, bf16[2,512,1024]{2,1,0:T(8,128)(2,1)} %key_ref.1, ...), custom_call_target="tpu_custom_call" | custom-call | flops 5000000000 | bytes 8000000 | tf_op jit(solution)/shard_map/attention_backward/pallas_call | solution.py:311
  27.0 0.0 collective-permute-done.1
  27.0 0.0 collective-permute-done
  27.0 10.8 %all-to-all-start = ((bf16[16,2,32,512]{3,2,1,0:T(8,128)(2,1)}), bf16[16,2,32,512]{3,2,1,0:T(8,128)(2,1)S(1)}, u32[]{:S(2)}, u32[]{:S(2)}) async-start(bf16[16,2,32,512]{3,2,1,0:T(8,128)(2,1)} %get-tuple-element.19), calls=%async_computation | async-start | bytes 2097152 | tf_op jit(solution)/shard_map/all_to_all | solution.py:376
  37.8 0.0 copy-start
  37.8 4.2 %collective-permute-start.2 = (bf16[2,32,512]{2,1,0:T(8,128)(2,1)S(1)}, bf16[2,32,512]{2,1,0:T(8,128)(2,1)S(1)}, u32[]{:S(2)}, u32[]{:S(2)}) collective-permute-start(bf16[2,32,512]{2,1,0:T(8,128)(2,1)S(1)} %pad_maximum_fusion), channel_id=1, source_target_pairs={{0,128},{16,144},{32,160},{48,176},{64,192},{80,208},{96,224},{112... | collective-permute-start | bytes 196616 | tf_op jit(solution)/shard_map/ppermute | solution.py:294
  42.0 6.6 %collective-permute-done.2 = bf16[2,32,512]{2,1,0:T(8,128)(2,1)S(1)} collective-permute-done((bf16[2,32,512]{2,1,0:T(8,128)(2,1)S(1)}, bf16[2,32,512]{2,1,0:T(8,128)(2,1)S(1)}, u32[]{:S(2)}, u32[]{:S(2)}) %collective-permute-start.2) | collective-permute-done | bytes 65568 | tf_op jit(solution)/shard_map/ppermute | solution.py:294
  48.6 6.0 %all-to-all-done.parts_ref = bf16[16,2,32,512]{3,2,1,0:T(8,128)(2,1)S(1)} async-done(((bf16[16,2,32,512]{3,2,1,0:T(8,128)(2,1)}), bf16[16,2,32,512]{3,2,1,0:T(8,128)(2,1)S(1)}, u32[]{:S(2)}, u32[]{:S(2)}) %all-to-all-start) | async-done | bytes 1048608 | tf_op jit(solution)/shard_map/all_to_all | solution.py:376
  54.6 1.2 %lowrank_sum.1 = bf16[16,2,32,512]{3,2,1,0:T(8,128)(2,1)} custom-call(bf16[16,2,32,512]{3,2,1,0:T(8,128)(2,1)S(1)} %all-to-all-done.parts_ref), custom_call_target="tpu_custom_call" | custom-call | tf_op jit(solution)/shard_map/lowrank_sum/pallas_call | solution.py:380
  55.8 3.7 %all-to-all-start.1 = ((bf16[16,2,32,512]{3,2,1,0:T(8,128)(2,1)}), bf16[16,2,32,512]{3,2,1,0:T(8,128)(2,1)S(1)}, u32[]{:S(2)}, u32[]{:S(2)}) async-start(bf16[16,2,32,512]{3,2,1,0:T(8,128)(2,1)} %lowrank_sum.1), calls=%async_computation.1 | async-start | bytes 2097152 | tf_op jit(solution)/shard_map/all_to_all | solution.py:388
  59.5 2.1 %collective-permute-start.3 = (bf16[4,32,512]{2,1,0:T(8,128)(2,1)S(1)}, bf16[4,32,512]{2,1,0:T(8,128)(2,1)S(1)}, u32[]{:S(2)}, u32[]{:S(2)}) collective-permute-start(bf16[4,32,512]{2,1,0:T(8,128)(2,1)S(1)} %constant_dynamic-update-slice_fusion), channel_id=1, source_target_pairs={{0,64},{16,80},{32,96},{48,112},{64,0},{80,16},{96,32},{112,48},{1... | collective-permute-start | bytes 393224 | tf_op jit(solution)/shard_map/ppermute | solution.py:294
  61.6 5.8 %collective-permute-done.3 = bf16[4,32,512]{2,1,0:T(8,128)(2,1)S(1)} collective-permute-done((bf16[4,32,512]{2,1,0:T(8,128)(2,1)S(1)}, bf16[4,32,512]{2,1,0:T(8,128)(2,1)S(1)}, u32[]{:S(2)}, u32[]{:S(2)}) %collective-permute-start.3) | collective-permute-done | bytes 131104 | tf_op jit(solution)/shard_map/ppermute | solution.py:294
  67.4 7.4 %all-to-all-done.1.lowrank_ref = bf16[16,2,32,512]{3,2,1,0:T(8,128)(2,1)S(1)} async-done(((bf16[16,2,32,512]{3,2,1,0:T(8,128)(2,1)}), bf16[16,2,32,512]{3,2,1,0:T(8,128)(2,1)S(1)}, u32[]{:S(2)}, u32[]{:S(2)}) %all-to-all-start.1) | async-done | bytes 1048608 | tf_op jit(solution)/shard_map/all_to_all | solution.py:388
  74.8 3.9 %collective-permute-start.4 = (bf16[8,32,512]{2,1,0:T(8,128)(2,1)S(1)}, bf16[8,32,512]{2,1,0:T(8,128)(2,1)S(1)}, u32[]{:S(2)}, u32[]{:S(2)}) collective-permute-start(bf16[8,32,512]{2,1,0:T(8,128)(2,1)S(1)} %constant_dynamic-update-slice_fusion.2.refs_0_), channel_id=1, source_target_pairs={{0,32},{16,48},{32,0},{48,16},{64,96},{80,112},{96,64},{112,80},{1... | collective-permute-start | bytes 786440 | tf_op jit(solution)/shard_map/ppermute | solution.py:294
  78.7 0.0 copy-done
  78.7 0.0 copy-start.1
  78.7 1.2 %copy-done.1 = bf16[2,512,512]{2,1,0:T(8,128)(2,1)S(1)} copy-done((bf16[2,512,512]{2,1,0:T(8,128)(2,1)S(1)}, bf16[2,512,512]{2,1,0:T(8,128)(2,1)}, u32[]{:S(2)}) %copy-start.1) | copy-done | bytes 1048600
  79.9 2.5 %partial_features.1 = bf16[16,128,128]{2,1,0:T(8,128)(2,1)} custom-call(bf16[16,2,32,512]{3,2,1,0:T(8,128)(2,1)S(1)} %all-to-all-done.1.lowrank_ref, bf16[2,512,512]{2,1,0:T(8,128)(2,1)S(1)} %copy-done.1, bf16[2,784,512]{2,1,0:T(8,128)(2,1)S(1)} %copy-done), custom_call_target="tpu_custom_call" | custom-call | tf_op jit(solution)/shard_map/partial_features/pallas_call | solution.py:395
  82.4 3.6 %all-to-all-start.2 = ((bf16[16,128,128]{2,1,0:T(8,128)(2,1)}), bf16[16,128,128]{2,1,0:T(8,128)(2,1)S(1)}, u32[]{:S(2)}, u32[]{:S(2)}) async-start(bf16[16,128,128]{2,1,0:T(8,128)(2,1)} %partial_features.1), calls=%async_computation.2 | async-start | bytes 1048576 | tf_op jit(solution)/shard_map/all_to_all | solution.py:404
  86.0 1.9 %collective-permute-start.5 = (bf16[8,32,512]{2,1,0:T(8,128)(2,1)S(1)}, bf16[8,32,512]{2,1,0:T(8,128)(2,1)S(1)}, u32[]{:S(2)}, u32[]{:S(2)}) collective-permute-start(bf16[8,32,512]{2,1,0:T(8,128)(2,1)S(1)} %constant_dynamic-update-slice_fusion.2.refs_0_), channel_id=1, source_target_pairs={{0,16},{16,0},{32,48},{48,32},{64,80},{80,64},{96,112},{112,96},{1... | collective-permute-start | bytes 786440 | tf_op jit(solution)/shard_map/ppermute | solution.py:297
  87.9 0.0 collective-permute-done.4.refs_1_
  87.9 2.4 %collective-permute-start.6 = (bf16[8,32,512]{2,1,0:T(8,128)(2,1)S(1)}, bf16[8,32,512]{2,1,0:T(8,128)(2,1)S(1)}, u32[]{:S(2)}, u32[]{:S(2)}) collective-permute-start(bf16[8,32,512]{2,1,0:T(8,128)(2,1)S(1)} %collective-permute-done.4.refs_1_), channel_id=1, source_target_pairs={{0,16},{16,0},{32,48},{48,32},{64,80},{80,64},{96,112},{112,96},{1... | collective-permute-start | bytes 786440 | tf_op jit(solution)/shard_map/ppermute | solution.py:297
  90.4 0.1 pad_add_fusion.place
  90.4 0.0 collective-permute-done.5.refs_2_
  90.4 5.6 %all-to-all-done.2.parts_ref = bf16[16,128,128]{2,1,0:T(8,128)(2,1)S(1)} async-done(((bf16[16,128,128]{2,1,0:T(8,128)(2,1)}), bf16[16,128,128]{2,1,0:T(8,128)(2,1)S(1)}, u32[]{:S(2)}, u32[]{:S(2)}) %all-to-all-start.2) | async-done | bytes 524320 | tf_op jit(solution)/shard_map/all_to_all | solution.py:404
  96.1 0.0 collective-permute-done.6.refs_3_
  96.1 1.8 %scores.1 = f32[2,64]{1,0:T(2,128)} custom-call(s32[2]{0:T(128)S(1)} %pad_add_fusion.place, bf16[16,128,128]{2,1,0:T(8,128)(2,1)S(1)} %all-to-all-done.2.parts_ref, bf16[8,32,512]{2,1,0:T(8,128)(2,1)S(1)} %constant_dynamic-update-slice_fusion.2.refs_0_, bf16[8,32,512]{2,1,0:T(8,128)(2,1)S(1)} %collective-permute-done.4.refs_1_, ...), custom_call_target="tpu_custom_call" | custom-call | tf_op jit(solution)/shard_map/scores/pallas_call | solution.py:408
  (5 shorter events, 0.0 us)
Async XLA Ops:
  0.0 27.0 %collective-permute-start.1 = (bf16[32,512]{1,0:T(8,128)(2,1)}, bf16[32,512]{1,0:T(8,128)(2,1)S(1)}, u32[]{:S(2)}, u32[]{:S(2)}) collective-permute-start(bf16[32,512]{1,0:T(8,128)(2,1)} %param.31), channel_id=1, source_target_pairs={{0,256},{1,288},{2,320},{3,352},{4,384},{5,416},{6,448},{7,480},{8... | collective-permute-start | bytes 98312 | tf_op jit(solution)/shard_map/ppermute | solution.py:283
  15.4 11.6 %collective-permute-start = (bf16[32,512]{1,0:T(8,128)(2,1)}, bf16[32,512]{1,0:T(8,128)(2,1)S(1)}, u32[]{:S(2)}, u32[]{:S(2)}) collective-permute-start(bf16[32,512]{1,0:T(8,128)(2,1)} %param.31), channel_id=1, source_target_pairs={{0,0},{1,32},{2,64},{3,96},{4,128},{5,160},{6,192},{7,224},{8,256}... | collective-permute-start | bytes 98312 | tf_op jit(solution)/shard_map/ppermute | solution.py:283
  27.0 27.6 %all-to-all-start = ((bf16[16,2,32,512]{3,2,1,0:T(8,128)(2,1)}), bf16[16,2,32,512]{3,2,1,0:T(8,128)(2,1)S(1)}, u32[]{:S(2)}, u32[]{:S(2)}) async-start(bf16[16,2,32,512]{3,2,1,0:T(8,128)(2,1)} %get-tuple-element.19), calls=%async_computation | async-start | bytes 2097152 | tf_op jit(solution)/shard_map/all_to_all | solution.py:376
  37.8 40.9 %copy-start = (bf16[2,784,512]{2,1,0:T(8,128)(2,1)S(1)}, bf16[2,784,512]{2,1,0:T(8,128)(2,1)}, u32[]{:S(2)}) copy-start(bf16[2,784,512]{2,1,0:T(8,128)(2,1)} %get-tuple-element.26.packed_ref) | copy-start | bytes 4816900
  37.8 10.8 %collective-permute-start.2 = (bf16[2,32,512]{2,1,0:T(8,128)(2,1)S(1)}, bf16[2,32,512]{2,1,0:T(8,128)(2,1)S(1)}, u32[]{:S(2)}, u32[]{:S(2)}) collective-permute-start(bf16[2,32,512]{2,1,0:T(8,128)(2,1)S(1)} %pad_maximum_fusion), channel_id=1, source_target_pairs={{0,128},{16,144},{32,160},{48,176},{64,192},{80,208},{96,224},{112... | collective-permute-start | bytes 196616 | tf_op jit(solution)/shard_map/ppermute | solution.py:294
  55.8 18.9 %all-to-all-start.1 = ((bf16[16,2,32,512]{3,2,1,0:T(8,128)(2,1)}), bf16[16,2,32,512]{3,2,1,0:T(8,128)(2,1)S(1)}, u32[]{:S(2)}, u32[]{:S(2)}) async-start(bf16[16,2,32,512]{3,2,1,0:T(8,128)(2,1)} %lowrank_sum.1), calls=%async_computation.1 | async-start | bytes 2097152 | tf_op jit(solution)/shard_map/all_to_all | solution.py:388
  59.5 7.9 %collective-permute-start.3 = (bf16[4,32,512]{2,1,0:T(8,128)(2,1)S(1)}, bf16[4,32,512]{2,1,0:T(8,128)(2,1)S(1)}, u32[]{:S(2)}, u32[]{:S(2)}) collective-permute-start(bf16[4,32,512]{2,1,0:T(8,128)(2,1)S(1)} %constant_dynamic-update-slice_fusion), channel_id=1, source_target_pairs={{0,64},{16,80},{32,96},{48,112},{64,0},{80,16},{96,32},{112,48},{1... | collective-permute-start | bytes 393224 | tf_op jit(solution)/shard_map/ppermute | solution.py:294
  74.8 13.2 %collective-permute-start.4 = (bf16[8,32,512]{2,1,0:T(8,128)(2,1)S(1)}, bf16[8,32,512]{2,1,0:T(8,128)(2,1)S(1)}, u32[]{:S(2)}, u32[]{:S(2)}) collective-permute-start(bf16[8,32,512]{2,1,0:T(8,128)(2,1)S(1)} %constant_dynamic-update-slice_fusion.2.refs_0_), channel_id=1, source_target_pairs={{0,32},{16,48},{32,0},{48,16},{64,96},{80,112},{96,64},{112,80},{1... | collective-permute-start | bytes 786440 | tf_op jit(solution)/shard_map/ppermute | solution.py:294
  78.7 1.2 %copy-start.1 = (bf16[2,512,512]{2,1,0:T(8,128)(2,1)S(1)}, bf16[2,512,512]{2,1,0:T(8,128)(2,1)}, u32[]{:S(2)}) copy-start(bf16[2,512,512]{2,1,0:T(8,128)(2,1)} %hidden_ref.3) | copy-start | bytes 3145732
  82.4 13.7 %all-to-all-start.2 = ((bf16[16,128,128]{2,1,0:T(8,128)(2,1)}), bf16[16,128,128]{2,1,0:T(8,128)(2,1)S(1)}, u32[]{:S(2)}, u32[]{:S(2)}) async-start(bf16[16,128,128]{2,1,0:T(8,128)(2,1)} %partial_features.1), calls=%async_computation.2 | async-start | bytes 1048576 | tf_op jit(solution)/shard_map/all_to_all | solution.py:404
  86.0 4.5 %collective-permute-start.5 = (bf16[8,32,512]{2,1,0:T(8,128)(2,1)S(1)}, bf16[8,32,512]{2,1,0:T(8,128)(2,1)S(1)}, u32[]{:S(2)}, u32[]{:S(2)}) collective-permute-start(bf16[8,32,512]{2,1,0:T(8,128)(2,1)S(1)} %constant_dynamic-update-slice_fusion.2.refs_0_), channel_id=1, source_target_pairs={{0,16},{16,0},{32,48},{48,32},{64,80},{80,64},{96,112},{112,96},{1... | collective-permute-start | bytes 786440 | tf_op jit(solution)/shard_map/ppermute | solution.py:297
  87.9 8.2 %collective-permute-start.6 = (bf16[8,32,512]{2,1,0:T(8,128)(2,1)S(1)}, bf16[8,32,512]{2,1,0:T(8,128)(2,1)S(1)}, u32[]{:S(2)}, u32[]{:S(2)}) collective-permute-start(bf16[8,32,512]{2,1,0:T(8,128)(2,1)S(1)} %collective-permute-done.4.refs_1_), channel_id=1, source_target_pairs={{0,16},{16,0},{32,48},{48,32},{64,80},{80,64},{96,112},{112,96},{1... | collective-permute-start | bytes 786440 | tf_op jit(solution)/shard_map/ppermute | solution.py:297

commit v8 on v7

--- a/solution.py
+++ b/solution.py
@@ -279,9 +279,9 @@
 
     levels = data_size // 2
 
-    def to_column(flip):
+    def to_column(block, flip):
         return lax.ppermute(
-            seed_feats,
+            block,
             ("dp", "mp"),
             [
                 (d * model_size + m, ((m ^ flip) * 2 + d % 2) * model_size + d // 2)
@@ -296,7 +296,6 @@
     def from_core(block):
         return lax.ppermute(block, "dp", [(d, d ^ 1) for d in range(data_size)])
 
-    seed_near, seed_far = to_column(0), to_column(levels // 2)
     chunk = 4 * R // model_size
     span = LONGEST + ROWS
     packed_rows = width + 2 * DH + 16
@@ -372,11 +371,11 @@
         tile_bank,
     )
 
-    send, seed_near, seed_far = lax.optimization_barrier((send, seed_near, seed_far))
+    send, seeds_own = lax.optimization_barrier((send, seed_feats))
     received = lax.all_to_all(send, "mp", 0, 0, tiled=True)
-    two = jnp.stack([seed_near, seed_far])
-    two_more = from_level(two, 4)
-    received, two, two_more = lax.optimization_barrier((received, two, two_more))
+    half, quarter = levels // 2, levels // 4
+    moved = [to_column(seeds_own, flip) for flip in (0, half, quarter, half + quarter)]
+    received, *moved = lax.optimization_barrier((received, *moved))
     summed = pl.pallas_call(
         sum_kernel,
         name="lowrank_sum",
@@ -386,7 +385,7 @@
         compiler_params=PARAMS,
     )(received)
     lowrank = lax.all_to_all(summed, "mp", 0, 0, tiled=True)
-    four = jnp.concatenate([two, two_more])
+    four = jnp.stack(moved)
     four_more = from_level(four, 2)
     lowrank, four, four_more = lax.optimization_barrier((lowrank, four, four_more))
     eight = jnp.concatenate([four, four_more])

time: 98.5 us -> 105 us (1.066)
  the two profiles are of different devices: /device:TPU:32 before, /device:TPU:64 now
where the time goes in v8:
time: 105 us; the launch traced here: 104 us
  starting transfers between devices  65.1 us (62%)
  waiting for transfers between devices  23.1 us (22%)
  Pallas kernels  14.2 us (14%)
  local copies, waits for them, and re-layouts  1.25 us (1%)
    ppermute x4, starting transfers between devices, to_column(): lax.ppermute(block, ('dp', 'mp'), [(d * model_size + m, ((m ^ flip) * 2 +...  30.9 us
    all_to_all x1, starting transfers between devices, local(): lowrank = lax.all_to_all(summed, 'mp', 0, 0, tiled=True)  14.4 us
    pallas_call x1, Pallas kernels, local(): pl.pallas_call(attention_kernel, name='attention_backward', out_shape=(ja...  8.74 us
    all_to_all x1, waiting for transfers between devices, local(): lowrank = lax.all_to_all(summed, 'mp', 0, 0, tiled=True)  7.19 us
    all_to_all x1, starting transfers between devices, local(): received = lax.all_to_all(send, 'mp', 0, 0, tiled=True)  7.05 us
    ppermute x2, waiting for transfers between devices, from_level(): lax.ppermute(block, 'dp', [(d, d ^ 2 * flip) for d in range(data_size)])  5.94 us
    all_to_all x1, waiting for transfers between devices, local(): feat_all = lax.all_to_all(feat_parts, 'mp', 0, 0, tiled=True)  5.61 us
    ppermute x2, starting transfers between devices, from_level(): lax.ppermute(block, 'dp', [(d, d ^ 2 * flip) for d in range(data_size)])  4.84 us
  transfers between devices with their start and end apart: 11, of which 5 were waited for; matrix products, arithmetic and copies ran while one was open for 0% of the time, Pallas kernels for 2%

profile of v8, /device:TPU:64, one launch (start us, length us, event | category | flops | bytes accessed | tf_op | source)
XLA Modules:
  0.0 104.0 jit_solution(15799581822433716109)
XLA Ops:
  0.0 8.7 %attention_backward.1 = (bf16[16,2,32,512]{3,2,1,0:T(8,128)(2,1)}, bf16[2,784,512]{2,1,0:T(8,128)(2,1)}) custom-call(s32[1]{0:T(128)} %bitcast.2.kv_index, bf16[2,512,512]{2,1,0:T(8,128)(2,1)} %hidden_ref.3, bf16[2,512,512]{2,1,0:T(8,128)(2,1)} %query_ref.1, bf16[2,512,512]{2,1,0:T(8,128)(2,1)} %grad_ref.1, bf16[2,512,1024]{2,1,0:T(8,128)(2,1)} %key_ref.1, ...), custom_call_target="tpu_custom_call" | custom-call | flops 5000000000 | bytes 8000000 | tf_op jit(solution)/shard_map/attention_backward/pallas_call | solution.py:310
  8.7 0.0 copy-start.2
  8.8 7.1 %all-to-all-start = ((bf16[16,2,32,512]{3,2,1,0:T(8,128)(2,1)}), bf16[16,2,32,512]{3,2,1,0:T(8,128)(2,1)S(1)}, u32[]{:S(2)}, u32[]{:S(2)}) async-start(bf16[16,2,32,512]{3,2,1,0:T(8,128)(2,1)} %get-tuple-element.20), calls=%async_computation | async-start | bytes 2097152 | tf_op jit(solution)/shard_map/all_to_all | solution.py:375
  15.8 0.0 copy-done.2
  15.8 0.0 copy-start
  15.8 14.8 %collective-permute-start.3 = (bf16[32,512]{1,0:T(8,128)(2,1)S(1)}, bf16[32,512]{1,0:T(8,128)(2,1)S(1)}, u32[]{:S(2)}, u32[]{:S(2)}) collective-permute-start(bf16[32,512]{1,0:T(8,128)(2,1)S(1)} %copy-done.2), channel_id=1, source_target_pairs={{0,384},{1,416},{2,448},{3,480},{4,256},{5,288},{6,320},{7,352},{8... | collective-permute-start | bytes 98312 | tf_op jit(solution)/shard_map/ppermute | solution.py:283
  30.7 5.5 %collective-permute-start.2 = (bf16[32,512]{1,0:T(8,128)(2,1)S(1)}, bf16[32,512]{1,0:T(8,128)(2,1)S(1)}, u32[]{:S(2)}, u32[]{:S(2)}) collective-permute-start(bf16[32,512]{1,0:T(8,128)(2,1)S(1)} %copy-done.2), channel_id=1, source_target_pairs={{0,128},{1,160},{2,192},{3,224},{4,0},{5,32},{6,64},{7,96},{8,384}... | collective-permute-start | bytes 98312 | tf_op jit(solution)/shard_map/ppermute | solution.py:283
  36.2 5.2 %collective-permute-start.1 = (bf16[32,512]{1,0:T(8,128)(2,1)S(1)}, bf16[32,512]{1,0:T(8,128)(2,1)S(1)}, u32[]{:S(2)}, u32[]{:S(2)}) collective-permute-start(bf16[32,512]{1,0:T(8,128)(2,1)S(1)} %copy-done.2), channel_id=1, source_target_pairs={{0,256},{1,288},{2,320},{3,352},{4,384},{5,416},{6,448},{7,480},{8... | collective-permute-start | bytes 98312 | tf_op jit(solution)/shard_map/ppermute | solution.py:283
  41.4 5.4 %collective-permute-start = (bf16[32,512]{1,0:T(8,128)(2,1)S(1)}, bf16[32,512]{1,0:T(8,128)(2,1)S(1)}, u32[]{:S(2)}, u32[]{:S(2)}) collective-permute-start(bf16[32,512]{1,0:T(8,128)(2,1)S(1)} %copy-done.2), channel_id=1, source_target_pairs={{0,0},{1,32},{2,64},{3,96},{4,128},{5,160},{6,192},{7,224},{8,256}... | collective-permute-start | bytes 98312 | tf_op jit(solution)/shard_map/ppermute | solution.py:283
  46.8 0.0 collective-permute-done.3
  46.8 0.0 collective-permute-done.2
  46.8 0.9 collective-permute-done.1
  47.7 3.5 %collective-permute-done = bf16[32,512]{1,0:T(8,128)(2,1)S(1)} collective-permute-done((bf16[32,512]{1,0:T(8,128)(2,1)S(1)}, bf16[32,512]{1,0:T(8,128)(2,1)S(1)}, u32[]{:S(2)}, u32[]{:S(2)}) %collective-permute-start) | collective-permute-done | bytes 32800 | tf_op jit(solution)/shard_map/ppermute | solution.py:283
  51.2 0.0 all-to-all-done.parts_ref
  51.2 1.2 %lowrank_sum.1 = bf16[16,2,32,512]{3,2,1,0:T(8,128)(2,1)} custom-call(bf16[16,2,32,512]{3,2,1,0:T(8,128)(2,1)S(1)} %all-to-all-done.parts_ref), custom_call_target="tpu_custom_call" | custom-call | tf_op jit(solution)/shard_map/lowrank_sum/pallas_call | solution.py:379
  52.4 14.4 %all-to-all-start.1 = ((bf16[16,2,32,512]{3,2,1,0:T(8,128)(2,1)}), bf16[16,2,32,512]{3,2,1,0:T(8,128)(2,1)S(1)}, u32[]{:S(2)}, u32[]{:S(2)}) async-start(bf16[16,2,32,512]{3,2,1,0:T(8,128)(2,1)} %lowrank_sum.1), calls=%async_computation.1 | async-start | bytes 2097152 | tf_op jit(solution)/shard_map/all_to_all | solution.py:387
  66.8 1.9 %collective-permute-start.4 = (bf16[4,32,512]{2,1,0:T(8,128)(2,1)S(1)}, bf16[4,32,512]{2,1,0:T(8,128)(2,1)S(1)}, u32[]{:S(2)}, u32[]{:S(2)}) collective-permute-start(bf16[4,32,512]{2,1,0:T(8,128)(2,1)S(1)} %pad_maximum_fusion), channel_id=1, source_target_pairs={{0,64},{16,80},{32,96},{48,112},{64,0},{80,16},{96,32},{112,48},{1... | collective-permute-start | bytes 393224 | tf_op jit(solution)/shard_map/ppermute | solution.py:294
  68.7 5.9 %collective-permute-done.4 = bf16[4,32,512]{2,1,0:T(8,128)(2,1)S(1)} collective-permute-done((bf16[4,32,512]{2,1,0:T(8,128)(2,1)S(1)}, bf16[4,32,512]{2,1,0:T(8,128)(2,1)S(1)}, u32[]{:S(2)}, u32[]{:S(2)}) %collective-permute-start.4) | collective-permute-done | bytes 131104 | tf_op jit(solution)/shard_map/ppermute | solution.py:294
  74.7 7.2 %all-to-all-done.1.lowrank_ref = bf16[16,2,32,512]{3,2,1,0:T(8,128)(2,1)S(1)} async-done(((bf16[16,2,32,512]{3,2,1,0:T(8,128)(2,1)}), bf16[16,2,32,512]{3,2,1,0:T(8,128)(2,1)S(1)}, u32[]{:S(2)}, u32[]{:S(2)}) %all-to-all-start.1) | async-done | bytes 1048608 | tf_op jit(solution)/shard_map/all_to_all | solution.py:387
  81.9 2.9 %collective-permute-start.5 = (bf16[8,32,512]{2,1,0:T(8,128)(2,1)S(1)}, bf16[8,32,512]{2,1,0:T(8,128)(2,1)S(1)}, u32[]{:S(2)}, u32[]{:S(2)}) collective-permute-start(bf16[8,32,512]{2,1,0:T(8,128)(2,1)S(1)} %constant_dynamic-update-slice_fusion.refs_0_), channel_id=1, source_target_pairs={{0,32},{16,48},{32,0},{48,16},{64,96},{80,112},{96,64},{112,80},{1... | collective-permute-start | bytes 786440 | tf_op jit(solution)/shard_map/ppermute | solution.py:294
  84.8 0.0 copy-start.1
  84.8 1.2 %copy-done.1 = bf16[2,512,512]{2,1,0:T(8,128)(2,1)S(1)} copy-done((bf16[2,512,512]{2,1,0:T(8,128)(2,1)S(1)}, bf16[2,512,512]{2,1,0:T(8,128)(2,1)}, u32[]{:S(2)}) %copy-start.1) | copy-done | bytes 1048600
  86.1 2.5 %partial_features.1 = bf16[16,128,128]{2,1,0:T(8,128)(2,1)} custom-call(bf16[16,2,32,512]{3,2,1,0:T(8,128)(2,1)S(1)} %all-to-all-done.1.lowrank_ref, bf16[2,512,512]{2,1,0:T(8,128)(2,1)S(1)} %copy-done.1, bf16[2,784,512]{2,1,0:T(8,128)(2,1)S(1)} %copy-done), custom_call_target="tpu_custom_call" | custom-call | tf_op jit(solution)/shard_map/partial_features/pallas_call | solution.py:394
  88.5 3.6 %all-to-all-start.2 = ((bf16[16,128,128]{2,1,0:T(8,128)(2,1)}), bf16[16,128,128]{2,1,0:T(8,128)(2,1)S(1)}, u32[]{:S(2)}, u32[]{:S(2)}) async-start(bf16[16,128,128]{2,1,0:T(8,128)(2,1)} %partial_features.1), calls=%async_computation.2 | async-start | bytes 1048576 | tf_op jit(solution)/shard_map/all_to_all | solution.py:403
  92.1 1.9 %collective-permute-start.6 = (bf16[8,32,512]{2,1,0:T(8,128)(2,1)S(1)}, bf16[8,32,512]{2,1,0:T(8,128)(2,1)S(1)}, u32[]{:S(2)}, u32[]{:S(2)}) collective-permute-start(bf16[8,32,512]{2,1,0:T(8,128)(2,1)S(1)} %constant_dynamic-update-slice_fusion.refs_0_), channel_id=1, source_target_pairs={{0,16},{16,0},{32,48},{48,32},{64,80},{80,64},{96,112},{112,96},{1... | collective-permute-start | bytes 786440 | tf_op jit(solution)/shard_map/ppermute | solution.py:297
  94.1 0.0 collective-permute-done.5.refs_1_
  94.1 2.4 %collective-permute-start.7 = (bf16[8,32,512]{2,1,0:T(8,128)(2,1)S(1)}, bf16[8,32,512]{2,1,0:T(8,128)(2,1)S(1)}, u32[]{:S(2)}, u32[]{:S(2)}) collective-permute-start(bf16[8,32,512]{2,1,0:T(8,128)(2,1)S(1)} %collective-permute-done.5.refs_1_), channel_id=1, source_target_pairs={{0,16},{16,0},{32,48},{48,32},{64,80},{80,64},{96,112},{112,96},{1... | collective-permute-start | bytes 786440 | tf_op jit(solution)/shard_map/ppermute | solution.py:297
  96.5 0.1 pad_add_fusion.place
  96.6 0.0 collective-permute-done.6.refs_2_
  96.6 5.6 %all-to-all-done.2.parts_ref = bf16[16,128,128]{2,1,0:T(8,128)(2,1)S(1)} async-done(((bf16[16,128,128]{2,1,0:T(8,128)(2,1)}), bf16[16,128,128]{2,1,0:T(8,128)(2,1)S(1)}, u32[]{:S(2)}, u32[]{:S(2)}) %all-to-all-start.2) | async-done | bytes 524320 | tf_op jit(solution)/shard_map/all_to_all | solution.py:403
  102.2 0.0 collective-permute-done.7.refs_3_
  102.2 1.8 %scores.1 = f32[2,64]{1,0:T(2,128)} custom-call(s32[2]{0:T(128)S(1)} %pad_add_fusion.place, bf16[16,128,128]{2,1,0:T(8,128)(2,1)S(1)} %all-to-all-done.2.parts_ref, bf16[8,32,512]{2,1,0:T(8,128)(2,1)S(1)} %constant_dynamic-update-slice_fusion.refs_0_, bf16[8,32,512]{2,1,0:T(8,128)(2,1)S(1)} %collective-permute-done.5.refs_1_, ...), custom_call_target="tpu_custom_call" | custom-call | tf_op jit(solution)/shard_map/scores/pallas_call | solution.py:407
  (4 shorter events, 0.0 us)
Async XLA Ops:
  8.7 7.1 %copy-start.2 = (bf16[32,512]{1,0:T(8,128)(2,1)S(1)}, bf16[32,512]{1,0:T(8,128)(2,1)}, u32[]{:S(2)}) copy-start(bf16[32,512]{1,0:T(8,128)(2,1)} %param.31) | copy-start | bytes 98308
  8.8 42.4 %all-to-all-start = ((bf16[16,2,32,512]{3,2,1,0:T(8,128)(2,1)}), bf16[16,2,32,512]{3,2,1,0:T(8,128)(2,1)S(1)}, u32[]{:S(2)}, u32[]{:S(2)}) async-start(bf16[16,2,32,512]{3,2,1,0:T(8,128)(2,1)} %get-tuple-element.20), calls=%async_computation | async-start | bytes 2097152 | tf_op jit(solution)/shard_map/all_to_all | solution.py:375
  15.8 69.0 %copy-start = (bf16[2,784,512]{2,1,0:T(8,128)(2,1)S(1)}, bf16[2,784,512]{2,1,0:T(8,128)(2,1)}, u32[]{:S(2)}) copy-start(bf16[2,784,512]{2,1,0:T(8,128)(2,1)} %get-tuple-element.28.packed_ref) | copy-start | bytes 4816900
  15.8 30.9 %collective-permute-start.3 = (bf16[32,512]{1,0:T(8,128)(2,1)S(1)}, bf16[32,512]{1,0:T(8,128)(2,1)S(1)}, u32[]{:S(2)}, u32[]{:S(2)}) collective-permute-start(bf16[32,512]{1,0:T(8,128)(2,1)S(1)} %copy-done.2), channel_id=1, source_target_pairs={{0,384},{1,416},{2,448},{3,480},{4,256},{5,288},{6,320},{7,352},{8... | collective-permute-start | bytes 98312 | tf_op jit(solution)/shard_map/ppermute | solution.py:283
  30.7 16.1 %collective-permute-start.2 = (bf16[32,512]{1,0:T(8,128)(2,1)S(1)}, bf16[32,512]{1,0:T(8,128)(2,1)S(1)}, u32[]{:S(2)}, u32[]{:S(2)}) collective-permute-start(bf16[32,512]{1,0:T(8,128)(2,1)S(1)} %copy-done.2), channel_id=1, source_target_pairs={{0,128},{1,160},{2,192},{3,224},{4,0},{5,32},{6,64},{7,96},{8,384}... | collective-permute-start | bytes 98312 | tf_op jit(solution)/shard_map/ppermute | solution.py:283
  36.2 11.5 %collective-permute-start.1 = (bf16[32,512]{1,0:T(8,128)(2,1)S(1)}, bf16[32,512]{1,0:T(8,128)(2,1)S(1)}, u32[]{:S(2)}, u32[]{:S(2)}) collective-permute-start(bf16[32,512]{1,0:T(8,128)(2,1)S(1)} %copy-done.2), channel_id=1, source_target_pairs={{0,256},{1,288},{2,320},{3,352},{4,384},{5,416},{6,448},{7,480},{8... | collective-permute-start | bytes 98312 | tf_op jit(solution)/shard_map/ppermute | solution.py:283
  41.4 9.8 %collective-permute-start = (bf16[32,512]{1,0:T(8,128)(2,1)S(1)}, bf16[32,512]{1,0:T(8,128)(2,1)S(1)}, u32[]{:S(2)}, u32[]{:S(2)}) collective-permute-start(bf16[32,512]{1,0:T(8,128)(2,1)S(1)} %copy-done.2), channel_id=1, source_target_pairs={{0,0},{1,32},{2,64},{3,96},{4,128},{5,160},{6,192},{7,224},{8,256}... | collective-permute-start | bytes 98312 | tf_op jit(solution)/shard_map/ppermute | solution.py:283
  52.4 29.5 %all-to-all-start.1 = ((bf16[16,2,32,512]{3,2,1,0:T(8,128)(2,1)}), bf16[16,2,32,512]{3,2,1,0:T(8,128)(2,1)S(1)}, u32[]{:S(2)}, u32[]{:S(2)}) async-start(bf16[16,2,32,512]{3,2,1,0:T(8,128)(2,1)} %lowrank_sum.1), calls=%async_computation.1 | async-start | bytes 2097152 | tf_op jit(solution)/shard_map/all_to_all | solution.py:387
  66.8 7.9 %collective-permute-start.4 = (bf16[4,32,512]{2,1,0:T(8,128)(2,1)S(1)}, bf16[4,32,512]{2,1,0:T(8,128)(2,1)S(1)}, u32[]{:S(2)}, u32[]{:S(2)}) collective-permute-start(bf16[4,32,512]{2,1,0:T(8,128)(2,1)S(1)} %pad_maximum_fusion), channel_id=1, source_target_pairs={{0,64},{16,80},{32,96},{48,112},{64,0},{80,16},{96,32},{112,48},{1... | collective-permute-start | bytes 393224 | tf_op jit(solution)/shard_map/ppermute | solution.py:294
  81.9 12.2 %collective-permute-start.5 = (bf16[8,32,512]{2,1,0:T(8,128)(2,1)S(1)}, bf16[8,32,512]{2,1,0:T(8,128)(2,1)S(1)}, u32[]{:S(2)}, u32[]{:S(2)}) collective-permute-start(bf16[8,32,512]{2,1,0:T(8,128)(2,1)S(1)} %constant_dynamic-update-slice_fusion.refs_0_), channel_id=1, source_target_pairs={{0,32},{16,48},{32,0},{48,16},{64,96},{80,112},{96,64},{112,80},{1... | collective-permute-start | bytes 786440 | tf_op jit(solution)/shard_map/ppermute | solution.py:294
  84.8 1.2 %copy-start.1 = (bf16[2,512,512]{2,1,0:T(8,128)(2,1)S(1)}, bf16[2,512,512]{2,1,0:T(8,128)(2,1)}, u32[]{:S(2)}) copy-start(bf16[2,512,512]{2,1,0:T(8,128)(2,1)} %hidden_ref.3) | copy-start | bytes 3145732
  88.5 13.6 %all-to-all-start.2 = ((bf16[16,128,128]{2,1,0:T(8,128)(2,1)}), bf16[16,128,128]{2,1,0:T(8,128)(2,1)S(1)}, u32[]{:S(2)}, u32[]{:S(2)}) async-start(bf16[16,128,128]{2,1,0:T(8,128)(2,1)} %partial_features.1), calls=%async_computation.2 | async-start | bytes 1048576 | tf_op jit(solution)/shard_map/all_to_all | solution.py:403
  92.1 4.5 %collective-permute-start.6 = (bf16[8,32,512]{2,1,0:T(8,128)(2,1)S(1)}, bf16[8,32,512]{2,1,0:T(8,128)(2,1)S(1)}, u32[]{:S(2)}, u32[]{:S(2)}) collective-permute-start(bf16[8,32,512]{2,1,0:T(8,128)(2,1)S(1)} %constant_dynamic-update-slice_fusion.refs_0_), channel_id=1, source_target_pairs={{0,16},{16,0},{32,48},{48,32},{64,80},{80,64},{96,112},{112,96},{1... | collective-permute-start | bytes 786440 | tf_op jit(solution)/shard_map/ppermute | solution.py:297
  94.1 8.1 %collective-permute-start.7 = (bf16[8,32,512]{2,1,0:T(8,128)(2,1)S(1)}, bf16[8,32,512]{2,1,0:T(8,128)(2,1)S(1)}, u32[]{:S(2)}, u32[]{:S(2)}) collective-permute-start(bf16[8,32,512]{2,1,0:T(8,128)(2,1)S(1)} %collective-permute-done.5.refs_1_), channel_id=1, source_target_pairs={{0,16},{16,0},{32,48},{48,32},{64,80},{80,64},{96,112},{112,96},{1... | collective-permute-start | bytes 786440 | tf_op jit(solution)/shard_map/ppermute | solution.py:297

commit v9 on v7

--- a/solution.py
+++ b/solution.py
@@ -388,7 +388,6 @@
     lowrank = lax.all_to_all(summed, "mp", 0, 0, tiled=True)
     four = jnp.concatenate([two, two_more])
     four_more = from_level(four, 2)
-    lowrank, four, four_more = lax.optimization_barrier((lowrank, four, four_more))
     eight = jnp.concatenate([four, four_more])
     eight_more = from_level(eight, 1)
 

time: 98.5 us -> 95.4 us (0.969)
  the two profiles are of different devices: /device:TPU:32 before, /device:TPU:8 now
where the time goes in v9:
time: 95.4 us; the launch traced here: 94.8 us
  starting transfers between devices  52.6 us (55%)
  waiting for transfers between devices  26.5 us (28%)
  Pallas kernels  14.2 us (15%)
  local copies, waits for them, and re-layouts  1.25 us (1%)
    ppermute x2, starting transfers between devices, to_column(): lax.ppermute(seed_feats, ('dp', 'mp'), [(d * model_size + m, ((m ^ flip)...  19.1 us
    ppermute x3, waiting for transfers between devices, from_level(): lax.ppermute(block, 'dp', [(d, d ^ 2 * flip) for d in range(data_size)])  15.1 us
    all_to_all x1, starting transfers between devices, local(): received = lax.all_to_all(send, 'mp', 0, 0, tiled=True)  11.3 us
    pallas_call x1, Pallas kernels, local(): pl.pallas_call(attention_kernel, name='attention_backward', out_shape=(ja...  8.76 us
    ppermute x3, starting transfers between devices, from_level(): lax.ppermute(block, 'dp', [(d, d ^ 2 * flip) for d in range(data_size)])  8.01 us
    all_to_all x1, starting transfers between devices, local(): feat_all = lax.all_to_all(feat_parts, 'mp', 0, 0, tiled=True)  4.95 us
    all_to_all x1, starting transfers between devices, local(): lowrank = lax.all_to_all(summed, 'mp', 0, 0, tiled=True)  4.9 us
    ppermute x2, starting transfers between devices, from_core(): return lax.ppermute(block, 'dp', [(d, d ^ 1) for d in range(data_size)])  4.33 us
  transfers between devices with their start and end apart: 10, of which 6 were waited for; matrix products, arithmetic and copies ran while one was open for 0% of the time, Pallas kernels for 12%

profile of v9, /device:TPU:8, one launch (start us, length us, event | category | flops | bytes accessed | tf_op | source)
XLA Modules:
  0.0 94.8 jit_solution(3878503999517671207)
XLA Ops:
  0.0 15.2 %collective-permute-start.1 = (bf16[32,512]{1,0:T(8,128)(2,1)}, bf16[32,512]{1,0:T(8,128)(2,1)S(1)}, u32[]{:S(2)}, u32[]{:S(2)}) collective-permute-start(bf16[32,512]{1,0:T(8,128)(2,1)} %param.31), channel_id=1, source_target_pairs={{0,256},{1,288},{2,320},{3,352},{4,384},{5,416},{6,448},{7,480},{8... | collective-permute-start | bytes 98312 | tf_op jit(solution)/shard_map/ppermute | solution.py:283
  15.2 3.9 %collective-permute-start = (bf16[32,512]{1,0:T(8,128)(2,1)}, bf16[32,512]{1,0:T(8,128)(2,1)S(1)}, u32[]{:S(2)}, u32[]{:S(2)}) collective-permute-start(bf16[32,512]{1,0:T(8,128)(2,1)} %param.31), channel_id=1, source_target_pairs={{0,0},{1,32},{2,64},{3,96},{4,128},{5,160},{6,192},{7,224},{8,256}... | collective-permute-start | bytes 98312 | tf_op jit(solution)/shard_map/ppermute | solution.py:283
  19.1 8.8 %attention_backward.1 = (bf16[16,2,32,512]{3,2,1,0:T(8,128)(2,1)}, bf16[2,784,512]{2,1,0:T(8,128)(2,1)}) custom-call(s32[1]{0:T(128)} %bitcast.2.kv_index, bf16[2,512,512]{2,1,0:T(8,128)(2,1)} %hidden_ref.3, bf16[2,512,512]{2,1,0:T(8,128)(2,1)} %query_ref.1, bf16[2,512,512]{2,1,0:T(8,128)(2,1)} %grad_ref.1, bf16[2,512,1024]{2,1,0:T(8,128)(2,1)} %key_ref.1, ...), custom_call_target="tpu_custom_call" | custom-call | flops 5000000000 | bytes 8000000 | tf_op jit(solution)/shard_map/attention_backward/pallas_call | solution.py:311
  27.9 0.0 collective-permute-done.1
  27.9 0.0 collective-permute-done
  27.9 11.3 %all-to-all-start = ((bf16[16,2,32,512]{3,2,1,0:T(8,128)(2,1)}), bf16[16,2,32,512]{3,2,1,0:T(8,128)(2,1)S(1)}, u32[]{:S(2)}, u32[]{:S(2)}) async-start(bf16[16,2,32,512]{3,2,1,0:T(8,128)(2,1)} %get-tuple-element.16), calls=%async_computation | async-start | bytes 2097152 | tf_op jit(solution)/shard_map/all_to_all | solution.py:376
  39.2 0.0 copy-start
  39.2 4.2 %collective-permute-start.2 = (bf16[2,32,512]{2,1,0:T(8,128)(2,1)S(1)}, bf16[2,32,512]{2,1,0:T(8,128)(2,1)S(1)}, u32[]{:S(2)}, u32[]{:S(2)}) collective-permute-start(bf16[2,32,512]{2,1,0:T(8,128)(2,1)S(1)} %pad_maximum_fusion.1), channel_id=1, source_target_pairs={{0,128},{16,144},{32,160},{48,176},{64,192},{80,208},{96,224},{112... | collective-permute-start | bytes 196616 | tf_op jit(solution)/shard_map/ppermute | solution.py:294
  43.4 7.9 %collective-permute-done.2 = bf16[2,32,512]{2,1,0:T(8,128)(2,1)S(1)} collective-permute-done((bf16[2,32,512]{2,1,0:T(8,128)(2,1)S(1)}, bf16[2,32,512]{2,1,0:T(8,128)(2,1)S(1)}, u32[]{:S(2)}, u32[]{:S(2)}) %collective-permute-start.2) | collective-permute-done | bytes 65568 | tf_op jit(solution)/shard_map/ppermute | solution.py:294
  51.3 3.4 %all-to-all-done.parts_ref = bf16[16,2,32,512]{3,2,1,0:T(8,128)(2,1)S(1)} async-done(((bf16[16,2,32,512]{3,2,1,0:T(8,128)(2,1)}), bf16[16,2,32,512]{3,2,1,0:T(8,128)(2,1)S(1)}, u32[]{:S(2)}, u32[]{:S(2)}) %all-to-all-start) | async-done | bytes 1048608 | tf_op jit(solution)/shard_map/all_to_all | solution.py:376
  54.7 1.2 %lowrank_sum.1 = bf16[16,2,32,512]{3,2,1,0:T(8,128)(2,1)} custom-call(bf16[16,2,32,512]{3,2,1,0:T(8,128)(2,1)S(1)} %all-to-all-done.parts_ref), custom_call_target="tpu_custom_call" | custom-call | tf_op jit(solution)/shard_map/lowrank_sum/pallas_call | solution.py:380
  55.9 4.9 %all-to-all-start.1 = ((bf16[16,2,32,512]{3,2,1,0:T(8,128)(2,1)}), bf16[16,2,32,512]{3,2,1,0:T(8,128)(2,1)S(1)}, u32[]{:S(2)}, u32[]{:S(2)}) async-start(bf16[16,2,32,512]{3,2,1,0:T(8,128)(2,1)} %lowrank_sum.1), calls=%async_computation.1 | async-start | bytes 2097152 | tf_op jit(solution)/shard_map/all_to_all | solution.py:388
  60.8 1.9 %collective-permute-start.3 = (bf16[4,32,512]{2,1,0:T(8,128)(2,1)S(1)}, bf16[4,32,512]{2,1,0:T(8,128)(2,1)S(1)}, u32[]{:S(2)}, u32[]{:S(2)}) collective-permute-start(bf16[4,32,512]{2,1,0:T(8,128)(2,1)S(1)} %pad_maximum_fusion), channel_id=1, source_target_pairs={{0,64},{16,80},{32,96},{48,112},{64,0},{80,16},{96,32},{112,48},{1... | collective-permute-start | bytes 393224 | tf_op jit(solution)/shard_map/ppermute | solution.py:294
  62.8 7.2 %collective-permute-done.3 = bf16[4,32,512]{2,1,0:T(8,128)(2,1)S(1)} collective-permute-done((bf16[4,32,512]{2,1,0:T(8,128)(2,1)S(1)}, bf16[4,32,512]{2,1,0:T(8,128)(2,1)S(1)}, u32[]{:S(2)}, u32[]{:S(2)}) %collective-permute-start.3) | collective-permute-done | bytes 131104 | tf_op jit(solution)/shard_map/ppermute | solution.py:294
  70.0 1.9 %collective-permute-start.4 = (bf16[8,32,512]{2,1,0:T(8,128)(2,1)S(1)}, bf16[8,32,512]{2,1,0:T(8,128)(2,1)S(1)}, u32[]{:S(2)}, u32[]{:S(2)}) collective-permute-start(bf16[8,32,512]{2,1,0:T(8,128)(2,1)S(1)} %constant_dynamic-update-slice_fusion.refs_0_), channel_id=1, source_target_pairs={{0,32},{16,48},{32,0},{48,16},{64,96},{80,112},{96,64},{112,80},{1... | collective-permute-start | bytes 786440 | tf_op jit(solution)/shard_map/ppermute | solution.py:294
  71.9 3.7 %all-to-all-done.1.lowrank_ref = bf16[16,2,32,512]{3,2,1,0:T(8,128)(2,1)S(1)} async-done(((bf16[16,2,32,512]{3,2,1,0:T(8,128)(2,1)}), bf16[16,2,32,512]{3,2,1,0:T(8,128)(2,1)S(1)}, u32[]{:S(2)}, u32[]{:S(2)}) %all-to-all-start.1) | async-done | bytes 1048608 | tf_op jit(solution)/shard_map/all_to_all | solution.py:388
  75.6 0.0 copy-done
  75.6 0.0 copy-start.1
  75.6 1.2 %copy-done.1 = bf16[2,512,512]{2,1,0:T(8,128)(2,1)S(1)} copy-done((bf16[2,512,512]{2,1,0:T(8,128)(2,1)S(1)}, bf16[2,512,512]{2,1,0:T(8,128)(2,1)}, u32[]{:S(2)}) %copy-start.1) | copy-done | bytes 1048600
  76.8 2.5 %partial_features.1 = bf16[16,128,128]{2,1,0:T(8,128)(2,1)} custom-call(bf16[16,2,32,512]{3,2,1,0:T(8,128)(2,1)S(1)} %all-to-all-done.1.lowrank_ref, bf16[2,512,512]{2,1,0:T(8,128)(2,1)S(1)} %copy-done.1, bf16[2,784,512]{2,1,0:T(8,128)(2,1)S(1)} %copy-done), custom_call_target="tpu_custom_call" | custom-call | tf_op jit(solution)/shard_map/partial_features/pallas_call | solution.py:394
  79.3 5.0 %all-to-all-start.2 = ((bf16[16,128,128]{2,1,0:T(8,128)(2,1)}), bf16[16,128,128]{2,1,0:T(8,128)(2,1)S(1)}, u32[]{:S(2)}, u32[]{:S(2)}) async-start(bf16[16,128,128]{2,1,0:T(8,128)(2,1)} %partial_features.1), calls=%async_computation.2 | async-start | bytes 1048576 | tf_op jit(solution)/shard_map/all_to_all | solution.py:403
  84.3 0.0 collective-permute-done.4.refs_1_
  84.3 1.9 %collective-permute-start.6 = (bf16[8,32,512]{2,1,0:T(8,128)(2,1)S(1)}, bf16[8,32,512]{2,1,0:T(8,128)(2,1)S(1)}, u32[]{:S(2)}, u32[]{:S(2)}) collective-permute-start(bf16[8,32,512]{2,1,0:T(8,128)(2,1)S(1)} %collective-permute-done.4.refs_1_), channel_id=1, source_target_pairs={{0,16},{16,0},{32,48},{48,32},{64,80},{80,64},{96,112},{112,96},{1... | collective-permute-start | bytes 786440 | tf_op jit(solution)/shard_map/ppermute | solution.py:297
  86.2 2.4 %collective-permute-start.5 = (bf16[8,32,512]{2,1,0:T(8,128)(2,1)S(1)}, bf16[8,32,512]{2,1,0:T(8,128)(2,1)S(1)}, u32[]{:S(2)}, u32[]{:S(2)}) collective-permute-start(bf16[8,32,512]{2,1,0:T(8,128)(2,1)S(1)} %constant_dynamic-update-slice_fusion.refs_0_), channel_id=1, source_target_pairs={{0,16},{16,0},{32,48},{48,32},{64,80},{80,64},{96,112},{112,96},{1... | collective-permute-start | bytes 786440 | tf_op jit(solution)/shard_map/ppermute | solution.py:297
  88.6 0.1 pad_add_fusion.place
  88.7 0.0 collective-permute-done.6.refs_3_
  88.7 1.0 %collective-permute-done.5.refs_2_ = bf16[8,32,512]{2,1,0:T(8,128)(2,1)S(1)} collective-permute-done((bf16[8,32,512]{2,1,0:T(8,128)(2,1)S(1)}, bf16[8,32,512]{2,1,0:T(8,128)(2,1)S(1)}, u32[]{:S(2)}, u32[]{:S(2)}) %collective-permute-start.5) | collective-permute-done | bytes 262176 | tf_op jit(solution)/shard_map/ppermute | solution.py:297
  89.8 3.2 %all-to-all-done.2.parts_ref = bf16[16,128,128]{2,1,0:T(8,128)(2,1)S(1)} async-done(((bf16[16,128,128]{2,1,0:T(8,128)(2,1)}), bf16[16,128,128]{2,1,0:T(8,128)(2,1)S(1)}, u32[]{:S(2)}, u32[]{:S(2)}) %all-to-all-start.2) | async-done | bytes 524320 | tf_op jit(solution)/shard_map/all_to_all | solution.py:403
  93.0 1.8 %scores.1 = f32[2,64]{1,0:T(2,128)} custom-call(s32[2]{0:T(128)S(1)} %pad_add_fusion.place, bf16[16,128,128]{2,1,0:T(8,128)(2,1)S(1)} %all-to-all-done.2.parts_ref, bf16[8,32,512]{2,1,0:T(8,128)(2,1)S(1)} %constant_dynamic-update-slice_fusion.refs_0_, bf16[8,32,512]{2,1,0:T(8,128)(2,1)S(1)} %collective-permute-done.4.refs_1_, ...), custom_call_target="tpu_custom_call" | custom-call | tf_op jit(solution)/shard_map/scores/pallas_call | solution.py:407
  (5 shorter events, 0.0 us)
Async XLA Ops:
  0.0 27.9 %collective-permute-start.1 = (bf16[32,512]{1,0:T(8,128)(2,1)}, bf16[32,512]{1,0:T(8,128)(2,1)S(1)}, u32[]{:S(2)}, u32[]{:S(2)}) collective-permute-start(bf16[32,512]{1,0:T(8,128)(2,1)} %param.31), channel_id=1, source_target_pairs={{0,256},{1,288},{2,320},{3,352},{4,384},{5,416},{6,448},{7,480},{8... | collective-permute-start | bytes 98312 | tf_op jit(solution)/shard_map/ppermute | solution.py:283
  15.2 12.7 %collective-permute-start = (bf16[32,512]{1,0:T(8,128)(2,1)}, bf16[32,512]{1,0:T(8,128)(2,1)S(1)}, u32[]{:S(2)}, u32[]{:S(2)}) collective-permute-start(bf16[32,512]{1,0:T(8,128)(2,1)} %param.31), channel_id=1, source_target_pairs={{0,0},{1,32},{2,64},{3,96},{4,128},{5,160},{6,192},{7,224},{8,256}... | collective-permute-start | bytes 98312 | tf_op jit(solution)/shard_map/ppermute | solution.py:283
  27.9 26.8 %all-to-all-start = ((bf16[16,2,32,512]{3,2,1,0:T(8,128)(2,1)}), bf16[16,2,32,512]{3,2,1,0:T(8,128)(2,1)S(1)}, u32[]{:S(2)}, u32[]{:S(2)}) async-start(bf16[16,2,32,512]{3,2,1,0:T(8,128)(2,1)} %get-tuple-element.16), calls=%async_computation | async-start | bytes 2097152 | tf_op jit(solution)/shard_map/all_to_all | solution.py:376
  39.2 36.4 %copy-start = (bf16[2,784,512]{2,1,0:T(8,128)(2,1)S(1)}, bf16[2,784,512]{2,1,0:T(8,128)(2,1)}, u32[]{:S(2)}) copy-start(bf16[2,784,512]{2,1,0:T(8,128)(2,1)} %get-tuple-element.20.packed_ref) | copy-start | bytes 4816900
  39.2 12.1 %collective-permute-start.2 = (bf16[2,32,512]{2,1,0:T(8,128)(2,1)S(1)}, bf16[2,32,512]{2,1,0:T(8,128)(2,1)S(1)}, u32[]{:S(2)}, u32[]{:S(2)}) collective-permute-start(bf16[2,32,512]{2,1,0:T(8,128)(2,1)S(1)} %pad_maximum_fusion.1), channel_id=1, source_target_pairs={{0,128},{16,144},{32,160},{48,176},{64,192},{80,208},{96,224},{112... | collective-permute-start | bytes 196616 | tf_op jit(solution)/shard_map/ppermute | solution.py:294
  55.9 19.7 %all-to-all-start.1 = ((bf16[16,2,32,512]{3,2,1,0:T(8,128)(2,1)}), bf16[16,2,32,512]{3,2,1,0:T(8,128)(2,1)S(1)}, u32[]{:S(2)}, u32[]{:S(2)}) async-start(bf16[16,2,32,512]{3,2,1,0:T(8,128)(2,1)} %lowrank_sum.1), calls=%async_computation.1 | async-start | bytes 2097152 | tf_op jit(solution)/shard_map/all_to_all | solution.py:388
  60.8 9.2 %collective-permute-start.3 = (bf16[4,32,512]{2,1,0:T(8,128)(2,1)S(1)}, bf16[4,32,512]{2,1,0:T(8,128)(2,1)S(1)}, u32[]{:S(2)}, u32[]{:S(2)}) collective-permute-start(bf16[4,32,512]{2,1,0:T(8,128)(2,1)S(1)} %pad_maximum_fusion), channel_id=1, source_target_pairs={{0,64},{16,80},{32,96},{48,112},{64,0},{80,16},{96,32},{112,48},{1... | collective-permute-start | bytes 393224 | tf_op jit(solution)/shard_map/ppermute | solution.py:294
  70.0 14.3 %collective-permute-start.4 = (bf16[8,32,512]{2,1,0:T(8,128)(2,1)S(1)}, bf16[8,32,512]{2,1,0:T(8,128)(2,1)S(1)}, u32[]{:S(2)}, u32[]{:S(2)}) collective-permute-start(bf16[8,32,512]{2,1,0:T(8,128)(2,1)S(1)} %constant_dynamic-update-slice_fusion.refs_0_), channel_id=1, source_target_pairs={{0,32},{16,48},{32,0},{48,16},{64,96},{80,112},{96,64},{112,80},{1... | collective-permute-start | bytes 786440 | tf_op jit(solution)/shard_map/ppermute | solution.py:294
  75.6 1.2 %copy-start.1 = (bf16[2,512,512]{2,1,0:T(8,128)(2,1)S(1)}, bf16[2,512,512]{2,1,0:T(8,128)(2,1)}, u32[]{:S(2)}) copy-start(bf16[2,512,512]{2,1,0:T(8,128)(2,1)} %hidden_ref.3) | copy-start | bytes 3145732
  79.3 13.7 %all-to-all-start.2 = ((bf16[16,128,128]{2,1,0:T(8,128)(2,1)}), bf16[16,128,128]{2,1,0:T(8,128)(2,1)S(1)}, u32[]{:S(2)}, u32[]{:S(2)}) async-start(bf16[16,128,128]{2,1,0:T(8,128)(2,1)} %partial_features.1), calls=%async_computation.2 | async-start | bytes 1048576 | tf_op jit(solution)/shard_map/all_to_all | solution.py:403
  84.3 4.4 %collective-permute-start.6 = (bf16[8,32,512]{2,1,0:T(8,128)(2,1)S(1)}, bf16[8,32,512]{2,1,0:T(8,128)(2,1)S(1)}, u32[]{:S(2)}, u32[]{:S(2)}) collective-permute-start(bf16[8,32,512]{2,1,0:T(8,128)(2,1)S(1)} %collective-permute-done.4.refs_1_), channel_id=1, source_target_pairs={{0,16},{16,0},{32,48},{48,32},{64,80},{80,64},{96,112},{112,96},{1... | collective-permute-start | bytes 786440 | tf_op jit(solution)/shard_map/ppermute | solution.py:297
  86.2 3.6 %collective-permute-start.5 = (bf16[8,32,512]{2,1,0:T(8,128)(2,1)S(1)}, bf16[8,32,512]{2,1,0:T(8,128)(2,1)S(1)}, u32[]{:S(2)}, u32[]{:S(2)}) collective-permute-start(bf16[8,32,512]{2,1,0:T(8,128)(2,1)S(1)} %constant_dynamic-update-slice_fusion.refs_0_), channel_id=1, source_target_pairs={{0,16},{16,0},{32,48},{48,32},{64,80},{80,64},{96,112},{112,96},{1... | collective-permute-start | bytes 786440 | tf_op jit(solution)/shard_map/ppermute | solution.py:297

commit v10 on v9

--- a/solution.py
+++ b/solution.py
@@ -166,6 +166,10 @@
 def sum_kernel(parts_ref, out_ref):
     total = jnp.sum(parts_ref[...].astype(F32), axis=0)
     out_ref[...] = jnp.broadcast_to(total.astype(BF16)[None], out_ref.shape)
+
+
+def stage_kernel(hidden_ref, packed_ref, out_ref):
+    out_ref[...] = hidden_ref[...]
 
 
 def feature_kernel(lowrank_ref, hidden_ref, packed_ref, out_ref):
@@ -376,7 +380,9 @@
     received = lax.all_to_all(send, "mp", 0, 0, tiled=True)
     two = jnp.stack([seed_near, seed_far])
     two_more = from_level(two, 4)
-    received, two, two_more = lax.optimization_barrier((received, two, two_more))
+    received, two, two_more, hidden_later, packed = lax.optimization_barrier(
+        (received, two, two_more, hidden_in, packed)
+    )
     summed = pl.pallas_call(
         sum_kernel,
         name="lowrank_sum",
@@ -391,6 +397,17 @@
     eight = jnp.concatenate([four, four_more])
     eight_more = from_level(eight, 1)
 
+    hidden_near = pl.pallas_call(
+        stage_kernel,
+        name="stage_operands",
+        out_shape=jax.ShapeDtypeStruct(hidden_in.shape, BF16),
+        in_specs=[VMEM] * 2,
+        out_specs=VMEM,
+        compiler_params=PARAMS,
+        cost_estimate=pl.CostEstimate(
+            flops=10_000_000, bytes_accessed=4_000_000, transcendentals=0
+        ),
+    )(hidden_later, packed)
     feat_parts = pl.pallas_call(
         feature_kernel,
         name="partial_features",
@@ -398,7 +415,7 @@
         in_specs=[VMEM] * 3,
         out_specs=VMEM,
         compiler_params=PARAMS,
-    )(lowrank, hidden_in, packed)
+    )(lowrank, hidden_near, packed)
     feat_parts, eight = lax.optimization_barrier((feat_parts, eight))
     feat_all = lax.all_to_all(feat_parts, "mp", 0, 0, tiled=True)
     other = [from_core(part) for part in (eight, eight_more)]

time: 95.4 us -> 94.6 us (level)
  the two profiles are of different devices: /device:TPU:8 before, /device:TPU:32 now
where the time goes in v10:
time: 94.6 us; the launch traced here: 94 us
  starting transfers between devices  54.1 us (57%)
  waiting for transfers between devices  22.9 us (24%)
  Pallas kernels  15.5 us (16%)
  local copies, waits for them, and re-layouts  1.25 us (1%)
    ppermute x2, starting transfers between devices, to_column(): lax.ppermute(seed_feats, ('dp', 'mp'), [(d * model_size + m, ((m ^ flip)...  17.3 us
    ppermute x3, starting transfers between devices, from_level(): lax.ppermute(block, 'dp', [(d, d ^ 2 * flip) for d in range(data_size)])  12.3 us
    ppermute x3, waiting for transfers between devices, from_level(): lax.ppermute(block, 'dp', [(d, d ^ 2 * flip) for d in range(data_size)])  10.9 us
    all_to_all x1, starting transfers between devices, local(): received = lax.all_to_all(send, 'mp', 0, 0, tiled=True)  10.8 us
    pallas_call x1, Pallas kernels, local(): pl.pallas_call(attention_kernel, name='attention_backward', out_shape=(ja...  8.77 us
    all_to_all x1, starting transfers between devices, local(): feat_all = lax.all_to_all(feat_parts, 'mp', 0, 0, tiled=True)  5.02 us
    all_to_all x1, waiting for transfers between devices, local(): feat_all = lax.all_to_all(feat_parts, 'mp', 0, 0, tiled=True)  4.6 us
    all_to_all x1, starting transfers between devices, local(): lowrank = lax.all_to_all(summed, 'mp', 0, 0, tiled=True)  4.33 us
  transfers between devices with their start and end apart: 10, of which 6 were waited for; matrix products, arithmetic and copies ran while one was open for 0% of the time, Pallas kernels for 13%

profile of v10, /device:TPU:32, one launch (start us, length us, event | category | flops | bytes accessed | tf_op | source)
XLA Modules:
  0.0 94.0 jit_solution(6919378620165550724)
XLA Ops:
  0.0 3.0 %collective-permute-start = (bf16[32,512]{1,0:T(8,128)(2,1)}, bf16[32,512]{1,0:T(8,128)(2,1)S(1)}, u32[]{:S(2)}, u32[]{:S(2)}) collective-permute-start(bf16[32,512]{1,0:T(8,128)(2,1)} %param.31), channel_id=1, source_target_pairs={{0,0},{1,32},{2,64},{3,96},{4,128},{5,160},{6,192},{7,224},{8,256}... | collective-permute-start | bytes 98312 | tf_op jit(solution)/shard_map/ppermute | solution.py:287
  3.0 14.3 %collective-permute-start.1 = (bf16[32,512]{1,0:T(8,128)(2,1)}, bf16[32,512]{1,0:T(8,128)(2,1)S(1)}, u32[]{:S(2)}, u32[]{:S(2)}) collective-permute-start(bf16[32,512]{1,0:T(8,128)(2,1)} %param.31), channel_id=1, source_target_pairs={{0,256},{1,288},{2,320},{3,352},{4,384},{5,416},{6,448},{7,480},{8... | collective-permute-start | bytes 98312 | tf_op jit(solution)/shard_map/ppermute | solution.py:287
  17.3 8.8 %attention_backward.1 = (bf16[16,2,32,512]{3,2,1,0:T(8,128)(2,1)}, bf16[2,784,512]{2,1,0:T(8,128)(2,1)}) custom-call(s32[1]{0:T(128)} %bitcast.2.kv_index, bf16[2,512,512]{2,1,0:T(8,128)(2,1)} %hidden_ref.2, bf16[2,512,512]{2,1,0:T(8,128)(2,1)} %query_ref.1, bf16[2,512,512]{2,1,0:T(8,128)(2,1)} %grad_ref.1, bf16[2,512,1024]{2,1,0:T(8,128)(2,1)} %key_ref.1, ...), custom_call_target="tpu_custom_call" | custom-call | flops 5000000000 | bytes 8000000 | tf_op jit(solution)/shard_map/attention_backward/pallas_call | solution.py:315
  26.1 0.0 collective-permute-done
  26.1 0.0 collective-permute-done.1
  26.1 10.8 %all-to-all-start = ((bf16[16,2,32,512]{3,2,1,0:T(8,128)(2,1)}), bf16[16,2,32,512]{3,2,1,0:T(8,128)(2,1)S(1)}, u32[]{:S(2)}, u32[]{:S(2)}) async-start(bf16[16,2,32,512]{3,2,1,0:T(8,128)(2,1)} %get-tuple-element.18), calls=%async_computation | async-start | bytes 2097152 | tf_op jit(solution)/shard_map/all_to_all | solution.py:380
  37.0 4.9 %collective-permute-start.2 = (bf16[2,32,512]{2,1,0:T(8,128)(2,1)S(1)}, bf16[2,32,512]{2,1,0:T(8,128)(2,1)S(1)}, u32[]{:S(2)}, u32[]{:S(2)}) collective-permute-start(bf16[2,32,512]{2,1,0:T(8,128)(2,1)S(1)} %pad_maximum_fusion.1), channel_id=1, source_target_pairs={{0,128},{16,144},{32,160},{48,176},{64,192},{80,208},{96,224},{112... | collective-permute-start | bytes 196616 | tf_op jit(solution)/shard_map/ppermute | solution.py:298
  41.9 6.5 %collective-permute-done.2 = bf16[2,32,512]{2,1,0:T(8,128)(2,1)S(1)} collective-permute-done((bf16[2,32,512]{2,1,0:T(8,128)(2,1)S(1)}, bf16[2,32,512]{2,1,0:T(8,128)(2,1)S(1)}, u32[]{:S(2)}, u32[]{:S(2)}) %collective-permute-start.2) | collective-permute-done | bytes 65568 | tf_op jit(solution)/shard_map/ppermute | solution.py:298
  48.4 4.2 %all-to-all-done.parts_ref = bf16[16,2,32,512]{3,2,1,0:T(8,128)(2,1)S(1)} async-done(((bf16[16,2,32,512]{3,2,1,0:T(8,128)(2,1)}), bf16[16,2,32,512]{3,2,1,0:T(8,128)(2,1)S(1)}, u32[]{:S(2)}, u32[]{:S(2)}) %all-to-all-start) | async-done | bytes 1048608 | tf_op jit(solution)/shard_map/all_to_all | solution.py:380
  52.6 0.0 copy-start
  52.6 1.2 %lowrank_sum.1 = bf16[16,2,32,512]{3,2,1,0:T(8,128)(2,1)} custom-call(bf16[16,2,32,512]{3,2,1,0:T(8,128)(2,1)S(1)} %all-to-all-done.parts_ref), custom_call_target="tpu_custom_call" | custom-call | tf_op jit(solution)/shard_map/lowrank_sum/pallas_call | solution.py:386
  53.8 4.3 %all-to-all-start.1 = ((bf16[16,2,32,512]{3,2,1,0:T(8,128)(2,1)}), bf16[16,2,32,512]{3,2,1,0:T(8,128)(2,1)}, u32[]{:S(2)}, u32[]{:S(2)}) async-start(bf16[16,2,32,512]{3,2,1,0:T(8,128)(2,1)} %lowrank_sum.1), calls=%async_computation.1 | async-start | bytes 2097152 | tf_op jit(solution)/shard_map/all_to_all | solution.py:394
  58.1 3.4 %collective-permute-start.3 = (bf16[4,32,512]{2,1,0:T(8,128)(2,1)S(1)}, bf16[4,32,512]{2,1,0:T(8,128)(2,1)S(1)}, u32[]{:S(2)}, u32[]{:S(2)}) collective-permute-start(bf16[4,32,512]{2,1,0:T(8,128)(2,1)S(1)} %pad_maximum_fusion), channel_id=1, source_target_pairs={{0,64},{16,80},{32,96},{48,112},{64,0},{80,16},{96,32},{112,48},{1... | collective-permute-start | bytes 393224 | tf_op jit(solution)/shard_map/ppermute | solution.py:298
  61.6 4.4 %collective-permute-done.3 = bf16[4,32,512]{2,1,0:T(8,128)(2,1)S(1)} collective-permute-done((bf16[4,32,512]{2,1,0:T(8,128)(2,1)S(1)}, bf16[4,32,512]{2,1,0:T(8,128)(2,1)S(1)}, u32[]{:S(2)}, u32[]{:S(2)}) %collective-permute-start.3) | collective-permute-done | bytes 131104 | tf_op jit(solution)/shard_map/ppermute | solution.py:298
  66.0 3.9 %collective-permute-start.4 = (bf16[8,32,512]{2,1,0:T(8,128)(2,1)S(1)}, bf16[8,32,512]{2,1,0:T(8,128)(2,1)S(1)}, u32[]{:S(2)}, u32[]{:S(2)}) collective-permute-start(bf16[8,32,512]{2,1,0:T(8,128)(2,1)S(1)} %constant_dynamic-update-slice_fusion.refs_0_), channel_id=1, source_target_pairs={{0,32},{16,48},{32,0},{48,16},{64,96},{80,112},{96,64},{112,80},{1... | collective-permute-start | bytes 786440 | tf_op jit(solution)/shard_map/ppermute | solution.py:298
  70.0 0.0 copy-done
  70.0 0.0 copy-start.1
  70.0 1.2 %copy-done.1 = bf16[2,512,512]{2,1,0:T(8,128)(2,1)S(1)} copy-done((bf16[2,512,512]{2,1,0:T(8,128)(2,1)S(1)}, bf16[2,512,512]{2,1,0:T(8,128)(2,1)}, u32[]{:S(2)}) %copy-start.1) | copy-done | bytes 1048600
  71.2 0.1 stage_operands.1.hidden_ref
  71.3 2.1 %all-to-all-done.1.lowrank_ref = bf16[16,2,32,512]{3,2,1,0:T(8,128)(2,1)} async-done(((bf16[16,2,32,512]{3,2,1,0:T(8,128)(2,1)}), bf16[16,2,32,512]{3,2,1,0:T(8,128)(2,1)}, u32[]{:S(2)}, u32[]{:S(2)}) %all-to-all-start.1) | async-done | bytes 1048608 | tf_op jit(solution)/shard_map/all_to_all | solution.py:394
  73.4 3.7 %partial_features.1 = bf16[16,128,128]{2,1,0:T(8,128)(2,1)} custom-call(bf16[16,2,32,512]{3,2,1,0:T(8,128)(2,1)} %all-to-all-done.1.lowrank_ref, bf16[2,512,512]{2,1,0:T(8,128)(2,1)S(1)} %stage_operands.1.hidden_ref, bf16[2,784,512]{2,1,0:T(8,128)(2,1)S(1)} %copy-done), custom_call_target="tpu_custom_call" | custom-call | tf_op jit(solution)/shard_map/partial_features/pallas_call | solution.py:411
  77.1 5.0 %all-to-all-start.2 = ((bf16[16,128,128]{2,1,0:T(8,128)(2,1)}), bf16[16,128,128]{2,1,0:T(8,128)(2,1)S(1)}, u32[]{:S(2)}, u32[]{:S(2)}) async-start(bf16[16,128,128]{2,1,0:T(8,128)(2,1)} %partial_features.1), calls=%async_computation.2 | async-start | bytes 1048576 | tf_op jit(solution)/shard_map/all_to_all | solution.py:420
  82.1 0.0 collective-permute-done.4.refs_1_
  82.1 1.9 %collective-permute-start.6 = (bf16[8,32,512]{2,1,0:T(8,128)(2,1)S(1)}, bf16[8,32,512]{2,1,0:T(8,128)(2,1)S(1)}, u32[]{:S(2)}, u32[]{:S(2)}) collective-permute-start(bf16[8,32,512]{2,1,0:T(8,128)(2,1)S(1)} %collective-permute-done.4.refs_1_), channel_id=1, source_target_pairs={{0,16},{16,0},{32,48},{48,32},{64,80},{80,64},{96,112},{112,96},{1... | collective-permute-start | bytes 786440 | tf_op jit(solution)/shard_map/ppermute | solution.py:301
  84.0 2.4 %collective-permute-start.5 = (bf16[8,32,512]{2,1,0:T(8,128)(2,1)S(1)}, bf16[8,32,512]{2,1,0:T(8,128)(2,1)S(1)}, u32[]{:S(2)}, u32[]{:S(2)}) collective-permute-start(bf16[8,32,512]{2,1,0:T(8,128)(2,1)S(1)} %constant_dynamic-update-slice_fusion.refs_0_), channel_id=1, source_target_pairs={{0,16},{16,0},{32,48},{48,32},{64,80},{80,64},{96,112},{112,96},{1... | collective-permute-start | bytes 786440 | tf_op jit(solution)/shard_map/ppermute | solution.py:301
  86.5 0.1 pad_add_fusion.place
  86.5 0.0 collective-permute-done.6.refs_3_
  86.5 1.0 %collective-permute-done.5.refs_2_ = bf16[8,32,512]{2,1,0:T(8,128)(2,1)S(1)} collective-permute-done((bf16[8,32,512]{2,1,0:T(8,128)(2,1)S(1)}, bf16[8,32,512]{2,1,0:T(8,128)(2,1)S(1)}, u32[]{:S(2)}, u32[]{:S(2)}) %collective-permute-start.5) | collective-permute-done | bytes 262176 | tf_op jit(solution)/shard_map/ppermute | solution.py:301
  87.6 4.6 %all-to-all-done.2.parts_ref = bf16[16,128,128]{2,1,0:T(8,128)(2,1)S(1)} async-done(((bf16[16,128,128]{2,1,0:T(8,128)(2,1)}), bf16[16,128,128]{2,1,0:T(8,128)(2,1)S(1)}, u32[]{:S(2)}, u32[]{:S(2)}) %all-to-all-start.2) | async-done | bytes 524320 | tf_op jit(solution)/shard_map/all_to_all | solution.py:420
  92.2 1.8 %scores.1 = f32[2,64]{1,0:T(2,128)} custom-call(s32[2]{0:T(128)S(1)} %pad_add_fusion.place, bf16[16,128,128]{2,1,0:T(8,128)(2,1)S(1)} %all-to-all-done.2.parts_ref, bf16[8,32,512]{2,1,0:T(8,128)(2,1)S(1)} %constant_dynamic-update-slice_fusion.refs_0_, bf16[8,32,512]{2,1,0:T(8,128)(2,1)S(1)} %collective-permute-done.4.refs_1_, ...), custom_call_target="tpu_custom_call" | custom-call | tf_op jit(solution)/shard_map/scores/pallas_call | solution.py:424
  (5 shorter events, 0.0 us)
Async XLA Ops:
  0.0 26.1 %collective-permute-start = (bf16[32,512]{1,0:T(8,128)(2,1)}, bf16[32,512]{1,0:T(8,128)(2,1)S(1)}, u32[]{:S(2)}, u32[]{:S(2)}) collective-permute-start(bf16[32,512]{1,0:T(8,128)(2,1)} %param.31), channel_id=1, source_target_pairs={{0,0},{1,32},{2,64},{3,96},{4,128},{5,160},{6,192},{7,224},{8,256}... | collective-permute-start | bytes 98312 | tf_op jit(solution)/shard_map/ppermute | solution.py:287
  3.0 23.1 %collective-permute-start.1 = (bf16[32,512]{1,0:T(8,128)(2,1)}, bf16[32,512]{1,0:T(8,128)(2,1)S(1)}, u32[]{:S(2)}, u32[]{:S(2)}) collective-permute-start(bf16[32,512]{1,0:T(8,128)(2,1)} %param.31), channel_id=1, source_target_pairs={{0,256},{1,288},{2,320},{3,352},{4,384},{5,416},{6,448},{7,480},{8... | collective-permute-start | bytes 98312 | tf_op jit(solution)/shard_map/ppermute | solution.py:287
  26.1 26.5 %all-to-all-start = ((bf16[16,2,32,512]{3,2,1,0:T(8,128)(2,1)}), bf16[16,2,32,512]{3,2,1,0:T(8,128)(2,1)S(1)}, u32[]{:S(2)}, u32[]{:S(2)}) async-start(bf16[16,2,32,512]{3,2,1,0:T(8,128)(2,1)} %get-tuple-element.18), calls=%async_computation | async-start | bytes 2097152 | tf_op jit(solution)/shard_map/all_to_all | solution.py:380
  37.0 11.5 %collective-permute-start.2 = (bf16[2,32,512]{2,1,0:T(8,128)(2,1)S(1)}, bf16[2,32,512]{2,1,0:T(8,128)(2,1)S(1)}, u32[]{:S(2)}, u32[]{:S(2)}) collective-permute-start(bf16[2,32,512]{2,1,0:T(8,128)(2,1)S(1)} %pad_maximum_fusion.1), channel_id=1, source_target_pairs={{0,128},{16,144},{32,160},{48,176},{64,192},{80,208},{96,224},{112... | collective-permute-start | bytes 196616 | tf_op jit(solution)/shard_map/ppermute | solution.py:298
  52.6 17.3 %copy-start = (bf16[2,784,512]{2,1,0:T(8,128)(2,1)S(1)}, bf16[2,784,512]{2,1,0:T(8,128)(2,1)}, u32[]{:S(2)}) copy-start(bf16[2,784,512]{2,1,0:T(8,128)(2,1)} %get-tuple-element.24.packed_ref) | copy-start | bytes 4816900
  53.8 19.6 %all-to-all-start.1 = ((bf16[16,2,32,512]{3,2,1,0:T(8,128)(2,1)}), bf16[16,2,32,512]{3,2,1,0:T(8,128)(2,1)}, u32[]{:S(2)}, u32[]{:S(2)}) async-start(bf16[16,2,32,512]{3,2,1,0:T(8,128)(2,1)} %lowrank_sum.1), calls=%async_computation.1 | async-start | bytes 2097152 | tf_op jit(solution)/shard_map/all_to_all | solution.py:394
  58.1 7.9 %collective-permute-start.3 = (bf16[4,32,512]{2,1,0:T(8,128)(2,1)S(1)}, bf16[4,32,512]{2,1,0:T(8,128)(2,1)S(1)}, u32[]{:S(2)}, u32[]{:S(2)}) collective-permute-start(bf16[4,32,512]{2,1,0:T(8,128)(2,1)S(1)} %pad_maximum_fusion), channel_id=1, source_target_pairs={{0,64},{16,80},{32,96},{48,112},{64,0},{80,16},{96,32},{112,48},{1... | collective-permute-start | bytes 393224 | tf_op jit(solution)/shard_map/ppermute | solution.py:298
  66.0 16.1 %collective-permute-start.4 = (bf16[8,32,512]{2,1,0:T(8,128)(2,1)S(1)}, bf16[8,32,512]{2,1,0:T(8,128)(2,1)S(1)}, u32[]{:S(2)}, u32[]{:S(2)}) collective-permute-start(bf16[8,32,512]{2,1,0:T(8,128)(2,1)S(1)} %constant_dynamic-update-slice_fusion.refs_0_), channel_id=1, source_target_pairs={{0,32},{16,48},{32,0},{48,16},{64,96},{80,112},{96,64},{112,80},{1... | collective-permute-start | bytes 786440 | tf_op jit(solution)/shard_map/ppermute | solution.py:298
  70.0 1.2 %copy-start.1 = (bf16[2,512,512]{2,1,0:T(8,128)(2,1)S(1)}, bf16[2,512,512]{2,1,0:T(8,128)(2,1)}, u32[]{:S(2)}) copy-start(bf16[2,512,512]{2,1,0:T(8,128)(2,1)} %hidden_ref.2) | copy-start | bytes 3145732
  77.1 15.1 %all-to-all-start.2 = ((bf16[16,128,128]{2,1,0:T(8,128)(2,1)}), bf16[16,128,128]{2,1,0:T(8,128)(2,1)S(1)}, u32[]{:S(2)}, u32[]{:S(2)}) async-start(bf16[16,128,128]{2,1,0:T(8,128)(2,1)} %partial_features.1), calls=%async_computation.2 | async-start | bytes 1048576 | tf_op jit(solution)/shard_map/all_to_all | solution.py:420
  82.1 4.4 %collective-permute-start.6 = (bf16[8,32,512]{2,1,0:T(8,128)(2,1)S(1)}, bf16[8,32,512]{2,1,0:T(8,128)(2,1)S(1)}, u32[]{:S(2)}, u32[]{:S(2)}) collective-permute-start(bf16[8,32,512]{2,1,0:T(8,128)(2,1)S(1)} %collective-permute-done.4.refs_1_), channel_id=1, source_target_pairs={{0,16},{16,0},{32,48},{48,32},{64,80},{80,64},{96,112},{112,96},{1... | collective-permute-start | bytes 786440 | tf_op jit(solution)/shard_map/ppermute | solution.py:301
  84.0 3.6 %collective-permute-start.5 = (bf16[8,32,512]{2,1,0:T(8,128)(2,1)S(1)}, bf16[8,32,512]{2,1,0:T(8,128)(2,1)S(1)}, u32[]{:S(2)}, u32[]{:S(2)}) collective-permute-start(bf16[8,32,512]{2,1,0:T(8,128)(2,1)S(1)} %constant_dynamic-update-slice_fusion.refs_0_), channel_id=1, source_target_pairs={{0,16},{16,0},{32,48},{48,32},{64,80},{80,64},{96,112},{112,96},{1... | collective-permute-start | bytes 786440 | tf_op jit(solution)/shard_map/ppermute | solution.py:301

commit v11 on v10

--- a/solution.py
+++ b/solution.py
@@ -172,11 +172,24 @@
     out_ref[...] = hidden_ref[...]
 
 
-def feature_kernel(lowrank_ref, hidden_ref, packed_ref, out_ref):
+def feature_kernel(
+    lowrank_hbm, hidden_ref, packed_ref, out_ref, lowrank_ref, chosen_ref, lowrank_sem
+):
+    copy = pltpu.make_async_copy(lowrank_hbm, lowrank_ref, lowrank_sem)
+    copy.start()
     cands = hidden_ref.shape[0]
     width = hidden_ref.shape[2]
     values = slice(width, width + DH)
     tile_rows = slice(width + DH, width + 2 * DH)
+    buckets = KB * NT
+    ids = packed_ref[0, width + 2 * DH :].astype(F32)
+    ids = (ids[4:8] * KB + ids[0:4]).astype(jnp.int32)
+    spans = [(kind * width, width if kind < 3 else DH) for kind in range(4)]
+    for kind, (start, count) in enumerate(spans):
+        where = lax.broadcasted_iota(jnp.int32, (buckets, count), 0)
+        chosen = jnp.where(where == ids[kind : kind + 1, :count], 1.0, 0.0).astype(BF16)
+        chosen_ref[:, start : start + count] = chosen
+    copy.wait()
     pieces = [[], [], [], []]
     for cand in range(cands):
         lowrank = lowrank_ref[:, cand].reshape(4 * R, S)
@@ -185,16 +198,10 @@
         pieces[1].append(down[R:])
         pieces[2].append(dot_nt(lowrank[:R], packed_ref[cand, :width]))
         pieces[3].append(dot_nt(lowrank[R : 2 * R], packed_ref[cand, values]))
-    buckets = KB * NT
-    ids = packed_ref[0, width + 2 * DH :].astype(F32)
-    ids = (ids[4:8] * KB + ids[0:4]).astype(jnp.int32)
     sums = jnp.zeros((buckets, cands * R), F32)
-    for kind in range(4):
+    for kind, (start, count) in enumerate(spans):
         rows = jnp.concatenate(pieces[kind], axis=0).astype(BF16)
-        count = rows.shape[1]
-        where = lax.broadcasted_iota(jnp.int32, (buckets, count), 0)
-        chosen = jnp.where(where == ids[kind : kind + 1, :count], 1.0, 0.0).astype(BF16)
-        sums = sums + dot_nt(chosen, rows)
+        sums = sums + dot_nt(chosen_ref[:, start : start + count], rows)
     wide = jnp.concatenate(
         [
             jnp.concatenate(
@@ -412,8 +419,13 @@
         feature_kernel,
         name="partial_features",
         out_shape=jax.ShapeDtypeStruct((model_size, cands * KB, PB), BF16),
-        in_specs=[VMEM] * 3,
+        in_specs=[pl.BlockSpec(memory_space=pl.ANY), VMEM, VMEM],
         out_specs=VMEM,
+        scratch_shapes=[
+            pltpu.VMEM(lowrank.shape, BF16),
+            pltpu.VMEM((KB * NT, 3 * width + DH), BF16),
+            pltpu.SemaphoreType.DMA,
+        ],
         compiler_params=PARAMS,
     )(lowrank, hidden_near, packed)
     feat_parts, eight = lax.optimization_barrier((feat_parts, eight))

time: 94.6 us -> 94.7 us (level)
  no operation moved by 1% of the time
where the time goes in v11:
time: 94.7 us; the launch traced here: 94 us
  starting transfers between devices  54.1 us (57%)
  waiting for transfers between devices  22.9 us (24%)
  Pallas kernels  15.5 us (16%)
  local copies, waits for them, and re-layouts  1.25 us (1%)
    ppermute x2, starting transfers between devices, to_column(): lax.ppermute(seed_feats, ('dp', 'mp'), [(d * model_size + m, ((m ^ flip)...  17.3 us
    ppermute x3, starting transfers between devices, from_level(): lax.ppermute(block, 'dp', [(d, d ^ 2 * flip) for d in range(data_size)])  12.3 us
    ppermute x3, waiting for transfers between devices, from_level(): lax.ppermute(block, 'dp', [(d, d ^ 2 * flip) for d in range(data_size)])  10.9 us
    all_to_all x1, starting transfers between devices, local(): received = lax.all_to_all(send, 'mp', 0, 0, tiled=True)  10.8 us
    pallas_call x1, Pallas kernels, local(): pl.pallas_call(attention_kernel, name='attention_backward', out_shape=(ja...  8.77 us
    all_to_all x1, starting transfers between devices, local(): feat_all = lax.all_to_all(feat_parts, 'mp', 0, 0, tiled=True)  5.03 us
    all_to_all x1, waiting for transfers between devices, local(): feat_all = lax.all_to_all(feat_parts, 'mp', 0, 0, tiled=True)  4.6 us
    all_to_all x1, starting transfers between devices, local(): lowrank = lax.all_to_all(summed, 'mp', 0, 0, tiled=True)  4.33 us
  transfers between devices with their start and end apart: 10, of which 6 were waited for; matrix products, arithmetic and copies ran while one was open for 0% of the time, Pallas kernels for 13%

profile of v11, /device:TPU:32, one launch (start us, length us, event | category | flops | bytes accessed | tf_op | source)
XLA Modules:
  0.0 94.0 jit_solution(10049291431899542402)
XLA Ops:
  0.0 3.0 %collective-permute-start = (bf16[32,512]{1,0:T(8,128)(2,1)}, bf16[32,512]{1,0:T(8,128)(2,1)S(1)}, u32[]{:S(2)}, u32[]{:S(2)}) collective-permute-start(bf16[32,512]{1,0:T(8,128)(2,1)} %param.31), channel_id=1, source_target_pairs={{0,0},{1,32},{2,64},{3,96},{4,128},{5,160},{6,192},{7,224},{8,256}... | collective-permute-start | bytes 98312 | tf_op jit(solution)/shard_map/ppermute | solution.py:294
  3.0 14.3 %collective-permute-start.1 = (bf16[32,512]{1,0:T(8,128)(2,1)}, bf16[32,512]{1,0:T(8,128)(2,1)S(1)}, u32[]{:S(2)}, u32[]{:S(2)}) collective-permute-start(bf16[32,512]{1,0:T(8,128)(2,1)} %param.31), channel_id=1, source_target_pairs={{0,256},{1,288},{2,320},{3,352},{4,384},{5,416},{6,448},{7,480},{8... | collective-permute-start | bytes 98312 | tf_op jit(solution)/shard_map/ppermute | solution.py:294
  17.3 8.8 %attention_backward.1 = (bf16[16,2,32,512]{3,2,1,0:T(8,128)(2,1)}, bf16[2,784,512]{2,1,0:T(8,128)(2,1)}) custom-call(s32[1]{0:T(128)} %bitcast.2.kv_index, bf16[2,512,512]{2,1,0:T(8,128)(2,1)} %hidden_ref.2, bf16[2,512,512]{2,1,0:T(8,128)(2,1)} %query_ref.1, bf16[2,512,512]{2,1,0:T(8,128)(2,1)} %grad_ref.1, bf16[2,512,1024]{2,1,0:T(8,128)(2,1)} %key_ref.1, ...), custom_call_target="tpu_custom_call" | custom-call | flops 5000000000 | bytes 8000000 | tf_op jit(solution)/shard_map/attention_backward/pallas_call | solution.py:322
  26.1 0.0 collective-permute-done
  26.1 0.0 collective-permute-done.1
  26.1 10.8 %all-to-all-start = ((bf16[16,2,32,512]{3,2,1,0:T(8,128)(2,1)}), bf16[16,2,32,512]{3,2,1,0:T(8,128)(2,1)S(1)}, u32[]{:S(2)}, u32[]{:S(2)}) async-start(bf16[16,2,32,512]{3,2,1,0:T(8,128)(2,1)} %get-tuple-element.18), calls=%async_computation | async-start | bytes 2097152 | tf_op jit(solution)/shard_map/all_to_all | solution.py:387
  37.0 4.9 %collective-permute-start.2 = (bf16[2,32,512]{2,1,0:T(8,128)(2,1)S(1)}, bf16[2,32,512]{2,1,0:T(8,128)(2,1)S(1)}, u32[]{:S(2)}, u32[]{:S(2)}) collective-permute-start(bf16[2,32,512]{2,1,0:T(8,128)(2,1)S(1)} %pad_maximum_fusion.1), channel_id=1, source_target_pairs={{0,128},{16,144},{32,160},{48,176},{64,192},{80,208},{96,224},{112... | collective-permute-start | bytes 196616 | tf_op jit(solution)/shard_map/ppermute | solution.py:305
  41.9 6.5 %collective-permute-done.2 = bf16[2,32,512]{2,1,0:T(8,128)(2,1)S(1)} collective-permute-done((bf16[2,32,512]{2,1,0:T(8,128)(2,1)S(1)}, bf16[2,32,512]{2,1,0:T(8,128)(2,1)S(1)}, u32[]{:S(2)}, u32[]{:S(2)}) %collective-permute-start.2) | collective-permute-done | bytes 65568 | tf_op jit(solution)/shard_map/ppermute | solution.py:305
  48.4 4.2 %all-to-all-done.parts_ref = bf16[16,2,32,512]{3,2,1,0:T(8,128)(2,1)S(1)} async-done(((bf16[16,2,32,512]{3,2,1,0:T(8,128)(2,1)}), bf16[16,2,32,512]{3,2,1,0:T(8,128)(2,1)S(1)}, u32[]{:S(2)}, u32[]{:S(2)}) %all-to-all-start) | async-done | bytes 1048608 | tf_op jit(solution)/shard_map/all_to_all | solution.py:387
  52.6 0.0 copy-start
  52.6 1.2 %lowrank_sum.1 = bf16[16,2,32,512]{3,2,1,0:T(8,128)(2,1)} custom-call(bf16[16,2,32,512]{3,2,1,0:T(8,128)(2,1)S(1)} %all-to-all-done.parts_ref), custom_call_target="tpu_custom_call" | custom-call | tf_op jit(solution)/shard_map/lowrank_sum/pallas_call | solution.py:393
  53.8 4.3 %all-to-all-start.1 = ((bf16[16,2,32,512]{3,2,1,0:T(8,128)(2,1)}), bf16[16,2,32,512]{3,2,1,0:T(8,128)(2,1)}, u32[]{:S(2)}, u32[]{:S(2)}) async-start(bf16[16,2,32,512]{3,2,1,0:T(8,128)(2,1)} %lowrank_sum.1), calls=%async_computation.1 | async-start | bytes 2097152 | tf_op jit(solution)/shard_map/all_to_all | solution.py:401
  58.1 3.4 %collective-permute-start.3 = (bf16[4,32,512]{2,1,0:T(8,128)(2,1)S(1)}, bf16[4,32,512]{2,1,0:T(8,128)(2,1)S(1)}, u32[]{:S(2)}, u32[]{:S(2)}) collective-permute-start(bf16[4,32,512]{2,1,0:T(8,128)(2,1)S(1)} %pad_maximum_fusion), channel_id=1, source_target_pairs={{0,64},{16,80},{32,96},{48,112},{64,0},{80,16},{96,32},{112,48},{1... | collective-permute-start | bytes 393224 | tf_op jit(solution)/shard_map/ppermute | solution.py:305
  61.6 4.4 %collective-permute-done.3 = bf16[4,32,512]{2,1,0:T(8,128)(2,1)S(1)} collective-permute-done((bf16[4,32,512]{2,1,0:T(8,128)(2,1)S(1)}, bf16[4,32,512]{2,1,0:T(8,128)(2,1)S(1)}, u32[]{:S(2)}, u32[]{:S(2)}) %collective-permute-start.3) | collective-permute-done | bytes 131104 | tf_op jit(solution)/shard_map/ppermute | solution.py:305
  66.0 3.9 %collective-permute-start.4 = (bf16[8,32,512]{2,1,0:T(8,128)(2,1)S(1)}, bf16[8,32,512]{2,1,0:T(8,128)(2,1)S(1)}, u32[]{:S(2)}, u32[]{:S(2)}) collective-permute-start(bf16[8,32,512]{2,1,0:T(8,128)(2,1)S(1)} %constant_dynamic-update-slice_fusion.refs_0_), channel_id=1, source_target_pairs={{0,32},{16,48},{32,0},{48,16},{64,96},{80,112},{96,64},{112,80},{1... | collective-permute-start | bytes 786440 | tf_op jit(solution)/shard_map/ppermute | solution.py:305
  70.0 0.0 copy-done
  70.0 0.0 copy-start.1
  70.0 1.2 %copy-done.1 = bf16[2,512,512]{2,1,0:T(8,128)(2,1)S(1)} copy-done((bf16[2,512,512]{2,1,0:T(8,128)(2,1)S(1)}, bf16[2,512,512]{2,1,0:T(8,128)(2,1)}, u32[]{:S(2)}) %copy-start.1) | copy-done | bytes 1048600
  71.2 0.1 stage_operands.1.hidden_ref
  71.3 2.1 %all-to-all-done.1.lowrank_hbm = bf16[16,2,32,512]{3,2,1,0:T(8,128)(2,1)} async-done(((bf16[16,2,32,512]{3,2,1,0:T(8,128)(2,1)}), bf16[16,2,32,512]{3,2,1,0:T(8,128)(2,1)}, u32[]{:S(2)}, u32[]{:S(2)}) %all-to-all-start.1) | async-done | bytes 1048608 | tf_op jit(solution)/shard_map/all_to_all | solution.py:401
  73.4 3.7 %partial_features.1 = bf16[16,128,128]{2,1,0:T(8,128)(2,1)} custom-call(bf16[16,2,32,512]{3,2,1,0:T(8,128)(2,1)} %all-to-all-done.1.lowrank_hbm, bf16[2,512,512]{2,1,0:T(8,128)(2,1)S(1)} %stage_operands.1.hidden_ref, bf16[2,784,512]{2,1,0:T(8,128)(2,1)S(1)} %copy-done), custom_call_target="tpu_custom_call" | custom-call | tf_op jit(solution)/shard_map/partial_features/pallas_call | solution.py:418
  77.1 5.0 %all-to-all-start.2 = ((bf16[16,128,128]{2,1,0:T(8,128)(2,1)}), bf16[16,128,128]{2,1,0:T(8,128)(2,1)S(1)}, u32[]{:S(2)}, u32[]{:S(2)}) async-start(bf16[16,128,128]{2,1,0:T(8,128)(2,1)} %partial_features.1), calls=%async_computation.2 | async-start | bytes 1048576 | tf_op jit(solution)/shard_map/all_to_all | solution.py:432
  82.1 0.0 collective-permute-done.4.refs_1_
  82.1 1.9 %collective-permute-start.6 = (bf16[8,32,512]{2,1,0:T(8,128)(2,1)S(1)}, bf16[8,32,512]{2,1,0:T(8,128)(2,1)S(1)}, u32[]{:S(2)}, u32[]{:S(2)}) collective-permute-start(bf16[8,32,512]{2,1,0:T(8,128)(2,1)S(1)} %collective-permute-done.4.refs_1_), channel_id=1, source_target_pairs={{0,16},{16,0},{32,48},{48,32},{64,80},{80,64},{96,112},{112,96},{1... | collective-permute-start | bytes 786440 | tf_op jit(solution)/shard_map/ppermute | solution.py:308
  84.1 2.4 %collective-permute-start.5 = (bf16[8,32,512]{2,1,0:T(8,128)(2,1)S(1)}, bf16[8,32,512]{2,1,0:T(8,128)(2,1)S(1)}, u32[]{:S(2)}, u32[]{:S(2)}) collective-permute-start(bf16[8,32,512]{2,1,0:T(8,128)(2,1)S(1)} %constant_dynamic-update-slice_fusion.refs_0_), channel_id=1, source_target_pairs={{0,16},{16,0},{32,48},{48,32},{64,80},{80,64},{96,112},{112,96},{1... | collective-permute-start | bytes 786440 | tf_op jit(solution)/shard_map/ppermute | solution.py:308
  86.5 0.1 pad_add_fusion.place
  86.6 0.0 collective-permute-done.6.refs_3_
  86.6 1.0 %collective-permute-done.5.refs_2_ = bf16[8,32,512]{2,1,0:T(8,128)(2,1)S(1)} collective-permute-done((bf16[8,32,512]{2,1,0:T(8,128)(2,1)S(1)}, bf16[8,32,512]{2,1,0:T(8,128)(2,1)S(1)}, u32[]{:S(2)}, u32[]{:S(2)}) %collective-permute-start.5) | collective-permute-done | bytes 262176 | tf_op jit(solution)/shard_map/ppermute | solution.py:308
  87.6 4.6 %all-to-all-done.2.parts_ref = bf16[16,128,128]{2,1,0:T(8,128)(2,1)S(1)} async-done(((bf16[16,128,128]{2,1,0:T(8,128)(2,1)}), bf16[16,128,128]{2,1,0:T(8,128)(2,1)S(1)}, u32[]{:S(2)}, u32[]{:S(2)}) %all-to-all-start.2) | async-done | bytes 524320 | tf_op jit(solution)/shard_map/all_to_all | solution.py:432
  92.2 1.8 %scores.1 = f32[2,64]{1,0:T(2,128)} custom-call(s32[2]{0:T(128)S(1)} %pad_add_fusion.place, bf16[16,128,128]{2,1,0:T(8,128)(2,1)S(1)} %all-to-all-done.2.parts_ref, bf16[8,32,512]{2,1,0:T(8,128)(2,1)S(1)} %constant_dynamic-update-slice_fusion.refs_0_, bf16[8,32,512]{2,1,0:T(8,128)(2,1)S(1)} %collective-permute-done.4.refs_1_, ...), custom_call_target="tpu_custom_call" | custom-call | tf_op jit(solution)/shard_map/scores/pallas_call | solution.py:436
  (5 shorter events, 0.0 us)
Async XLA Ops:
  0.0 26.1 %collective-permute-start = (bf16[32,512]{1,0:T(8,128)(2,1)}, bf16[32,512]{1,0:T(8,128)(2,1)S(1)}, u32[]{:S(2)}, u32[]{:S(2)}) collective-permute-start(bf16[32,512]{1,0:T(8,128)(2,1)} %param.31), channel_id=1, source_target_pairs={{0,0},{1,32},{2,64},{3,96},{4,128},{5,160},{6,192},{7,224},{8,256}... | collective-permute-start | bytes 98312 | tf_op jit(solution)/shard_map/ppermute | solution.py:294
  3.0 23.1 %collective-permute-start.1 = (bf16[32,512]{1,0:T(8,128)(2,1)}, bf16[32,512]{1,0:T(8,128)(2,1)S(1)}, u32[]{:S(2)}, u32[]{:S(2)}) collective-permute-start(bf16[32,512]{1,0:T(8,128)(2,1)} %param.31), channel_id=1, source_target_pairs={{0,256},{1,288},{2,320},{3,352},{4,384},{5,416},{6,448},{7,480},{8... | collective-permute-start | bytes 98312 | tf_op jit(solution)/shard_map/ppermute | solution.py:294
  26.1 26.5 %all-to-all-start = ((bf16[16,2,32,512]{3,2,1,0:T(8,128)(2,1)}), bf16[16,2,32,512]{3,2,1,0:T(8,128)(2,1)S(1)}, u32[]{:S(2)}, u32[]{:S(2)}) async-start(bf16[16,2,32,512]{3,2,1,0:T(8,128)(2,1)} %get-tuple-element.18), calls=%async_computation | async-start | bytes 2097152 | tf_op jit(solution)/shard_map/all_to_all | solution.py:387
  37.0 11.5 %collective-permute-start.2 = (bf16[2,32,512]{2,1,0:T(8,128)(2,1)S(1)}, bf16[2,32,512]{2,1,0:T(8,128)(2,1)S(1)}, u32[]{:S(2)}, u32[]{:S(2)}) collective-permute-start(bf16[2,32,512]{2,1,0:T(8,128)(2,1)S(1)} %pad_maximum_fusion.1), channel_id=1, source_target_pairs={{0,128},{16,144},{32,160},{48,176},{64,192},{80,208},{96,224},{112... | collective-permute-start | bytes 196616 | tf_op jit(solution)/shard_map/ppermute | solution.py:305
  52.6 17.3 %copy-start = (bf16[2,784,512]{2,1,0:T(8,128)(2,1)S(1)}, bf16[2,784,512]{2,1,0:T(8,128)(2,1)}, u32[]{:S(2)}) copy-start(bf16[2,784,512]{2,1,0:T(8,128)(2,1)} %get-tuple-element.24.packed_ref) | copy-start | bytes 4816900
  53.8 19.6 %all-to-all-start.1 = ((bf16[16,2,32,512]{3,2,1,0:T(8,128)(2,1)}), bf16[16,2,32,512]{3,2,1,0:T(8,128)(2,1)}, u32[]{:S(2)}, u32[]{:S(2)}) async-start(bf16[16,2,32,512]{3,2,1,0:T(8,128)(2,1)} %lowrank_sum.1), calls=%async_computation.1 | async-start | bytes 2097152 | tf_op jit(solution)/shard_map/all_to_all | solution.py:401
  58.1 7.9 %collective-permute-start.3 = (bf16[4,32,512]{2,1,0:T(8,128)(2,1)S(1)}, bf16[4,32,512]{2,1,0:T(8,128)(2,1)S(1)}, u32[]{:S(2)}, u32[]{:S(2)}) collective-permute-start(bf16[4,32,512]{2,1,0:T(8,128)(2,1)S(1)} %pad_maximum_fusion), channel_id=1, source_target_pairs={{0,64},{16,80},{32,96},{48,112},{64,0},{80,16},{96,32},{112,48},{1... | collective-permute-start | bytes 393224 | tf_op jit(solution)/shard_map/ppermute | solution.py:305
  66.0 16.1 %collective-permute-start.4 = (bf16[8,32,512]{2,1,0:T(8,128)(2,1)S(1)}, bf16[8,32,512]{2,1,0:T(8,128)(2,1)S(1)}, u32[]{:S(2)}, u32[]{:S(2)}) collective-permute-start(bf16[8,32,512]{2,1,0:T(8,128)(2,1)S(1)} %constant_dynamic-update-slice_fusion.refs_0_), channel_id=1, source_target_pairs={{0,32},{16,48},{32,0},{48,16},{64,96},{80,112},{96,64},{112,80},{1... | collective-permute-start | bytes 786440 | tf_op jit(solution)/shard_map/ppermute | solution.py:305
  70.0 1.2 %copy-start.1 = (bf16[2,512,512]{2,1,0:T(8,128)(2,1)S(1)}, bf16[2,512,512]{2,1,0:T(8,128)(2,1)}, u32[]{:S(2)}) copy-start(bf16[2,512,512]{2,1,0:T(8,128)(2,1)} %hidden_ref.2) | copy-start | bytes 3145732
  77.1 15.1 %all-to-all-start.2 = ((bf16[16,128,128]{2,1,0:T(8,128)(2,1)}), bf16[16,128,128]{2,1,0:T(8,128)(2,1)S(1)}, u32[]{:S(2)}, u32[]{:S(2)}) async-start(bf16[16,128,128]{2,1,0:T(8,128)(2,1)} %partial_features.1), calls=%async_computation.2 | async-start | bytes 1048576 | tf_op jit(solution)/shard_map/all_to_all | solution.py:432
  82.1 4.4 %collective-permute-start.6 = (bf16[8,32,512]{2,1,0:T(8,128)(2,1)S(1)}, bf16[8,32,512]{2,1,0:T(8,128)(2,1)S(1)}, u32[]{:S(2)}, u32[]{:S(2)}) collective-permute-start(bf16[8,32,512]{2,1,0:T(8,128)(2,1)S(1)} %collective-permute-done.4.refs_1_), channel_id=1, source_target_pairs={{0,16},{16,0},{32,48},{48,32},{64,80},{80,64},{96,112},{112,96},{1... | collective-permute-start | bytes 786440 | tf_op jit(solution)/shard_map/ppermute | solution.py:308
  84.1 3.6 %collective-permute-start.5 = (bf16[8,32,512]{2,1,0:T(8,128)(2,1)S(1)}, bf16[8,32,512]{2,1,0:T(8,128)(2,1)S(1)}, u32[]{:S(2)}, u32[]{:S(2)}) collective-permute-start(bf16[8,32,512]{2,1,0:T(8,128)(2,1)S(1)} %constant_dynamic-update-slice_fusion.refs_0_), channel_id=1, source_target_pairs={{0,16},{16,0},{32,48},{48,32},{64,80},{80,64},{96,112},{112,96},{1... | collective-permute-start | bytes 786440 | tf_op jit(solution)/shard_map/ppermute | solution.py:308

commit v12 on v11

--- a/solution.py
+++ b/solution.py
@@ -173,11 +173,15 @@
 
 
 def feature_kernel(
-    lowrank_hbm, hidden_ref, packed_ref, out_ref, lowrank_ref, chosen_ref, lowrank_sem
+    lowrank_hbm, hidden_ref, packed_ref, out_ref, lowrank_ref, chosen_ref, lowrank_sems
 ):
-    copy = pltpu.make_async_copy(lowrank_hbm, lowrank_ref, lowrank_sem)
-    copy.start()
     cands = hidden_ref.shape[0]
+    copies = [
+        pltpu.make_async_copy(lowrank_hbm.at[:, c], lowrank_ref.at[c], lowrank_sems.at[c])
+        for c in range(cands)
+    ]
+    for copy in copies:
+        copy.start()
     width = hidden_ref.shape[2]
     values = slice(width, width + DH)
     tile_rows = slice(width + DH, width + 2 * DH)
@@ -189,10 +193,10 @@
         where = lax.broadcasted_iota(jnp.int32, (buckets, count), 0)
         chosen = jnp.where(where == ids[kind : kind + 1, :count], 1.0, 0.0).astype(BF16)
         chosen_ref[:, start : start + count] = chosen
-    copy.wait()
     pieces = [[], [], [], []]
     for cand in range(cands):
-        lowrank = lowrank_ref[:, cand].reshape(4 * R, S)
+        copies[cand].wait()
+        lowrank = lowrank_ref[cand].reshape(4 * R, S)
         down = dot_nn(lowrank[2 * R :], hidden_ref[cand])
         pieces[0].append(down[:R])
         pieces[1].append(down[R:])
@@ -422,9 +426,9 @@
         in_specs=[pl.BlockSpec(memory_space=pl.ANY), VMEM, VMEM],
         out_specs=VMEM,
         scratch_shapes=[
-            pltpu.VMEM(lowrank.shape, BF16),
+            pltpu.VMEM((cands, model_size, chunk, seq_len), BF16),
             pltpu.VMEM((KB * NT, 3 * width + DH), BF16),
-            pltpu.SemaphoreType.DMA,
+            pltpu.SemaphoreType.DMA((cands,)),
         ],
         compiler_params=PARAMS,
     )(lowrank, hidden_near, packed)

time: 94.7 us -> 94.7 us (level)
  no operation moved by 1% of the time
where the time goes in v12:
time: 94.7 us; the launch traced here: 94 us
  starting transfers between devices  54.1 us (57%)
  waiting for transfers between devices  22.9 us (24%)
  Pallas kernels  15.5 us (16%)
  local copies, waits for them, and re-layouts  1.25 us (1%)
    ppermute x2, starting transfers between devices, to_column(): lax.ppermute(seed_feats, ('dp', 'mp'), [(d * model_size + m, ((m ^ flip)...  17.3 us
    ppermute x3, starting transfers between devices, from_level(): lax.ppermute(block, 'dp', [(d, d ^ 2 * flip) for d in range(data_size)])  12.3 us
    ppermute x3, waiting for transfers between devices, from_level(): lax.ppermute(block, 'dp', [(d, d ^ 2 * flip) for d in range(data_size)])  10.9 us
    all_to_all x1, starting transfers between devices, local(): received = lax.all_to_all(send, 'mp', 0, 0, tiled=True)  10.8 us
    pallas_call x1, Pallas kernels, local(): pl.pallas_call(attention_kernel, name='attention_backward', out_shape=(ja...  8.77 us
    all_to_all x1, starting transfers between devices, local(): feat_all = lax.all_to_all(feat_parts, 'mp', 0, 0, tiled=True)  5.03 us
    all_to_all x1, waiting for transfers between devices, local(): feat_all = lax.all_to_all(feat_parts, 'mp', 0, 0, tiled=True)  4.6 us
    all_to_all x1, starting transfers between devices, local(): lowrank = lax.all_to_all(summed, 'mp', 0, 0, tiled=True)  4.33 us
  transfers between devices with their start and end apart: 10, of which 6 were waited for; matrix products, arithmetic and copies ran while one was open for 0% of the time, Pallas kernels for 13%

profile of v12, /device:TPU:32, one launch (start us, length us, event | category | flops | bytes accessed | tf_op | source)
XLA Modules:
  0.0 94.0 jit_solution(2601212929218076964)
XLA Ops:
  0.0 3.0 %collective-permute-start = (bf16[32,512]{1,0:T(8,128)(2,1)}, bf16[32,512]{1,0:T(8,128)(2,1)S(1)}, u32[]{:S(2)}, u32[]{:S(2)}) collective-permute-start(bf16[32,512]{1,0:T(8,128)(2,1)} %param.31), channel_id=1, source_target_pairs={{0,0},{1,32},{2,64},{3,96},{4,128},{5,160},{6,192},{7,224},{8,256}... | collective-permute-start | bytes 98312 | tf_op jit(solution)/shard_map/ppermute | solution.py:298
  3.0 14.3 %collective-permute-start.1 = (bf16[32,512]{1,0:T(8,128)(2,1)}, bf16[32,512]{1,0:T(8,128)(2,1)S(1)}, u32[]{:S(2)}, u32[]{:S(2)}) collective-permute-start(bf16[32,512]{1,0:T(8,128)(2,1)} %param.31), channel_id=1, source_target_pairs={{0,256},{1,288},{2,320},{3,352},{4,384},{5,416},{6,448},{7,480},{8... | collective-permute-start | bytes 98312 | tf_op jit(solution)/shard_map/ppermute | solution.py:298
  17.3 8.8 %attention_backward.1 = (bf16[16,2,32,512]{3,2,1,0:T(8,128)(2,1)}, bf16[2,784,512]{2,1,0:T(8,128)(2,1)}) custom-call(s32[1]{0:T(128)} %bitcast.2.kv_index, bf16[2,512,512]{2,1,0:T(8,128)(2,1)} %hidden_ref.2, bf16[2,512,512]{2,1,0:T(8,128)(2,1)} %query_ref.1, bf16[2,512,512]{2,1,0:T(8,128)(2,1)} %grad_ref.1, bf16[2,512,1024]{2,1,0:T(8,128)(2,1)} %key_ref.1, ...), custom_call_target="tpu_custom_call" | custom-call | flops 5000000000 | bytes 8000000 | tf_op jit(solution)/shard_map/attention_backward/pallas_call | solution.py:326
  26.1 0.0 collective-permute-done
  26.1 0.0 collective-permute-done.1
  26.1 10.8 %all-to-all-start = ((bf16[16,2,32,512]{3,2,1,0:T(8,128)(2,1)}), bf16[16,2,32,512]{3,2,1,0:T(8,128)(2,1)S(1)}, u32[]{:S(2)}, u32[]{:S(2)}) async-start(bf16[16,2,32,512]{3,2,1,0:T(8,128)(2,1)} %get-tuple-element.18), calls=%async_computation | async-start | bytes 2097152 | tf_op jit(solution)/shard_map/all_to_all | solution.py:391
  37.0 4.9 %collective-permute-start.2 = (bf16[2,32,512]{2,1,0:T(8,128)(2,1)S(1)}, bf16[2,32,512]{2,1,0:T(8,128)(2,1)S(1)}, u32[]{:S(2)}, u32[]{:S(2)}) collective-permute-start(bf16[2,32,512]{2,1,0:T(8,128)(2,1)S(1)} %pad_maximum_fusion.1), channel_id=1, source_target_pairs={{0,128},{16,144},{32,160},{48,176},{64,192},{80,208},{96,224},{112... | collective-permute-start | bytes 196616 | tf_op jit(solution)/shard_map/ppermute | solution.py:309
  41.9 6.5 %collective-permute-done.2 = bf16[2,32,512]{2,1,0:T(8,128)(2,1)S(1)} collective-permute-done((bf16[2,32,512]{2,1,0:T(8,128)(2,1)S(1)}, bf16[2,32,512]{2,1,0:T(8,128)(2,1)S(1)}, u32[]{:S(2)}, u32[]{:S(2)}) %collective-permute-start.2) | collective-permute-done | bytes 65568 | tf_op jit(solution)/shard_map/ppermute | solution.py:309
  48.4 4.2 %all-to-all-done.parts_ref = bf16[16,2,32,512]{3,2,1,0:T(8,128)(2,1)S(1)} async-done(((bf16[16,2,32,512]{3,2,1,0:T(8,128)(2,1)}), bf16[16,2,32,512]{3,2,1,0:T(8,128)(2,1)S(1)}, u32[]{:S(2)}, u32[]{:S(2)}) %all-to-all-start) | async-done | bytes 1048608 | tf_op jit(solution)/shard_map/all_to_all | solution.py:391
  52.6 0.0 copy-start
  52.6 1.2 %lowrank_sum.1 = bf16[16,2,32,512]{3,2,1,0:T(8,128)(2,1)} custom-call(bf16[16,2,32,512]{3,2,1,0:T(8,128)(2,1)S(1)} %all-to-all-done.parts_ref), custom_call_target="tpu_custom_call" | custom-call | tf_op jit(solution)/shard_map/lowrank_sum/pallas_call | solution.py:397
  53.8 4.3 %all-to-all-start.1 = ((bf16[16,2,32,512]{3,2,1,0:T(8,128)(2,1)}), bf16[16,2,32,512]{3,2,1,0:T(8,128)(2,1)}, u32[]{:S(2)}, u32[]{:S(2)}) async-start(bf16[16,2,32,512]{3,2,1,0:T(8,128)(2,1)} %lowrank_sum.1), calls=%async_computation.1 | async-start | bytes 2097152 | tf_op jit(solution)/shard_map/all_to_all | solution.py:405
  58.1 3.4 %collective-permute-start.3 = (bf16[4,32,512]{2,1,0:T(8,128)(2,1)S(1)}, bf16[4,32,512]{2,1,0:T(8,128)(2,1)S(1)}, u32[]{:S(2)}, u32[]{:S(2)}) collective-permute-start(bf16[4,32,512]{2,1,0:T(8,128)(2,1)S(1)} %pad_maximum_fusion), channel_id=1, source_target_pairs={{0,64},{16,80},{32,96},{48,112},{64,0},{80,16},{96,32},{112,48},{1... | collective-permute-start | bytes 393224 | tf_op jit(solution)/shard_map/ppermute | solution.py:309
  61.6 4.4 %collective-permute-done.3 = bf16[4,32,512]{2,1,0:T(8,128)(2,1)S(1)} collective-permute-done((bf16[4,32,512]{2,1,0:T(8,128)(2,1)S(1)}, bf16[4,32,512]{2,1,0:T(8,128)(2,1)S(1)}, u32[]{:S(2)}, u32[]{:S(2)}) %collective-permute-start.3) | collective-permute-done | bytes 131104 | tf_op jit(solution)/shard_map/ppermute | solution.py:309
  66.0 3.9 %collective-permute-start.4 = (bf16[8,32,512]{2,1,0:T(8,128)(2,1)S(1)}, bf16[8,32,512]{2,1,0:T(8,128)(2,1)S(1)}, u32[]{:S(2)}, u32[]{:S(2)}) collective-permute-start(bf16[8,32,512]{2,1,0:T(8,128)(2,1)S(1)} %constant_dynamic-update-slice_fusion.refs_0_), channel_id=1, source_target_pairs={{0,32},{16,48},{32,0},{48,16},{64,96},{80,112},{96,64},{112,80},{1... | collective-permute-start | bytes 786440 | tf_op jit(solution)/shard_map/ppermute | solution.py:309
  70.0 0.0 copy-done
  70.0 0.0 copy-start.1
  70.0 1.2 %copy-done.1 = bf16[2,512,512]{2,1,0:T(8,128)(2,1)S(1)} copy-done((bf16[2,512,512]{2,1,0:T(8,128)(2,1)S(1)}, bf16[2,512,512]{2,1,0:T(8,128)(2,1)}, u32[]{:S(2)}) %copy-start.1) | copy-done | bytes 1048600
  71.2 0.1 stage_operands.1.hidden_ref
  71.3 2.1 %all-to-all-done.1.lowrank_hbm = bf16[16,2,32,512]{3,2,1,0:T(8,128)(2,1)} async-done(((bf16[16,2,32,512]{3,2,1,0:T(8,128)(2,1)}), bf16[16,2,32,512]{3,2,1,0:T(8,128)(2,1)}, u32[]{:S(2)}, u32[]{:S(2)}) %all-to-all-start.1) | async-done | bytes 1048608 | tf_op jit(solution)/shard_map/all_to_all | solution.py:405
  73.4 3.8 %partial_features.1 = bf16[16,128,128]{2,1,0:T(8,128)(2,1)} custom-call(bf16[16,2,32,512]{3,2,1,0:T(8,128)(2,1)} %all-to-all-done.1.lowrank_hbm, bf16[2,512,512]{2,1,0:T(8,128)(2,1)S(1)} %stage_operands.1.hidden_ref, bf16[2,784,512]{2,1,0:T(8,128)(2,1)S(1)} %copy-done), custom_call_target="tpu_custom_call" | custom-call | tf_op jit(solution)/shard_map/partial_features/pallas_call | solution.py:422
  77.1 5.0 %all-to-all-start.2 = ((bf16[16,128,128]{2,1,0:T(8,128)(2,1)}), bf16[16,128,128]{2,1,0:T(8,128)(2,1)S(1)}, u32[]{:S(2)}, u32[]{:S(2)}) async-start(bf16[16,128,128]{2,1,0:T(8,128)(2,1)} %partial_features.1), calls=%async_computation.2 | async-start | bytes 1048576 | tf_op jit(solution)/shard_map/all_to_all | solution.py:436
  82.2 0.0 collective-permute-done.4.refs_1_
  82.2 1.9 %collective-permute-start.6 = (bf16[8,32,512]{2,1,0:T(8,128)(2,1)S(1)}, bf16[8,32,512]{2,1,0:T(8,128)(2,1)S(1)}, u32[]{:S(2)}, u32[]{:S(2)}) collective-permute-start(bf16[8,32,512]{2,1,0:T(8,128)(2,1)S(1)} %collective-permute-done.4.refs_1_), channel_id=1, source_target_pairs={{0,16},{16,0},{32,48},{48,32},{64,80},{80,64},{96,112},{112,96},{1... | collective-permute-start | bytes 786440 | tf_op jit(solution)/shard_map/ppermute | solution.py:312
  84.1 2.4 %collective-permute-start.5 = (bf16[8,32,512]{2,1,0:T(8,128)(2,1)S(1)}, bf16[8,32,512]{2,1,0:T(8,128)(2,1)S(1)}, u32[]{:S(2)}, u32[]{:S(2)}) collective-permute-start(bf16[8,32,512]{2,1,0:T(8,128)(2,1)S(1)} %constant_dynamic-update-slice_fusion.refs_0_), channel_id=1, source_target_pairs={{0,16},{16,0},{32,48},{48,32},{64,80},{80,64},{96,112},{112,96},{1... | collective-permute-start | bytes 786440 | tf_op jit(solution)/shard_map/ppermute | solution.py:312
  86.5 0.1 pad_add_fusion.place
  86.6 0.0 collective-permute-done.6.refs_3_
  86.6 1.0 %collective-permute-done.5.refs_2_ = bf16[8,32,512]{2,1,0:T(8,128)(2,1)S(1)} collective-permute-done((bf16[8,32,512]{2,1,0:T(8,128)(2,1)S(1)}, bf16[8,32,512]{2,1,0:T(8,128)(2,1)S(1)}, u32[]{:S(2)}, u32[]{:S(2)}) %collective-permute-start.5) | collective-permute-done | bytes 262176 | tf_op jit(solution)/shard_map/ppermute | solution.py:312
  87.7 4.6 %all-to-all-done.2.parts_ref = bf16[16,128,128]{2,1,0:T(8,128)(2,1)S(1)} async-done(((bf16[16,128,128]{2,1,0:T(8,128)(2,1)}), bf16[16,128,128]{2,1,0:T(8,128)(2,1)S(1)}, u32[]{:S(2)}, u32[]{:S(2)}) %all-to-all-start.2) | async-done | bytes 524320 | tf_op jit(solution)/shard_map/all_to_all | solution.py:436
  92.3 1.8 %scores.1 = f32[2,64]{1,0:T(2,128)} custom-call(s32[2]{0:T(128)S(1)} %pad_add_fusion.place, bf16[16,128,128]{2,1,0:T(8,128)(2,1)S(1)} %all-to-all-done.2.parts_ref, bf16[8,32,512]{2,1,0:T(8,128)(2,1)S(1)} %constant_dynamic-update-slice_fusion.refs_0_, bf16[8,32,512]{2,1,0:T(8,128)(2,1)S(1)} %collective-permute-done.4.refs_1_, ...), custom_call_target="tpu_custom_call" | custom-call | tf_op jit(solution)/shard_map/scores/pallas_call | solution.py:440
  (5 shorter events, 0.0 us)
Async XLA Ops:
  0.0 26.1 %collective-permute-start = (bf16[32,512]{1,0:T(8,128)(2,1)}, bf16[32,512]{1,0:T(8,128)(2,1)S(1)}, u32[]{:S(2)}, u32[]{:S(2)}) collective-permute-start(bf16[32,512]{1,0:T(8,128)(2,1)} %param.31), channel_id=1, source_target_pairs={{0,0},{1,32},{2,64},{3,96},{4,128},{5,160},{6,192},{7,224},{8,256}... | collective-permute-start | bytes 98312 | tf_op jit(solution)/shard_map/ppermute | solution.py:298
  3.0 23.1 %collective-permute-start.1 = (bf16[32,512]{1,0:T(8,128)(2,1)}, bf16[32,512]{1,0:T(8,128)(2,1)S(1)}, u32[]{:S(2)}, u32[]{:S(2)}) collective-permute-start(bf16[32,512]{1,0:T(8,128)(2,1)} %param.31), channel_id=1, source_target_pairs={{0,256},{1,288},{2,320},{3,352},{4,384},{5,416},{6,448},{7,480},{8... | collective-permute-start | bytes 98312 | tf_op jit(solution)/shard_map/ppermute | solution.py:298
  26.1 26.5 %all-to-all-start = ((bf16[16,2,32,512]{3,2,1,0:T(8,128)(2,1)}), bf16[16,2,32,512]{3,2,1,0:T(8,128)(2,1)S(1)}, u32[]{:S(2)}, u32[]{:S(2)}) async-start(bf16[16,2,32,512]{3,2,1,0:T(8,128)(2,1)} %get-tuple-element.18), calls=%async_computation | async-start | bytes 2097152 | tf_op jit(solution)/shard_map/all_to_all | solution.py:391
  37.0 11.5 %collective-permute-start.2 = (bf16[2,32,512]{2,1,0:T(8,128)(2,1)S(1)}, bf16[2,32,512]{2,1,0:T(8,128)(2,1)S(1)}, u32[]{:S(2)}, u32[]{:S(2)}) collective-permute-start(bf16[2,32,512]{2,1,0:T(8,128)(2,1)S(1)} %pad_maximum_fusion.1), channel_id=1, source_target_pairs={{0,128},{16,144},{32,160},{48,176},{64,192},{80,208},{96,224},{112... | collective-permute-start | bytes 196616 | tf_op jit(solution)/shard_map/ppermute | solution.py:309
  52.6 17.3 %copy-start = (bf16[2,784,512]{2,1,0:T(8,128)(2,1)S(1)}, bf16[2,784,512]{2,1,0:T(8,128)(2,1)}, u32[]{:S(2)}) copy-start(bf16[2,784,512]{2,1,0:T(8,128)(2,1)} %get-tuple-element.24.packed_ref) | copy-start | bytes 4816900
  53.8 19.6 %all-to-all-start.1 = ((bf16[16,2,32,512]{3,2,1,0:T(8,128)(2,1)}), bf16[16,2,32,512]{3,2,1,0:T(8,128)(2,1)}, u32[]{:S(2)}, u32[]{:S(2)}) async-start(bf16[16,2,32,512]{3,2,1,0:T(8,128)(2,1)} %lowrank_sum.1), calls=%async_computation.1 | async-start | bytes 2097152 | tf_op jit(solution)/shard_map/all_to_all | solution.py:405
  58.1 7.9 %collective-permute-start.3 = (bf16[4,32,512]{2,1,0:T(8,128)(2,1)S(1)}, bf16[4,32,512]{2,1,0:T(8,128)(2,1)S(1)}, u32[]{:S(2)}, u32[]{:S(2)}) collective-permute-start(bf16[4,32,512]{2,1,0:T(8,128)(2,1)S(1)} %pad_maximum_fusion), channel_id=1, source_target_pairs={{0,64},{16,80},{32,96},{48,112},{64,0},{80,16},{96,32},{112,48},{1... | collective-permute-start | bytes 393224 | tf_op jit(solution)/shard_map/ppermute | solution.py:309
  66.0 16.1 %collective-permute-start.4 = (bf16[8,32,512]{2,1,0:T(8,128)(2,1)S(1)}, bf16[8,32,512]{2,1,0:T(8,128)(2,1)S(1)}, u32[]{:S(2)}, u32[]{:S(2)}) collective-permute-start(bf16[8,32,512]{2,1,0:T(8,128)(2,1)S(1)} %constant_dynamic-update-slice_fusion.refs_0_), channel_id=1, source_target_pairs={{0,32},{16,48},{32,0},{48,16},{64,96},{80,112},{96,64},{112,80},{1... | collective-permute-start | bytes 786440 | tf_op jit(solution)/shard_map/ppermute | solution.py:309
  70.0 1.2 %copy-start.1 = (bf16[2,512,512]{2,1,0:T(8,128)(2,1)S(1)}, bf16[2,512,512]{2,1,0:T(8,128)(2,1)}, u32[]{:S(2)}) copy-start(bf16[2,512,512]{2,1,0:T(8,128)(2,1)} %hidden_ref.2) | copy-start | bytes 3145732
  77.1 15.1 %all-to-all-start.2 = ((bf16[16,128,128]{2,1,0:T(8,128)(2,1)}), bf16[16,128,128]{2,1,0:T(8,128)(2,1)S(1)}, u32[]{:S(2)}, u32[]{:S(2)}) async-start(bf16[16,128,128]{2,1,0:T(8,128)(2,1)} %partial_features.1), calls=%async_computation.2 | async-start | bytes 1048576 | tf_op jit(solution)/shard_map/all_to_all | solution.py:436
  82.2 4.4 %collective-permute-start.6 = (bf16[8,32,512]{2,1,0:T(8,128)(2,1)S(1)}, bf16[8,32,512]{2,1,0:T(8,128)(2,1)S(1)}, u32[]{:S(2)}, u32[]{:S(2)}) collective-permute-start(bf16[8,32,512]{2,1,0:T(8,128)(2,1)S(1)} %collective-permute-done.4.refs_1_), channel_id=1, source_target_pairs={{0,16},{16,0},{32,48},{48,32},{64,80},{80,64},{96,112},{112,96},{1... | collective-permute-start | bytes 786440 | tf_op jit(solution)/shard_map/ppermute | solution.py:312
  84.1 3.6 %collective-permute-start.5 = (bf16[8,32,512]{2,1,0:T(8,128)(2,1)S(1)}, bf16[8,32,512]{2,1,0:T(8,128)(2,1)S(1)}, u32[]{:S(2)}, u32[]{:S(2)}) collective-permute-start(bf16[8,32,512]{2,1,0:T(8,128)(2,1)S(1)} %constant_dynamic-update-slice_fusion.refs_0_), channel_id=1, source_target_pairs={{0,16},{16,0},{32,48},{48,32},{64,80},{80,64},{96,112},{112,96},{1... | collective-permute-start | bytes 786440 | tf_op jit(solution)/shard_map/ppermute | solution.py:312
